TPU v7x, 512 devices: a whole 4x8x8 slice. The times are simulated.
512 devices in a mesh: region: 8 (over x, z_hi), dev: 64 (over y, z_lo, core).
Axes of the slice: x: 4, y: 8, z: 8 (z_hi: 2, z_lo: 4; z = z_hi * 4 + z_lo), core: 2. Of those that a mesh axis runs over, the one named last changes fastest.
Arguments:
- object_field: float32 [2, 131072, 512], P(None, ('region', 'dev')), may hold values from -6 to 6
- probe: float32 [2, 256, 256], replicated, may hold values from -6 to 6
- amplitudes: float32 [8, 64, 4, 256, 256], P('region', 'dev'), may hold values from 0.5 to 4
- row_offset: int32 [8, 64, 4], P('region', 'dev'), may hold values from 0 to 255
- col_offset: int32 [8, 64, 4], P('region', 'dev'), may hold values from 0 to 256
- frame_count: int32 [8, 64], P('region', 'dev'), may hold values from 1 to 4, as said below
Outputs:
- new_object: float32 [2, 131072, 512], P(None, ('region', 'dev'))
- new_probe: float32 [2, 256, 256], replicated
Inputs may be any that keep to these rules, and one draw needn't show every extreme that they name: `frame_count`: in each region, device j and device j + 32 together hold at most 6 frames, and some device holds 4.
All inputs are finite; a program needn't handle non-finite values.
Results may differ from a plain program's by a relative error of at most 0.0003.
Values sent between devices are 32-bit elements; how exact they have to be, the bound alone decides.
No kernel may reach another device: no remote copies, remote signals or barrier semaphores. Data moves between devices by JAX's collectives and lax.ppermute only.
A program may use at most 64 MiB of HBM per device.

v0:
```python
import numpy as np
import ml_dtypes

import jax
import jax.numpy as jnp
from jax import lax
from jax.experimental import pallas as pl
from jax.experimental.pallas import tpu as pltpu
from jax.sharding import PartitionSpec as P

AXES = ("region", "dev")
BLOCK = 32


def in_two(table):
    high = table.astype(ml_dtypes.bfloat16)
    low = (table - high.astype(np.float64)).astype(ml_dtypes.bfloat16)
    return high, low


def half_tables(length):
    half = length // 2
    k = np.arange(half)[:, None]
    n = np.arange(half)[None, :]
    forms = []
    for shift in (0, 1):
        turn = (n * (2 * k + shift)) % length
        angle = -2.0 * np.pi * turn / length
        real = np.cos(angle) / np.sqrt(length)
        imag = np.sin(angle) / np.sqrt(length)
        forms.append(np.block([[real, -imag], [imag, real]]))
    return forms


def frame_tables(length):
    left, right = [], []
    for form in half_tables(length):
        high, low = in_two(form)
        left.append(np.concatenate([high, high, low], axis=1))
        high_t, low_t = high.T, low.T
        right.append(np.concatenate([high_t, high_t, low_t], axis=1))
    lefts = np.stack([left[0], left[1], right[0], right[1]])
    downs = []
    for form in half_tables(length):
        high, low = in_two(form)
        downs.append((np.concatenate([high.T, high.T, low.T], axis=0), np.concatenate([high, high, low], axis=0)))
    rights = np.stack([downs[0][0], downs[1][0], downs[0][1], downs[1][1]])
    return lefts, rights


def order_table(length):
    half = length // 2
    table = np.zeros((length, length), np.float32)
    table[2 * np.arange(half), np.arange(half)] = 1.0
    table[2 * np.arange(half) + 1, half + np.arange(half)] = 1.0
    return table.astype(ml_dtypes.bfloat16)


def split2(x):
    high = x.astype(jnp.bfloat16)
    low = (x - high.astype(jnp.float32)).astype(jnp.bfloat16)
    return high, low


def placed(row, col):
    block = jnp.minimum(col // 128, 1)
    return (
        pl.multiple_of(row // 8 * 8, 8),
        row % 8,
        pl.multiple_of(block * 128, 128),
        col - block * 128,
    )


def tiles(x):
    return x.reshape(x.shape[0] // 8, 8, x.shape[1])


def cut_columns(x, rest):
    shift = (128 - rest) & 127
    r = [pltpu.roll(x[:, 128 * j : 128 * j + 128], shift, axis=1) for j in range(3)]
    inside = lax.broadcasted_iota(jnp.int32, r[0].shape, 1) < 128 - rest
    return jnp.concatenate([jnp.where(inside, r[0], r[1]), jnp.where(inside, r[1], r[2])], axis=1)


def turned(x, shift):
    return pltpu.roll(tiles(x), shift & 7, axis=1)


def read_window(read, size, rest_row, rest_col, use):
    after = turned(cut_columns(read(size, 8), rest_col), 8 - rest_row)
    for i in reversed(range(size // BLOCK)):
        here = turned(cut_columns(read(i * BLOCK, BLOCK), rest_col), 8 - rest_row)
        later = jnp.concatenate([here[1:], after], axis=0)
        sub = lax.broadcasted_iota(jnp.int32, here.shape, 1)
        use(i, jnp.where(sub < 8 - rest_row, here, later).reshape(BLOCK, -1))
        after = here[:1]


def moved_columns(x, rest):
    shift = rest & 127
    ra = pltpu.roll(x[:, :128], shift, axis=1)
    rb = pltpu.roll(x[:, 128:], shift, axis=1)
    inside = lax.broadcasted_iota(jnp.int32, ra.shape, 1) >= rest
    zero = jnp.zeros_like(ra)
    return jnp.concatenate(
        [jnp.where(inside, ra, zero), jnp.where(inside, rb, ra), jnp.where(inside, zero, rb)], axis=1
    )


def moved_rows(x, before, rest_row):
    here = turned(x, rest_row)
    earlier = jnp.concatenate([before, here[:-1]], axis=0)
    sub = lax.broadcasted_iota(jnp.int32, here.shape, 1)
    return jnp.where(sub >= rest_row, here, earlier).reshape(x.shape), here[-1:]


def last_rows(before, rest_row):
    sub = lax.broadcasted_iota(jnp.int32, before.shape, 1)
    return jnp.where(sub >= rest_row, 0.0, before).reshape(8, -1)


def prepare_kernel(rows, cols, counts, amp_ref, probe_ref, order_ref, out_ref, weight_ref, total, side):
    band = weight_ref.shape[0]
    size = probe_ref.shape[1]
    half = size // 2
    total[...] = jnp.zeros_like(total)

    def add_power(source, frame, down):
        start, rest_row, base, rest_col = placed(rows[source, frame], cols[source, frame])
        before = jnp.zeros((1, 8, 384), jnp.float32)
        for i in range(size // BLOCK):
            pr = probe_ref[0, i * BLOCK : (i + 1) * BLOCK, :]
            pi = probe_ref[1, i * BLOCK : (i + 1) * BLOCK, :]
            part, before = moved_rows(moved_columns(pr * pr + pi * pi, rest_col), before, rest_row)
            place = (pl.ds(start + (down + i * BLOCK), BLOCK), pl.ds(base, 384))
            total[place] = total[place] + part
        place = (pl.ds(start + (down + size), 8), pl.ds(base, 384))
        total[place] = total[place] + last_rows(before, rest_row)

    def own(frame, carry):
        add_power(0, frame, band)
        return carry

    def previous(frame, carry):
        add_power(1, frame, 0)
        return carry

    lax.fori_loop(0, counts[0], own, 0)
    lax.fori_loop(0, counts[1], previous, 0)
    for i in range(band // BLOCK):
        weight_ref[i * BLOCK : (i + 1) * BLOCK, :] = 1.0 / (
            total[band + i * BLOCK : band + (i + 1) * BLOCK, :] + 1.0
        )

    def permute(frame, carry):
        x = amp_ref[frame]
        high = x.astype(jnp.bfloat16)
        left = x - high.astype(jnp.float32)
        mid = left.astype(jnp.bfloat16)
        low = (left - mid.astype(jnp.float32)).astype(jnp.bfloat16)
        order = order_ref[...]
        y = (
            jnp.dot(high, order, preferred_element_type=jnp.float32)
            + jnp.dot(mid, order, preferred_element_type=jnp.float32)
            + jnp.dot(low, order, preferred_element_type=jnp.float32)
        )
        for j in (0, 1):
            column = slice(j * half, (j + 1) * half)
            side[...] = y[:, column]
            for parity in (0, 1):
                out_ref[frame, parity * half : (parity + 1) * half, column] = side[
                    pl.ds(parity, half, stride=2), :
                ]
        return carry

    lax.fori_loop(0, counts[0], permute, 0)


def frames_kernel(
    rows, cols, counts, field_ref, rim_ref, probe_ref, amp_ref, lefts, rights,
    mine_ref, other_ref, own_ref, over_ref,
    ext, win, xh, xl, fa, fb, total, grad,
):
    band = field_ref.shape[1]
    size = probe_ref.shape[1]
    half = size // 2
    steps = half // BLOCK
    ext[:, :band] = field_ref[...]
    ext[:, band:] = rim_ref[...]
    total[...] = jnp.zeros_like(total)
    grad[...] = jnp.zeros_like(grad)

    def keep(which, place, value):
        high, low = split2(value)
        xh[(which, *place)] = high
        xl[(which, *place)] = low

    def by_right(which, table):
        high = xh[which]
        x = jnp.concatenate([high, xl[which], high], axis=1)
        return jnp.dot(x, rights[table], preferred_element_type=jnp.float32)

    def by_left(which, table):
        high = xh[which]
        x = jnp.concatenate([high, xl[which], high], axis=0)
        return jnp.dot(lefts[table], x, preferred_element_type=jnp.float32)

    def one_frame(frame, carry):
        start, rest_row, base, rest_col = placed(rows[0, frame], cols[0, frame])

        def into(c):
            def use(i, rows_cut):
                win[c, i * BLOCK : (i + 1) * BLOCK, :] = rows_cut

            return use

        for c in (0, 1):
            read_window(
                lambda at, count: ext[c, pl.ds(start + at, count), pl.ds(base, 384)],
                size, rest_row, rest_col, into(c),
            )
        for i in range(size // BLOCK):
            row = slice(i * BLOCK, (i + 1) * BLOCK)
            wr, wi = win[0, row, :], win[1, row, :]
            pr, pi = probe_ref[0, row, :], probe_ref[1, row, :]
            er = pr * wr - pi * wi
            ei = pr * wi + pi * wr
            keep(0, (row, slice(0, half)), er[:, :half] + er[:, half:])
            keep(0, (row, slice(half, size)), ei[:, :half] + ei[:, half:])
            keep(1, (row, slice(0, half)), er[:, :half] - er[:, half:])
            keep(1, (row, slice(half, size)), ei[:, :half] - ei[:, half:])
        fa[...] = by_right(0, 0)
        fb[...] = by_right(1, 1)
        for i in range(steps):
            top = slice(i * BLOCK, (i + 1) * BLOCK)
            low = slice(half + i * BLOCK, half + (i + 1) * BLOCK)
            for ref, out in ((fa, slice(0, half)), (fb, slice(half, size))):
                t, b = ref[top, :], ref[low, :]
                s, d = t + b, t - b
                keep(0, (top, out), s[:, :half])
                keep(0, (low, out), s[:, half:])
                keep(1, (top, out), d[:, :half])
                keep(1, (low, out), d[:, half:])
        fa[...] = by_left(0, 0)
        fb[...] = by_left(1, 1)
        for i in range(steps):
            top = slice(i * BLOCK, (i + 1) * BLOCK)
            low = slice(half + i * BLOCK, half + (i + 1) * BLOCK)
            for which, ref in ((0, fa), (1, fb)):
                re, im = ref[top, :], ref[low, :]
                a = amp_ref[frame, pl.ds(which * half + i * BLOCK, BLOCK), :]
                factor = 1.0 - a * lax.rsqrt(re * re + im * im + 0.25)
                keep(which, (top, slice(0, size)), re * factor)
                keep(which, (low, slice(0, size)), im * factor)
        fa[...] = by_left(0, 2)
        fb[...] = by_left(1, 3)
        for i in range(steps):
            top = slice(i * BLOCK, (i + 1) * BLOCK)
            low = slice(half + i * BLOCK, half + (i + 1) * BLOCK)
            for part, out in ((top, slice(0, half)), (low, slice(half, size))):
                p, q = fa[part, :], fb[part, :]
                s, d = p + q, p - q
                for place, v in ((top, s), (low, d)):
                    keep(0, (place, out), v[:, :half])
                    keep(1, (place, out), v[:, half:])
        fa[...] = by_right(0, 2)
        fb[...] = by_right(1, 3)
        before = [jnp.zeros((1, 8, 384), jnp.float32)] * 2
        for i in range(size // BLOCK):
            row = slice(i * BLOCK, (i + 1) * BLOCK)
            p, q = fa[row, :], fb[row, :]
            s, d = p + q, p - q
            br = jnp.concatenate([s[:, :half], d[:, :half]], axis=1)
            bi = jnp.concatenate([s[:, half:], d[:, half:]], axis=1)
            wr, wi = win[0, row, :], win[1, row, :]
            grad[0, row, :] = grad[0, row, :] + (wr * br + wi * bi)
            grad[1, row, :] = grad[1, row, :] + (wr * bi - wi * br)
            pr, pi = probe_ref[0, row, :], probe_ref[1, row, :]
            for c, v in ((0, pr * br + pi * bi), (1, pr * bi - pi * br)):
                part, before[c] = moved_rows(moved_columns(v, rest_col), before[c], rest_row)
                place = (c, pl.ds(start + i * BLOCK, BLOCK), pl.ds(base, 384))
                total[place] = total[place] + part
        for c in (0, 1):
            place = (c, pl.ds(start + size, 8), pl.ds(base, 384))
            total[place] = total[place] + last_rows(before[c], rest_row)
        return carry

    lax.fori_loop(0, counts[0], one_frame, 0)
    own_ref[...] = total[:, :band]
    over_ref[...] = total[:, band:]
    first = counts[2] == 0
    for i in range(size // BLOCK):
        row = slice(i * BLOCK, (i + 1) * BLOCK)
        re, im = grad[0, row, :], grad[1, row, :]
        mine_ref[row, :] = jnp.where(first, re, im)
        other_ref[row, :] = jnp.where(first, im, re)


def place_of(device):
    region, dev = divmod(device, 64)
    return {
        "x": region // 2,
        "z": (region % 2) * 4 + (dev // 2) % 4,
        "y": dev // 8,
        "core": dev % 2,
    }


def groups_along(names):
    groups = {}
    for device in range(512):
        place = place_of(device)
        key = tuple(v for k, v in place.items() if k not in names)
        groups.setdefault(key, []).append(device)
    return list(groups.values())


def exchanged(parts, names):
    return lax.all_to_all(parts, AXES, 0, 0, tiled=True, axis_index_groups=groups_along(names))


def copies(part, names):
    peers = len(groups_along(names)[0])
    return exchanged(jnp.broadcast_to(part[None], (peers, *part.shape)), names)


def on_device(object_field, probe, amplitudes, row_offset, col_offset, frame_count):
    band, width = object_field.shape[1:]
    size = probe.shape[1]
    slots = amplitudes.shape[2]
    smem = pl.BlockSpec(memory_space=pltpu.SMEM)
    vmem = pl.BlockSpec(memory_space=pltpu.VMEM)
    f32 = jnp.float32
    peers = lax.axis_size("dev")

    rim = lax.ppermute(object_field, "dev", [(i, i - 1) for i in range(1, peers)])
    facts = jnp.concatenate([row_offset[0, 0], col_offset[0, 0], frame_count[0]])
    facts_before = lax.ppermute(facts, "dev", [(i, i + 1) for i in range(peers - 1)])
    both = jnp.stack([facts, facts_before])
    rows, cols = both[:, :slots], both[:, slots : 2 * slots]
    core = lax.axis_index("dev") % 2
    counts = jnp.concatenate([both[:, 2 * slots], core[None]])

    lefts, rights = frame_tables(size)
    ordered, scale = pl.pallas_call(
        prepare_kernel,
        out_shape=(
            jax.ShapeDtypeStruct((slots, size, size), f32),
            jax.ShapeDtypeStruct((band, width), f32),
        ),
        in_specs=[smem, smem, smem, vmem, vmem, vmem],
        out_specs=(vmem, vmem),
        scratch_shapes=[
            pltpu.VMEM((2 * band + size, width), f32),
            pltpu.VMEM((size, size // 2), f32),
        ],
        cost_estimate=pl.CostEstimate(flops=800_000_000, bytes_accessed=3_200_000, transcendentals=0),
        name="prepare",
    )(rows, cols, counts, amplitudes[0, 0], probe, jnp.asarray(order_table(size)))

    bf16 = jnp.bfloat16
    mine, other, own, over = pl.pallas_call(
        frames_kernel,
        out_shape=(
            jax.ShapeDtypeStruct((size, size), f32),
            jax.ShapeDtypeStruct((size, size), f32),
            jax.ShapeDtypeStruct((2, band, width), f32),
            jax.ShapeDtypeStruct((2, size, width), f32),
        ),
        in_specs=[smem, smem, smem, vmem, vmem, vmem, vmem, vmem, vmem],
        out_specs=(vmem, vmem, vmem, vmem),
        scratch_shapes=[
            pltpu.VMEM((2, band + size, width), f32),
            pltpu.VMEM((2, size, size), f32),
            pltpu.VMEM((2, size, size), bf16),
            pltpu.VMEM((2, size, size), bf16),
            pltpu.VMEM((size, size), f32),
            pltpu.VMEM((size, size), f32),
            pltpu.VMEM((2, band + size, width), f32),
            pltpu.VMEM((2, size, size), f32),
        ],
        compiler_params=pltpu.CompilerParams(vmem_limit_bytes=40 * 1024 * 1024),
        cost_estimate=pl.CostEstimate(flops=3_300_000_000, bytes_accessed=8_000_000, transcendentals=262144),
        name="frames",
    )(rows, cols, counts, object_field, rim, probe, ordered, jnp.asarray(lefts), jnp.asarray(rights))

    swap = [(i, i ^ 1) for i in range(peers)]
    plane = mine + lax.ppermute(other, "dev", swap)
    parts = exchanged(plane.reshape(32, size // 32, size), ("x", "z"))
    share = jnp.sum(parts, axis=0)
    share = jnp.sum(copies(share, ("y",)), axis=0)
    plane = copies(share, ("x", "z")).reshape(size, size)
    plane_other = lax.ppermute(plane, "dev", swap)

    incoming = lax.ppermute(over, "dev", [(i, i + 1) for i in range(peers - 1)])
    new_field = object_field - jnp.concatenate(
        [own[:, :size] + incoming, own[:, size:]], axis=1
    ) * scale[None]

    squares = jnp.sum(plane * plane + plane_other * plane_other)
    step = 0.25 * lax.rsqrt(squares / (2 * size * size) + 1e-06)
    real = jnp.where(core == 0, plane, plane_other)
    imag = jnp.where(core == 0, plane_other, plane)
    new_probe = jnp.stack([probe[0] - step * real, probe[1] - step * imag])
    return (new_field, new_probe)


def solution(mesh):
    return jax.shard_map(
        on_device,
        mesh=mesh,
        in_specs=(
            P(None, ("region", "dev"), None),
            P(),
            P("region", "dev", None, None, None),
            P("region", "dev", None),
            P("region", "dev", None),
            P("region", "dev"),
        ),
        out_specs=(P(None, ("region", "dev"), None), P()),
        check_vma=False,
    )
```

profile of v0, /device:TPU:1, one launch (start us, length us, event | category | flops | bytes accessed | tf_op | source)
XLA Modules:
  0.0 115.5 jit_solution(1067665531746996321)
XLA Ops:
  0.6 0.0 copy-start
  0.6 0.0 copy-start.1
  0.7 8.9 %collective-permute-start.1 = (f32[2,256,512]{2,1,0:T(8,128)}, f32[2,256,512]{2,1,0:T(8,128)S(1)}, u32[]{:S(2)}, u32[]{:S(2)}) collective-permute-start(f32[2,256,512]{2,1,0:T(8,128)} %field_ref.1), channel_id=1, source_target_pairs={{1,0},{2,1},{3,2},{4,3},{5,4},{6,5},{7,6},{8,7},{9,8},{10,9},{11,1... | collective-permute-start | bytes 3145736 | tf_op jit(solution)/shard_map/ppermute | solution.py:337
  10.2 0.7 pad_add_fusion.1
  11.0 1.9 %collective-permute-start = (s32[9]{0:T(128)S(1)}, s32[9]{0:T(128)S(1)}, u32[]{:S(2)}, u32[]{:S(2)}) collective-permute-start(s32[9]{0:T(128)S(1)} %pad_add_fusion.1), channel_id=1, source_target_pairs={{0,1},{1,2},{2,3},{3,4},{4,5},{5,6},{6,7},{7,8},{8,9},{9,10},{10,1... | collective-permute-start | bytes 116 | tf_op jit(solution)/shard_map/ppermute | solution.py:339
  12.9 0.8 fusion.3
  13.7 0.3 collective-permute-done
  14.0 0.2 slice_reduce_fusion
  14.2 0.7 pad_add_fusion.2.counts
  14.8 0.0 copy-start.9
  14.8 0.7 fusion.2
  15.5 0.0 copy-start.2
  15.5 0.0 copy-start.3
  15.5 5.0 %prepare.1 = (f32[4,256,256]{2,1,0:T(8,128)}, f32[256,512]{1,0:T(8,128)}) custom-call(s32[2,4]{1,0:T(2,128)} %get-tuple-element.17.rows, s32[2,4]{1,0:T(2,128)} %get-tuple-element.16.cols, s32[3]{0:T(128)} %pad_add_fusion.2.counts, f32[4,256,256]{2,1,0:T(8,128)} %bitcast.34, f32[2,256,256]{2,1,0:T(8,128)} %probe_ref.3, bf16[256,256]{1,0:T(8,128)(2,1)} %constant.33.clone.order_ref), custom_call_target="tpu_custom_call" | custom-call | flops 800000000 | bytes 3200000 | tf_op jit(solution)/shard_map/prepare/pallas_call | solution.py:346
  20.5 0.0 collective-permute-done.1.rim_ref
  20.5 1.0 copy-done.4
  21.5 0.0 copy-done
  21.5 0.0 copy-done.1
  21.5 0.0 copy-done.9
  21.5 0.0 copy-done.2
  21.5 0.0 copy-done.3
  21.5 0.0 copy-start.5
  21.5 1.2 %copy-done.5 = f32[2,256,512]{2,1,0:T(8,128)S(1)} copy-done((f32[2,256,512]{2,1,0:T(8,128)S(1)}, f32[2,256,512]{2,1,0:T(8,128)}, u32[]{:S(2)}) %copy-start.5) | copy-done | bytes 1048600
  22.8 0.0 copy-start.7
  22.8 1.4 %copy-done.7 = bf16[4,768,256]{2,1,0:T(8,128)(2,1)S(1)} copy-done((bf16[4,768,256]{2,1,0:T(8,128)(2,1)S(1)}, bf16[4,768,256]{2,1,0:T(8,128)(2,1)}, u32[]{:S(2)}) %copy-start.7) | copy-done | bytes 1572888
  24.2 0.0 copy-start.8
  24.2 1.4 %copy-done.8 = bf16[4,256,768]{2,1,0:T(8,128)(2,1)S(1)} copy-done((bf16[4,256,768]{2,1,0:T(8,128)(2,1)S(1)}, bf16[4,256,768]{2,1,0:T(8,128)(2,1)}, u32[]{:S(2)}) %copy-start.8) | copy-done | bytes 1572888
  25.6 1.2 %copy-done.10 = f32[4,256,256]{2,1,0:T(8,128)S(1)} copy-done((f32[4,256,256]{2,1,0:T(8,128)S(1)}, f32[4,256,256]{2,1,0:T(8,128)}, u32[]{:S(2)}) %copy-start.10) | copy-done | bytes 1048600
  26.8 9.5 %frames.1 = (f32[256,256]{1,0:T(8,128)S(1)}, f32[256,256]{1,0:T(8,128)S(1)}, f32[2,256,512]{2,1,0:T(8,128)S(1)}, f32[2,256,512]{2,1,0:T(8,128)S(1)}) custom-call(s32[2,4]{1,0:T(2,128)S(1)} %copy-done.3, s32[2,4]{1,0:T(2,128)S(1)} %copy-done.2, s32[3]{0:T(128)S(1)} %copy-done.9, f32[2,256,512]{2,1,0:T(8,128)S(1)} %copy-done, f32[2,256,512]{2,1,0:T(8,128)S(1)} %copy-done.5, ...), custom_call_target="tpu_custom_call" | custom-call | flops 3300000000 | bytes 8000000 | tf_op jit(solution)/shard_map/frames/pallas_call | solution.py:363
  36.3 0.0 copy-start.6
  36.3 1.0 copy-done.6
  37.2 1.9 %collective-permute-start.3 = (f32[256,256]{1,0:T(8,128)S(1)}, f32[256,256]{1,0:T(8,128)S(1)}, u32[]{:S(2)}, u32[]{:S(2)}) collective-permute-start(f32[256,256]{1,0:T(8,128)S(1)} %get-tuple-element.13), channel_id=1, source_target_pairs={{0,1},{1,0},{2,3},{3,2},{4,5},{5,4},{6,7},{7,6},{8,9},{9,8},{10,11... | collective-permute-start | bytes 786440 | tf_op jit(solution)/shard_map/ppermute | solution.py:389
  39.2 1.5 %collective-permute-done.3 = f32[256,256]{1,0:T(8,128)S(1)} collective-permute-done((f32[256,256]{1,0:T(8,128)S(1)}, f32[256,256]{1,0:T(8,128)S(1)}, u32[]{:S(2)}, u32[]{:S(2)}) %collective-permute-start.3) | collective-permute-done | bytes 262176 | tf_op jit(solution)/shard_map/ppermute | solution.py:389
  40.7 0.8 add_bitcast_fusion
  41.4 10.3 %all-to-all-start = ((f32[32,8,256]{2,1,0:T(8,128)}), f32[32,8,256]{2,1,0:T(8,128)S(1)}, u32[]{:S(2)}, u32[]{:S(2)}) async-start(f32[32,8,256]{2,1,0:T(8,128)} %add_bitcast_fusion), calls=%async_computation | async-start | bytes 524288 | tf_op jit(solution)/shard_map/all_to_all | solution.py:320
  51.7 3.7 %collective-permute-start.2 = (f32[2,256,512]{2,1,0:T(8,128)}, f32[2,256,512]{2,1,0:T(8,128)}, u32[]{:S(2)}, u32[]{:S(2)}) collective-permute-start(f32[2,256,512]{2,1,0:T(8,128)} %copy-done.6), channel_id=1, source_target_pairs={{0,1},{1,2},{2,3},{3,4},{4,5},{5,6},{6,7},{7,8},{8,9},{9,10},{10,1... | collective-permute-start | bytes 3145736 | tf_op jit(solution)/shard_map/ppermute | solution.py:396
  55.5 6.4 %all-to-all-done = f32[32,8,256]{2,1,0:T(8,128)S(1)} async-done(((f32[32,8,256]{2,1,0:T(8,128)}), f32[32,8,256]{2,1,0:T(8,128)S(1)}, u32[]{:S(2)}, u32[]{:S(2)}) %all-to-all-start) | async-done | bytes 262176 | tf_op jit(solution)/shard_map/all_to_all | solution.py:320
  61.9 17.7 %all_to_all.15 = f32[8,8,256]{2,1,0:T(8,128)S(1)} all-to-all(f32[8,8,256]{2,1,0:T(8,128)S(1)} %broadcast_in_dim.7), channel_id=1, replica_groups={{0,8,16,24,32,40,48,56},{1,9,17,25,33,41,49,57},{2,10,18,26,34,42,50,58..., dimensions={0} | all-to-all | bytes 131072 | tf_op jit(solution)/shard_map/all_to_all | solution.py:320
  79.6 0.7 broadcast_in_dim.8
  80.3 8.7 %all-to-all-start.2 = ((f32[32,8,256]{2,1,0:T(8,128)}), f32[32,8,256]{2,1,0:T(8,128)S(1)}, u32[]{:S(2)}, u32[]{:S(2)}) async-start(f32[32,8,256]{2,1,0:T(8,128)} %broadcast_in_dim.8), calls=%async_computation.2 | async-start | bytes 524288 | tf_op jit(solution)/shard_map/all_to_all | solution.py:320
  89.1 9.6 %all-to-all-done.2 = f32[32,8,256]{2,1,0:T(8,128)S(1)} async-done(((f32[32,8,256]{2,1,0:T(8,128)}), f32[32,8,256]{2,1,0:T(8,128)S(1)}, u32[]{:S(2)}, u32[]{:S(2)}) %all-to-all-start.2) | async-done | bytes 262176 | tf_op jit(solution)/shard_map/all_to_all | solution.py:320
  98.7 11.7 %collective-permute-start.4 = (f32[256,256]{1,0:T(8,128)S(1)}, f32[256,256]{1,0:T(8,128)S(1)}, u32[]{:S(2)}, u32[]{:S(2)}) collective-permute-start(f32[256,256]{1,0:T(8,128)S(1)} %bitcast.28), channel_id=1, source_target_pairs={{0,1},{1,0},{2,3},{3,2},{4,5},{5,4},{6,7},{7,6},{8,9},{9,8},{10,11... | collective-permute-start | bytes 786440 | tf_op jit(solution)/shard_map/ppermute | solution.py:394
  110.4 0.0 collective-permute-done.2
  110.4 2.8 %multiply_subtract_fusion = f32[2,256,512]{2,1,0:T(8,128)} fusion(f32[2,256,512]{2,1,0:T(8,128)S(1)} %copy-done, f32[2,256,512]{2,1,0:T(8,128)S(1)} %get-tuple-element.9, f32[2,256,512]{2,1,0:T(8,128)} %collective-permute-done.2, f32[256,512]{1,0:T(8,128)} %get-tuple-element.11), kind=kLoop, calls=%fused_computation | loop fusion | flops 786432 | bytes 4718592 | tf_op jit(solution)/shard_map/sub | solution.py:397
  113.2 0.0 collective-permute-done.4
  113.2 0.7 add_reduce_fusion
  114.6 0.1 fusion.1
  114.6 0.8 pad_maximum_fusion
  (6 shorter events, 0.1 us)
Async XLA Ops:
  0.6 20.9 %copy-start = (f32[2,256,512]{2,1,0:T(8,128)S(1)}, f32[2,256,512]{2,1,0:T(8,128)}, u32[]{:S(2)}) copy-start(f32[2,256,512]{2,1,0:T(8,128)} %field_ref.1) | copy-start | bytes 3145732
  0.6 20.9 %copy-start.1 = (f32[2,256,256]{2,1,0:T(8,128)S(1)}, f32[2,256,256]{2,1,0:T(8,128)}, u32[]{:S(2)}) copy-start(f32[2,256,256]{2,1,0:T(8,128)} %probe_ref.3) | copy-start | bytes 1572868
  0.7 19.9 %collective-permute-start.1 = (f32[2,256,512]{2,1,0:T(8,128)}, f32[2,256,512]{2,1,0:T(8,128)S(1)}, u32[]{:S(2)}, u32[]{:S(2)}) collective-permute-start(f32[2,256,512]{2,1,0:T(8,128)} %field_ref.1), channel_id=1, source_target_pairs={{1,0},{2,1},{3,2},{4,3},{5,4},{6,5},{7,6},{8,7},{9,8},{10,9},{11,1... | collective-permute-start | bytes 3145736 | tf_op jit(solution)/shard_map/ppermute | solution.py:337
  11.0 3.0 %collective-permute-start = (s32[9]{0:T(128)S(1)}, s32[9]{0:T(128)S(1)}, u32[]{:S(2)}, u32[]{:S(2)}) collective-permute-start(s32[9]{0:T(128)S(1)} %pad_add_fusion.1), channel_id=1, source_target_pairs={{0,1},{1,2},{2,3},{3,4},{4,5},{5,6},{6,7},{7,8},{8,9},{9,10},{10,1... | collective-permute-start | bytes 116 | tf_op jit(solution)/shard_map/ppermute | solution.py:339
  14.8 6.7 %copy-start.9 = (s32[3]{0:T(128)S(1)}, s32[3]{0:T(128)}, u32[]{:S(2)}) copy-start(s32[3]{0:T(128)} %pad_add_fusion.2.counts) | copy-start | bytes 40
  15.5 6.0 %copy-start.2 = (s32[2,4]{1,0:T(2,128)S(1)}, s32[2,4]{1,0:T(2,128)}, u32[]{:S(2)}) copy-start(s32[2,4]{1,0:T(2,128)} %get-tuple-element.16.cols) | copy-start | bytes 100
  15.5 6.0 %copy-start.3 = (s32[2,4]{1,0:T(2,128)S(1)}, s32[2,4]{1,0:T(2,128)}, u32[]{:S(2)}) copy-start(s32[2,4]{1,0:T(2,128)} %get-tuple-element.17.rows) | copy-start | bytes 100
  20.5 1.0 copy-start.4
  21.5 1.2 %copy-start.5 = (f32[2,256,512]{2,1,0:T(8,128)S(1)}, f32[2,256,512]{2,1,0:T(8,128)}, u32[]{:S(2)}) copy-start(f32[2,256,512]{2,1,0:T(8,128)} %copy-done.4) | copy-start | bytes 3145732
  22.8 1.4 %copy-start.7 = (bf16[4,768,256]{2,1,0:T(8,128)(2,1)S(1)}, bf16[4,768,256]{2,1,0:T(8,128)(2,1)}, u32[]{:S(2)}) copy-start(bf16[4,768,256]{2,1,0:T(8,128)(2,1)} %constant.35.clone.rights) | copy-start | bytes 4718596
  24.2 1.4 %copy-start.8 = (bf16[4,256,768]{2,1,0:T(8,128)(2,1)S(1)}, bf16[4,256,768]{2,1,0:T(8,128)(2,1)}, u32[]{:S(2)}) copy-start(bf16[4,256,768]{2,1,0:T(8,128)(2,1)} %constant.34.clone.lefts) | copy-start | bytes 4718596
  25.6 1.2 %copy-start.10 = (f32[4,256,256]{2,1,0:T(8,128)S(1)}, f32[4,256,256]{2,1,0:T(8,128)}, u32[]{:S(2)}) copy-start(f32[4,256,256]{2,1,0:T(8,128)} %get-tuple-element.8.amp_ref) | copy-start | bytes 3145732
  36.3 1.0 copy-start.6
  37.2 3.4 %collective-permute-start.3 = (f32[256,256]{1,0:T(8,128)S(1)}, f32[256,256]{1,0:T(8,128)S(1)}, u32[]{:S(2)}, u32[]{:S(2)}) collective-permute-start(f32[256,256]{1,0:T(8,128)S(1)} %get-tuple-element.13), channel_id=1, source_target_pairs={{0,1},{1,0},{2,3},{3,2},{4,5},{5,4},{6,7},{7,6},{8,9},{9,8},{10,11... | collective-permute-start | bytes 786440 | tf_op jit(solution)/shard_map/ppermute | solution.py:389
  41.4 20.4 %all-to-all-start = ((f32[32,8,256]{2,1,0:T(8,128)}), f32[32,8,256]{2,1,0:T(8,128)S(1)}, u32[]{:S(2)}, u32[]{:S(2)}) async-start(f32[32,8,256]{2,1,0:T(8,128)} %add_bitcast_fusion), calls=%async_computation | async-start | bytes 524288 | tf_op jit(solution)/shard_map/all_to_all | solution.py:320
  51.7 58.7 %collective-permute-start.2 = (f32[2,256,512]{2,1,0:T(8,128)}, f32[2,256,512]{2,1,0:T(8,128)}, u32[]{:S(2)}, u32[]{:S(2)}) collective-permute-start(f32[2,256,512]{2,1,0:T(8,128)} %copy-done.6), channel_id=1, source_target_pairs={{0,1},{1,2},{2,3},{3,4},{4,5},{5,6},{6,7},{7,8},{8,9},{9,10},{10,1... | collective-permute-start | bytes 3145736 | tf_op jit(solution)/shard_map/ppermute | solution.py:396
  80.3 18.4 %all-to-all-start.2 = ((f32[32,8,256]{2,1,0:T(8,128)}), f32[32,8,256]{2,1,0:T(8,128)S(1)}, u32[]{:S(2)}, u32[]{:S(2)}) async-start(f32[32,8,256]{2,1,0:T(8,128)} %broadcast_in_dim.8), calls=%async_computation.2 | async-start | bytes 524288 | tf_op jit(solution)/shard_map/all_to_all | solution.py:320
  98.7 14.5 %collective-permute-start.4 = (f32[256,256]{1,0:T(8,128)S(1)}, f32[256,256]{1,0:T(8,128)S(1)}, u32[]{:S(2)}, u32[]{:S(2)}) collective-permute-start(f32[256,256]{1,0:T(8,128)S(1)} %bitcast.28), channel_id=1, source_target_pairs={{0,1},{1,0},{2,3},{3,2},{4,5},{5,4},{6,7},{7,6},{8,9},{9,8},{10,11... | collective-permute-start | bytes 786440 | tf_op jit(solution)/shard_map/ppermute | solution.py:394
where the time goes:
time: 116 us; the launch traced here: 115 us
  starting transfers between devices  47.2 us (41%)
  waiting for transfers between devices  17.8 us (15%)
  blocking collectives  17.7 us (15%)
  Pallas kernels  14.5 us (12%)
  local copies, waits for them, and re-layouts  8.8 us (8%)
  other arithmetic  7.3 us (6%)
  between operations  2.14 us (2%)
    all_to_all x2, starting transfers between devices, exchanged(): lax.all_to_all(parts, AXES, 0, 0, tiled=True, axis_index_groups=groups_al...  19 us
    all_to_all x1, blocking collectives, exchanged(): lax.all_to_all(parts, AXES, 0, 0, tiled=True, axis_index_groups=groups_al...  17.7 us
    all_to_all x2, waiting for transfers between devices, exchanged(): lax.all_to_all(parts, AXES, 0, 0, tiled=True, axis_index_groups=groups_al...  16 us
    ppermute x1, starting transfers between devices, on_device(): plane_other = lax.ppermute(plane, 'dev', swap)  11.7 us
    pallas_call x1, Pallas kernels, on_device(): pl.pallas_call(frames_kernel, out_shape=(jax.ShapeDtypeStruct((size, size...  9.47 us
    ppermute x1, starting transfers between devices, on_device(): lax.ppermute(object_field, 'dev', [(i, i - 1) for i in range(1, peers)])  8.92 us
    unnamed x22, local copies, waits for them, and re-layouts  7.22 us
    pallas_call x1, Pallas kernels, on_device(): pl.pallas_call(prepare_kernel, out_shape=(jax.ShapeDtypeStruct((slots, si...  5.02 us
  transfers between devices with their start and end apart: 7, of which 4 were waited for; matrix products, arithmetic and copies ran while one was open for 6% of the time, Pallas kernels for 4%

commit v1 on v0

--- a/solution.py
+++ b/solution.py
@@ -10,6 +10,8 @@
 
 AXES = ("region", "dev")
 BLOCK = 32
+WIDE = (("x", "z"), ("x", "y"))
+LINE = (("y",), ("z",))
 
 
 def in_two(table):
@@ -33,19 +35,9 @@
 
 
 def frame_tables(length):
-    left, right = [], []
-    for form in half_tables(length):
-        high, low = in_two(form)
-        left.append(np.concatenate([high, high, low], axis=1))
-        high_t, low_t = high.T, low.T
-        right.append(np.concatenate([high_t, high_t, low_t], axis=1))
-    lefts = np.stack([left[0], left[1], right[0], right[1]])
-    downs = []
-    for form in half_tables(length):
-        high, low = in_two(form)
-        downs.append((np.concatenate([high.T, high.T, low.T], axis=0), np.concatenate([high, high, low], axis=0)))
-    rights = np.stack([downs[0][0], downs[1][0], downs[0][1], downs[1][1]])
-    return lefts, rights
+    first, second = half_tables(length)
+    parts = [in_two(form) for form in (first, first.T, second, second.T)]
+    return np.stack([np.stack(pair) for pair in parts])
 
 
 def order_table(length):
@@ -178,18 +170,26 @@
 
 
 def frames_kernel(
-    rows, cols, counts, field_ref, rim_ref, probe_ref, amp_ref, lefts, rights,
+    rows, cols, counts, field_ref, rim_ref, probe_ref, amp_ref, tables_ref,
     mine_ref, other_ref, own_ref, over_ref,
-    ext, win, xh, xl, fa, fb, total, grad,
+    ext, amp, tables, win, xh, xl, fa, fb, total, grad, sems,
 ):
     band = field_ref.shape[1]
     size = probe_ref.shape[1]
     half = size // 2
     steps = half // BLOCK
-    ext[:, :band] = field_ref[...]
-    ext[:, band:] = rim_ref[...]
+    loads = [
+        pltpu.make_async_copy(field_ref, ext.at[:, :band], sems.at[0]),
+        pltpu.make_async_copy(rim_ref, ext.at[:, band:], sems.at[1]),
+        pltpu.make_async_copy(tables_ref, tables, sems.at[2]),
+        pltpu.make_async_copy(amp_ref, amp, sems.at[3]),
+    ]
+    for load in loads:
+        load.start()
     total[...] = jnp.zeros_like(total)
     grad[...] = jnp.zeros_like(grad)
+    for load in loads[:2]:
+        load.wait()
 
     def keep(which, place, value):
         high, low = split2(value)
@@ -199,12 +199,16 @@
     def by_right(which, table):
         high = xh[which]
         x = jnp.concatenate([high, xl[which], high], axis=1)
-        return jnp.dot(x, rights[table], preferred_element_type=jnp.float32)
+        t = tables[table, 0]
+        t = jnp.concatenate([t, t, tables[table, 1]], axis=0)
+        return jnp.dot(x, t, preferred_element_type=jnp.float32)
 
     def by_left(which, table):
         high = xh[which]
         x = jnp.concatenate([high, xl[which], high], axis=0)
-        return jnp.dot(lefts[table], x, preferred_element_type=jnp.float32)
+        t = tables[table, 0]
+        t = jnp.concatenate([t, t, tables[table, 1]], axis=1)
+        return jnp.dot(t, x, preferred_element_type=jnp.float32)
 
     def one_frame(frame, carry):
         start, rest_row, base, rest_col = placed(rows[0, frame], cols[0, frame])
@@ -230,8 +234,14 @@
             keep(0, (row, slice(half, size)), ei[:, :half] + ei[:, half:])
             keep(1, (row, slice(0, half)), er[:, :half] - er[:, half:])
             keep(1, (row, slice(half, size)), ei[:, :half] - ei[:, half:])
-        fa[...] = by_right(0, 0)
-        fb[...] = by_right(1, 1)
+
+        @pl.when(frame == 0)
+        def _():
+            for load in loads[2:]:
+                load.wait()
+
+        fa[...] = by_right(0, 1)
+        fb[...] = by_right(1, 3)
         for i in range(steps):
             top = slice(i * BLOCK, (i + 1) * BLOCK)
             low = slice(half + i * BLOCK, half + (i + 1) * BLOCK)
@@ -243,17 +253,17 @@
                 keep(1, (top, out), d[:, :half])
                 keep(1, (low, out), d[:, half:])
         fa[...] = by_left(0, 0)
-        fb[...] = by_left(1, 1)
+        fb[...] = by_left(1, 2)
         for i in range(steps):
             top = slice(i * BLOCK, (i + 1) * BLOCK)
             low = slice(half + i * BLOCK, half + (i + 1) * BLOCK)
             for which, ref in ((0, fa), (1, fb)):
                 re, im = ref[top, :], ref[low, :]
-                a = amp_ref[frame, pl.ds(which * half + i * BLOCK, BLOCK), :]
+                a = amp[frame, pl.ds(which * half + i * BLOCK, BLOCK), :]
                 factor = 1.0 - a * lax.rsqrt(re * re + im * im + 0.25)
                 keep(which, (top, slice(0, size)), re * factor)
                 keep(which, (low, slice(0, size)), im * factor)
-        fa[...] = by_left(0, 2)
+        fa[...] = by_left(0, 1)
         fb[...] = by_left(1, 3)
         for i in range(steps):
             top = slice(i * BLOCK, (i + 1) * BLOCK)
@@ -264,8 +274,8 @@
                 for place, v in ((top, s), (low, d)):
                     keep(0, (place, out), v[:, :half])
                     keep(1, (place, out), v[:, half:])
-        fa[...] = by_right(0, 2)
-        fb[...] = by_right(1, 3)
+        fa[...] = by_right(0, 0)
+        fb[...] = by_right(1, 2)
         before = [jnp.zeros((1, 8, 384), jnp.float32)] * 2
         for i in range(size // BLOCK):
             row = slice(i * BLOCK, (i + 1) * BLOCK)
@@ -287,14 +297,20 @@
         return carry
 
     lax.fori_loop(0, counts[0], one_frame, 0)
-    own_ref[...] = total[:, :band]
-    over_ref[...] = total[:, band:]
+    stores = [
+        pltpu.make_async_copy(total.at[:, band:], over_ref, sems.at[0]),
+        pltpu.make_async_copy(total.at[:, :band], own_ref, sems.at[1]),
+    ]
+    for store in stores:
+        store.start()
     first = counts[2] == 0
     for i in range(size // BLOCK):
         row = slice(i * BLOCK, (i + 1) * BLOCK)
         re, im = grad[0, row, :], grad[1, row, :]
         mine_ref[row, :] = jnp.where(first, re, im)
         other_ref[row, :] = jnp.where(first, im, re)
+    for store in stores:
+        store.wait()
 
 
 def place_of(device):
@@ -307,12 +323,12 @@
     }
 
 
-def groups_along(names):
+def groups_along(by_core):
     groups = {}
     for device in range(512):
         place = place_of(device)
-        key = tuple(v for k, v in place.items() if k not in names)
-        groups.setdefault(key, []).append(device)
+        key = tuple(v for k, v in place.items() if k not in by_core[place["core"]])
+        groups.setdefault((place["core"], key), []).append(device)
     return list(groups.values())
 
 
@@ -331,6 +347,7 @@
     slots = amplitudes.shape[2]
     smem = pl.BlockSpec(memory_space=pltpu.SMEM)
     vmem = pl.BlockSpec(memory_space=pltpu.VMEM)
+    hbm = pl.BlockSpec(memory_space=pltpu.HBM)
     f32 = jnp.float32
     peers = lax.axis_size("dev")
 
@@ -342,7 +359,6 @@
     core = lax.axis_index("dev") % 2
     counts = jnp.concatenate([both[:, 2 * slots], core[None]])
 
-    lefts, rights = frame_tables(size)
     ordered, scale = pl.pallas_call(
         prepare_kernel,
         out_shape=(
@@ -355,6 +371,7 @@
             pltpu.VMEM((2 * band + size, width), f32),
             pltpu.VMEM((size, size // 2), f32),
         ],
+        compiler_params=pltpu.CompilerParams(vmem_limit_bytes=65000 * 1024),
         cost_estimate=pl.CostEstimate(flops=800_000_000, bytes_accessed=3_200_000, transcendentals=0),
         name="prepare",
     )(rows, cols, counts, amplitudes[0, 0], probe, jnp.asarray(order_table(size)))
@@ -368,10 +385,12 @@
             jax.ShapeDtypeStruct((2, band, width), f32),
             jax.ShapeDtypeStruct((2, size, width), f32),
         ),
-        in_specs=[smem, smem, smem, vmem, vmem, vmem, vmem, vmem, vmem],
-        out_specs=(vmem, vmem, vmem, vmem),
+        in_specs=[smem, smem, smem, hbm, hbm, vmem, hbm, hbm],
+        out_specs=(vmem, vmem, hbm, hbm),
         scratch_shapes=[
             pltpu.VMEM((2, band + size, width), f32),
+            pltpu.VMEM((slots, size, size), f32),
+            pltpu.VMEM((4, 2, size, size), bf16),
             pltpu.VMEM((2, size, size), f32),
             pltpu.VMEM((2, size, size), bf16),
             pltpu.VMEM((2, size, size), bf16),
@@ -379,18 +398,21 @@
             pltpu.VMEM((size, size), f32),
             pltpu.VMEM((2, band + size, width), f32),
             pltpu.VMEM((2, size, size), f32),
+            pltpu.SemaphoreType.DMA((4,)),
         ],
-        compiler_params=pltpu.CompilerParams(vmem_limit_bytes=40 * 1024 * 1024),
+        compiler_params=pltpu.CompilerParams(vmem_limit_bytes=60 * 1024 * 1024),
         cost_estimate=pl.CostEstimate(flops=3_300_000_000, bytes_accessed=8_000_000, transcendentals=262144),
         name="frames",
-    )(rows, cols, counts, object_field, rim, probe, ordered, jnp.asarray(lefts), jnp.asarray(rights))
-
+    )(rows, cols, counts, object_field, rim, probe, ordered, jnp.asarray(frame_tables(size)))
+
+    first = core == 0
+    mine, other, first = lax.optimization_barrier((mine, other, first))
     swap = [(i, i ^ 1) for i in range(peers)]
     plane = mine + lax.ppermute(other, "dev", swap)
-    parts = exchanged(plane.reshape(32, size // 32, size), ("x", "z"))
+    parts = exchanged(plane.reshape(32, size // 32, size), WIDE)
     share = jnp.sum(parts, axis=0)
-    share = jnp.sum(copies(share, ("y",)), axis=0)
-    plane = copies(share, ("x", "z")).reshape(size, size)
+    share = jnp.sum(copies(share, LINE), axis=0)
+    plane = copies(share, WIDE).reshape(size, size)
     plane_other = lax.ppermute(plane, "dev", swap)
 
     incoming = lax.ppermute(over, "dev", [(i, i + 1) for i in range(peers - 1)])
@@ -400,8 +422,8 @@
 
     squares = jnp.sum(plane * plane + plane_other * plane_other)
     step = 0.25 * lax.rsqrt(squares / (2 * size * size) + 1e-06)
-    real = jnp.where(core == 0, plane, plane_other)
-    imag = jnp.where(core == 0, plane_other, plane)
+    real = jnp.where(first, plane, plane_other)
+    imag = jnp.where(first, plane_other, plane)
     new_probe = jnp.stack([probe[0] - step * real, probe[1] - step * imag])
     return (new_field, new_probe)
 

time: 116 us -> 105 us (0.905)
  blocking collectives: 17.7 us -> 32.6 us
  starting transfers between devices: 47.2 us -> 34.6 us
  waiting for transfers between devices: 17.8 us -> 10.4 us
  local copies, waits for them, and re-layouts: 8.8 us -> 1.47 us
  Pallas kernels: 14.5 us -> 16.1 us
    all_to_all x1 -> x2, blocking collectives: 17.7 us -> 32.6 us  [exchanged(): lax.all_to_all(parts, AXES, 0, 0, tiled=True, axis_index_groups=groups_al...]
    ppermute x1, starting transfers between devices: 11.7 us -> 3.32 us  [on_device(): plane_other = lax.ppermute(plane, 'dev', swap)]
    all_to_all x2 -> x1, waiting for transfers between devices: 16 us -> 7.72 us  [exchanged(): lax.all_to_all(parts, AXES, 0, 0, tiled=True, axis_index_groups=groups_al...]
    unnamed x22 -> x12, local copies, waits for them, and re-layouts: 7.22 us -> 0.67 us
    all_to_all x2 -> x1, starting transfers between devices: 19 us -> 16.8 us  [exchanged(): lax.all_to_all(parts, AXES, 0, 0, tiled=True, axis_index_groups=groups_al...]
    pallas_call x1, Pallas kernels: 9.47 us -> 11.7 us  [on_device(): pl.pallas_call(frames_kernel, out_shape=(jax.ShapeDtypeStruct((size, size...]
    ppermute x1, starting transfers between devices: 3.74 us -> 1.92 us  [on_device(): incoming = lax.ppermute(over, 'dev', [(i, i + 1) for i in range(peers - 1)])]
  transfers between devices with their start and end apart: 7 -> 6, of which waited for: 4 -> 3; matrix products, arithmetic and copies ran while one was open for 6% -> 4% of each run, Pallas kernels for 4% -> 4%
where the time goes in v1:
time: 105 us; the launch traced here: 104 us
  starting transfers between devices  34.6 us (33%)
  blocking collectives  32.6 us (31%)
  Pallas kernels  16.1 us (15%)
  waiting for transfers between devices  10.4 us (10%)
  other arithmetic  6.81 us (6%)
  between operations  2.14 us (2%)
  local copies, waits for them, and re-layouts  1.47 us (1%)
    all_to_all x2, blocking collectives, exchanged(): lax.all_to_all(parts, AXES, 0, 0, tiled=True, axis_index_groups=groups_al...  32.6 us
    all_to_all x1, starting transfers between devices, exchanged(): lax.all_to_all(parts, AXES, 0, 0, tiled=True, axis_index_groups=groups_al...  16.8 us
    pallas_call x1, Pallas kernels, on_device(): pl.pallas_call(frames_kernel, out_shape=(jax.ShapeDtypeStruct((size, size...  11.7 us
    ppermute x1, starting transfers between devices, on_device(): lax.ppermute(object_field, 'dev', [(i, i - 1) for i in range(1, peers)])  8.79 us
    all_to_all x1, waiting for transfers between devices, exchanged(): lax.all_to_all(parts, AXES, 0, 0, tiled=True, axis_index_groups=groups_al...  7.72 us
    pallas_call x1, Pallas kernels, on_device(): pl.pallas_call(prepare_kernel, out_shape=(jax.ShapeDtypeStruct((slots, si...  4.4 us
    ppermute x1, starting transfers between devices, on_device(): plane_other = lax.ppermute(plane, 'dev', swap)  3.32 us
    sub x1, other arithmetic, on_device(): object_field - jnp.concatenate([own[:, :size] + incoming, own[:, size:]],...  2.62 us
  transfers between devices with their start and end apart: 6, of which 3 were waited for; matrix products, arithmetic and copies ran while one was open for 4% of the time, Pallas kernels for 4%

profile of v1, /device:TPU:1, one launch (start us, length us, event | category | flops | bytes accessed | tf_op | source)
XLA Modules:
  0.0 104.1 jit_solution(10640566616980305323)
XLA Ops:
  0.6 8.8 %collective-permute-start.1 = (f32[2,256,512]{2,1,0:T(8,128)}, f32[2,256,512]{2,1,0:T(8,128)}, u32[]{:S(2)}, u32[]{:S(2)}) collective-permute-start(f32[2,256,512]{2,1,0:T(8,128)} %field_ref.1), channel_id=1, source_target_pairs={{1,0},{2,1},{3,2},{4,3},{5,4},{6,5},{7,6},{8,7},{9,8},{10,9},{11,1... | collective-permute-start | bytes 3145736 | tf_op jit(solution)/shard_map/ppermute | solution.py:354
  10.1 0.0 copy-start.4
  10.1 0.0 copy-start.5
  10.1 0.6 copy-done.4
  10.7 0.0 copy-done.5
  10.7 0.1 pad_add_fusion.1
  10.8 1.9 %collective-permute-start = (s32[9]{0:T(128)S(1)}, s32[9]{0:T(128)S(1)}, u32[]{:S(2)}, u32[]{:S(2)}) collective-permute-start(s32[9]{0:T(128)S(1)} %pad_add_fusion.1), channel_id=1, source_target_pairs={{0,1},{1,2},{2,3},{3,4},{4,5},{5,6},{6,7},{7,8},{8,9},{9,10},{10,1... | collective-permute-start | bytes 116 | tf_op jit(solution)/shard_map/ppermute | solution.py:356
  12.8 0.1 fusion.3
  12.8 1.0 collective-permute-done
  13.8 0.2 slice_reduce_fusion
  14.0 0.6 pad_add_fusion.2.counts
  14.7 0.6 fusion.2
  15.3 4.4 %prepare.1 = (f32[4,256,256]{2,1,0:T(8,128)}, f32[256,512]{1,0:T(8,128)}) custom-call(s32[2,4]{1,0:T(2,128)} %get-tuple-element.23.rows, s32[2,4]{1,0:T(2,128)} %get-tuple-element.22.cols, s32[3]{0:T(128)} %pad_add_fusion.2.counts, f32[4,256,256]{2,1,0:T(8,128)} %bitcast.34, f32[2,256,256]{2,1,0:T(8,128)} %probe_ref.3, bf16[256,256]{1,0:T(8,128)(2,1)} %constant.31.clone.order_ref), custom_call_target="tpu_custom_call" | custom-call | flops 800000000 | bytes 3200000 | tf_op jit(solution)/shard_map/prepare/pallas_call | solution.py:362
  19.7 0.0 collective-permute-done.1.rim_ref
  19.7 11.7 %frames.1 = (f32[256,256]{1,0:T(8,128)}, f32[256,256]{1,0:T(8,128)}, f32[2,256,512]{2,1,0:T(8,128)}, f32[2,256,512]{2,1,0:T(8,128)}) custom-call(s32[2,4]{1,0:T(2,128)} %get-tuple-element.23.rows, s32[2,4]{1,0:T(2,128)} %get-tuple-element.22.cols, s32[3]{0:T(128)} %pad_add_fusion.2.counts, f32[2,256,512]{2,1,0:T(8,128)} %field_ref.1, ...), custom_call_target="tpu_custom_call" | custom-call | flops 3300000000 | bytes 8000000 | tf_op jit(solution)/shard_map/frames/pallas_call | solution.py:380
  31.3 1.9 %collective-permute-start.3 = (f32[256,256]{1,0:T(8,128)}, f32[256,256]{1,0:T(8,128)S(1)}, u32[]{:S(2)}, u32[]{:S(2)}) collective-permute-start(f32[256,256]{1,0:T(8,128)} %get-tuple-element.18), channel_id=1, source_target_pairs={{0,1},{1,0},{2,3},{3,2},{4,5},{5,4},{6,7},{7,6},{8,9},{9,8},{10,11... | collective-permute-start | bytes 786440 | tf_op jit(solution)/shard_map/ppermute | solution.py:411
  33.3 1.7 %collective-permute-done.3 = f32[256,256]{1,0:T(8,128)S(1)} collective-permute-done((f32[256,256]{1,0:T(8,128)}, f32[256,256]{1,0:T(8,128)S(1)}, u32[]{:S(2)}, u32[]{:S(2)}) %collective-permute-start.3) | collective-permute-done | bytes 262176 | tf_op jit(solution)/shard_map/ppermute | solution.py:411
  35.0 0.0 copy-start.1
  35.0 1.8 %add_bitcast_fusion = f32[32,8,256]{2,1,0:T(8,128)} fusion(f32[256,256]{1,0:T(8,128)} %get-tuple-element.17, f32[256,256]{1,0:T(8,128)S(1)} %collective-permute-done.3), kind=kLoop, calls=%fused_computation.7 | loop fusion | flops 65536 | bytes 786432 | tf_op jit(solution)/shard_map/reshape | solution.py:412
  36.8 0.0 copy-start
  36.8 16.8 %all-to-all-start = ((f32[32,8,256]{2,1,0:T(8,128)}), f32[32,8,256]{2,1,0:T(8,128)S(1)}, u32[]{:S(2)}, u32[]{:S(2)}) async-start(f32[32,8,256]{2,1,0:T(8,128)} %add_bitcast_fusion), calls=%async_computation | async-start | bytes 524288 | tf_op jit(solution)/shard_map/all_to_all | solution.py:336
  53.5 1.9 %collective-permute-start.2 = (f32[2,256,512]{2,1,0:T(8,128)}, f32[2,256,512]{2,1,0:T(8,128)}, u32[]{:S(2)}, u32[]{:S(2)}) collective-permute-start(f32[2,256,512]{2,1,0:T(8,128)} %get-tuple-element.13), channel_id=1, source_target_pairs={{0,1},{1,2},{2,3},{3,4},{4,5},{5,6},{6,7},{7,8},{8,9},{9,10},{10,1... | collective-permute-start | bytes 3145736 | tf_op jit(solution)/shard_map/ppermute | solution.py:418
  55.5 7.7 %all-to-all-done = f32[32,8,256]{2,1,0:T(8,128)S(1)} async-done(((f32[32,8,256]{2,1,0:T(8,128)}), f32[32,8,256]{2,1,0:T(8,128)S(1)}, u32[]{:S(2)}, u32[]{:S(2)}) %all-to-all-start) | async-done | bytes 262176 | tf_op jit(solution)/shard_map/all_to_all | solution.py:336
  63.2 0.0 copy-start.2
  63.3 15.1 %all_to_all.15 = f32[8,8,256]{2,1,0:T(8,128)S(1)} all-to-all(f32[8,8,256]{2,1,0:T(8,128)S(1)} %broadcast_in_dim.7), channel_id=1, replica_groups={{0,8,16,24,32,40,48,56},{1,3,5,7,65,67,69,71},{2,10,18,26,34,42,50,58},..., dimensions={0} | all-to-all | bytes 131072 | tf_op jit(solution)/shard_map/all_to_all | solution.py:336
  78.4 17.5 %all_to_all.16 = f32[32,8,256]{2,1,0:T(8,128)S(1)} all-to-all(f32[32,8,256]{2,1,0:T(8,128)S(1)} %broadcast_in_dim.8), channel_id=1, replica_groups={{0,2,4,6,64,66,68,70,128,130,132,134,192,194,196,198,256,258,260,262,32..., dimensions={0} | all-to-all | bytes 524288 | tf_op jit(solution)/shard_map/all_to_all | solution.py:336
  95.9 3.3 %collective-permute-start.4 = (f32[256,256]{1,0:T(8,128)S(1)}, f32[256,256]{1,0:T(8,128)S(1)}, u32[]{:S(2)}, u32[]{:S(2)}) collective-permute-start(f32[256,256]{1,0:T(8,128)S(1)} %bitcast.28), channel_id=1, source_target_pairs={{0,1},{1,0},{2,3},{3,2},{4,5},{5,4},{6,7},{7,6},{8,9},{9,8},{10,11... | collective-permute-start | bytes 786440 | tf_op jit(solution)/shard_map/ppermute | solution.py:416
  99.2 0.0 collective-permute-done.2
  99.2 0.0 copy-done.1
  99.2 0.0 copy-done
  99.2 0.0 copy-done.2
  99.2 2.6 %multiply_subtract_fusion = f32[2,256,512]{2,1,0:T(8,128)} fusion(f32[2,256,512]{2,1,0:T(8,128)S(1)} %copy-done, f32[2,256,512]{2,1,0:T(8,128)S(1)} %copy-done.1, f32[2,256,512]{2,1,0:T(8,128)} %collective-permute-done.2, f32[256,512]{1,0:T(8,128)S(1)} %copy-done.2), kind=kLoop, calls=%fused_computation | loop fusion | flops 786432 | bytes 4718592 | tf_op jit(solution)/shard_map/sub | solution.py:419
  101.9 0.0 copy-start.3
  101.9 0.0 collective-permute-done.4
  101.9 0.7 add_reduce_fusion
  103.2 0.0 copy-done.3
  103.2 0.1 fusion.1
  103.3 0.8 pad_maximum_fusion
  (5 shorter events, 0.1 us)
Async XLA Ops:
  0.6 19.0 %collective-permute-start.1 = (f32[2,256,512]{2,1,0:T(8,128)}, f32[2,256,512]{2,1,0:T(8,128)}, u32[]{:S(2)}, u32[]{:S(2)}) collective-permute-start(f32[2,256,512]{2,1,0:T(8,128)} %field_ref.1), channel_id=1, source_target_pairs={{1,0},{2,1},{3,2},{4,3},{5,4},{6,5},{7,6},{8,7},{9,8},{10,9},{11,1... | collective-permute-start | bytes 3145736 | tf_op jit(solution)/shard_map/ppermute | solution.py:354
  10.1 0.7 copy-start.4
  10.1 0.7 copy-start.5
  10.8 3.0 %collective-permute-start = (s32[9]{0:T(128)S(1)}, s32[9]{0:T(128)S(1)}, u32[]{:S(2)}, u32[]{:S(2)}) collective-permute-start(s32[9]{0:T(128)S(1)} %pad_add_fusion.1), channel_id=1, source_target_pairs={{0,1},{1,2},{2,3},{3,4},{4,5},{5,6},{6,7},{7,8},{8,9},{9,10},{10,1... | collective-permute-start | bytes 116 | tf_op jit(solution)/shard_map/ppermute | solution.py:356
  31.3 3.6 %collective-permute-start.3 = (f32[256,256]{1,0:T(8,128)}, f32[256,256]{1,0:T(8,128)S(1)}, u32[]{:S(2)}, u32[]{:S(2)}) collective-permute-start(f32[256,256]{1,0:T(8,128)} %get-tuple-element.18), channel_id=1, source_target_pairs={{0,1},{1,0},{2,3},{3,2},{4,5},{5,4},{6,7},{7,6},{8,9},{9,8},{10,11... | collective-permute-start | bytes 786440 | tf_op jit(solution)/shard_map/ppermute | solution.py:411
  35.0 64.2 %copy-start.1 = (f32[2,256,512]{2,1,0:T(8,128)S(1)}, f32[2,256,512]{2,1,0:T(8,128)}, u32[]{:S(2)}) copy-start(f32[2,256,512]{2,1,0:T(8,128)} %get-tuple-element.12) | copy-start | bytes 3145732
  36.8 62.5 %copy-start = (f32[2,256,512]{2,1,0:T(8,128)S(1)}, f32[2,256,512]{2,1,0:T(8,128)}, u32[]{:S(2)}) copy-start(f32[2,256,512]{2,1,0:T(8,128)} %field_ref.1) | copy-start | bytes 3145732
  36.8 26.4 %all-to-all-start = ((f32[32,8,256]{2,1,0:T(8,128)}), f32[32,8,256]{2,1,0:T(8,128)S(1)}, u32[]{:S(2)}, u32[]{:S(2)}) async-start(f32[32,8,256]{2,1,0:T(8,128)} %add_bitcast_fusion), calls=%async_computation | async-start | bytes 524288 | tf_op jit(solution)/shard_map/all_to_all | solution.py:336
  53.5 45.7 %collective-permute-start.2 = (f32[2,256,512]{2,1,0:T(8,128)}, f32[2,256,512]{2,1,0:T(8,128)}, u32[]{:S(2)}, u32[]{:S(2)}) collective-permute-start(f32[2,256,512]{2,1,0:T(8,128)} %get-tuple-element.13), channel_id=1, source_target_pairs={{0,1},{1,2},{2,3},{3,4},{4,5},{5,6},{6,7},{7,8},{8,9},{9,10},{10,1... | collective-permute-start | bytes 3145736 | tf_op jit(solution)/shard_map/ppermute | solution.py:418
  63.2 36.0 %copy-start.2 = (f32[256,512]{1,0:T(8,128)S(1)}, f32[256,512]{1,0:T(8,128)}, u32[]{:S(2)}) copy-start(f32[256,512]{1,0:T(8,128)} %get-tuple-element.14) | copy-start | bytes 1572868
  95.9 6.0 %collective-permute-start.4 = (f32[256,256]{1,0:T(8,128)S(1)}, f32[256,256]{1,0:T(8,128)S(1)}, u32[]{:S(2)}, u32[]{:S(2)}) collective-permute-start(f32[256,256]{1,0:T(8,128)S(1)} %bitcast.28), channel_id=1, source_target_pairs={{0,1},{1,0},{2,3},{3,2},{4,5},{5,4},{6,7},{7,6},{8,9},{9,8},{10,11... | collective-permute-start | bytes 786440 | tf_op jit(solution)/shard_map/ppermute | solution.py:416
  101.9 1.4 %copy-start.3 = (f32[2,256,256]{2,1,0:T(8,128)S(1)}, f32[2,256,256]{2,1,0:T(8,128)}, u32[]{:S(2)}) copy-start(f32[2,256,256]{2,1,0:T(8,128)} %probe_ref.3) | copy-start | bytes 1572868

commit v2 on v1

--- a/solution.py
+++ b/solution.py
@@ -9,6 +9,8 @@
 from jax.sharding import PartitionSpec as P
 
 AXES = ("region", "dev")
+SLOTS = 4
+COUNT, CORE = 2 * SLOTS, 2 * SLOTS + 1
 BLOCK = 32
 WIDE = (("x", "z"), ("x", "y"))
 LINE = (("y",), ("z",))
@@ -64,6 +66,10 @@
     )
 
 
+def corner(facts, source, frame):
+    return facts[source, frame], facts[source, SLOTS + frame]
+
+
 def tiles(x):
     return x.reshape(x.shape[0] // 8, 8, x.shape[1])
 
@@ -112,14 +118,14 @@
     return jnp.where(sub >= rest_row, 0.0, before).reshape(8, -1)
 
 
-def prepare_kernel(rows, cols, counts, amp_ref, probe_ref, order_ref, out_ref, weight_ref, total, side):
+def prepare_kernel(facts, amp_ref, probe_ref, order_ref, out_ref, weight_ref, total, side):
     band = weight_ref.shape[0]
     size = probe_ref.shape[1]
     half = size // 2
     total[...] = jnp.zeros_like(total)
 
     def add_power(source, frame, down):
-        start, rest_row, base, rest_col = placed(rows[source, frame], cols[source, frame])
+        start, rest_row, base, rest_col = placed(*corner(facts, source, frame))
         before = jnp.zeros((1, 8, 384), jnp.float32)
         for i in range(size // BLOCK):
             pr = probe_ref[0, i * BLOCK : (i + 1) * BLOCK, :]
@@ -138,8 +144,8 @@
         add_power(1, frame, 0)
         return carry
 
-    lax.fori_loop(0, counts[0], own, 0)
-    lax.fori_loop(0, counts[1], previous, 0)
+    lax.fori_loop(0, facts[0, COUNT], own, 0)
+    lax.fori_loop(0, facts[1, COUNT], previous, 0)
     for i in range(band // BLOCK):
         weight_ref[i * BLOCK : (i + 1) * BLOCK, :] = 1.0 / (
             total[band + i * BLOCK : band + (i + 1) * BLOCK, :] + 1.0
@@ -166,144 +172,193 @@
                 ]
         return carry
 
-    lax.fori_loop(0, counts[0], permute, 0)
+    lax.fori_loop(0, facts[0, COUNT], permute, 0)
 
 
 def frames_kernel(
-    rows, cols, counts, field_ref, rim_ref, probe_ref, amp_ref, tables_ref,
+    facts, field_ref, rim_ref, probe_ref, amp_ref, tables_ref,
     mine_ref, other_ref, own_ref, over_ref,
-    ext, amp, tables, win, xh, xl, fa, fb, total, grad, sems,
+    ext, probe, amp, tables, win, xh, xl, fa, fb, total, grad, sems, out_sems,
 ):
     band = field_ref.shape[1]
     size = probe_ref.shape[1]
     half = size // 2
     steps = half // BLOCK
-    loads = [
-        pltpu.make_async_copy(field_ref, ext.at[:, :band], sems.at[0]),
-        pltpu.make_async_copy(rim_ref, ext.at[:, band:], sems.at[1]),
-        pltpu.make_async_copy(tables_ref, tables, sems.at[2]),
-        pltpu.make_async_copy(amp_ref, amp, sems.at[3]),
-    ]
+    count = facts[0, COUNT]
+
+    pieces = []
+    for c in (0, 1):
+        for j in (0, 1):
+            rows = slice(j * half, (j + 1) * half)
+            pieces.append((field_ref.at[c, rows], ext.at[c, rows]))
+            pieces.append((rim_ref.at[c, rows], ext.at[c, band + j * half : band + (j + 1) * half]))
+    urgent = len(pieces)
+    for c in (0, 1):
+        pieces.append((probe_ref.at[c], probe.at[c]))
+    for k in range(4):
+        pieces.append((tables_ref.at[k], tables.at[k]))
+        pieces.append((amp_ref.at[k], amp.at[k]))
+    loads = [pltpu.make_async_copy(src, dst, sems.at[k]) for k, (src, dst) in enumerate(pieces)]
     for load in loads:
         load.start()
     total[...] = jnp.zeros_like(total)
     grad[...] = jnp.zeros_like(grad)
-    for load in loads[:2]:
+    for load in loads[: urgent + 2]:
         load.wait()
 
-    def keep(which, place, value):
+    def keep(b, which, place, value):
         high, low = split2(value)
-        xh[(which, *place)] = high
-        xl[(which, *place)] = low
-
-    def by_right(which, table):
-        high = xh[which]
-        x = jnp.concatenate([high, xl[which], high], axis=1)
+        xh[(b, which, *place)] = high
+        xl[(b, which, *place)] = low
+
+    def by_right(b, which, table):
+        high = xh[b, which]
+        x = jnp.concatenate([high, xl[b, which], high], axis=1)
         t = tables[table, 0]
         t = jnp.concatenate([t, t, tables[table, 1]], axis=0)
         return jnp.dot(x, t, preferred_element_type=jnp.float32)
 
-    def by_left(which, table):
-        high = xh[which]
-        x = jnp.concatenate([high, xl[which], high], axis=0)
+    def by_left(b, which, table):
+        high = xh[b, which]
+        x = jnp.concatenate([high, xl[b, which], high], axis=0)
         t = tables[table, 0]
         t = jnp.concatenate([t, t, tables[table, 1]], axis=1)
         return jnp.dot(t, x, preferred_element_type=jnp.float32)
 
-    def one_frame(frame, carry):
-        start, rest_row, base, rest_col = placed(rows[0, frame], cols[0, frame])
+    def cut(b, place):
+        start, rest_row, base, rest_col = place
 
         def into(c):
             def use(i, rows_cut):
-                win[c, i * BLOCK : (i + 1) * BLOCK, :] = rows_cut
+                win[b, c, i * BLOCK : (i + 1) * BLOCK, :] = rows_cut
 
             return use
 
         for c in (0, 1):
             read_window(
-                lambda at, count: ext[c, pl.ds(start + at, count), pl.ds(base, 384)],
+                lambda at, rows: ext[c, pl.ds(start + at, rows), pl.ds(base, 384)],
                 size, rest_row, rest_col, into(c),
             )
         for i in range(size // BLOCK):
             row = slice(i * BLOCK, (i + 1) * BLOCK)
-            wr, wi = win[0, row, :], win[1, row, :]
-            pr, pi = probe_ref[0, row, :], probe_ref[1, row, :]
+            wr, wi = win[b, 0, row, :], win[b, 1, row, :]
+            pr, pi = probe[0, row, :], probe[1, row, :]
             er = pr * wr - pi * wi
             ei = pr * wi + pi * wr
-            keep(0, (row, slice(0, half)), er[:, :half] + er[:, half:])
-            keep(0, (row, slice(half, size)), ei[:, :half] + ei[:, half:])
-            keep(1, (row, slice(0, half)), er[:, :half] - er[:, half:])
-            keep(1, (row, slice(half, size)), ei[:, :half] - ei[:, half:])
-
-        @pl.when(frame == 0)
-        def _():
-            for load in loads[2:]:
-                load.wait()
-
-        fa[...] = by_right(0, 1)
-        fb[...] = by_right(1, 3)
+            keep(b, 0, (row, slice(0, half)), er[:, :half] + er[:, half:])
+            keep(b, 0, (row, slice(half, size)), ei[:, :half] + ei[:, half:])
+            keep(b, 1, (row, slice(0, half)), er[:, :half] - er[:, half:])
+            keep(b, 1, (row, slice(half, size)), ei[:, :half] - ei[:, half:])
+
+    def right_forward(b):
+        fa[b] = by_right(b, 0, 1)
+        fb[b] = by_right(b, 1, 3)
+
+    def fold_rows(b):
         for i in range(steps):
             top = slice(i * BLOCK, (i + 1) * BLOCK)
             low = slice(half + i * BLOCK, half + (i + 1) * BLOCK)
             for ref, out in ((fa, slice(0, half)), (fb, slice(half, size))):
-                t, b = ref[top, :], ref[low, :]
-                s, d = t + b, t - b
-                keep(0, (top, out), s[:, :half])
-                keep(0, (low, out), s[:, half:])
-                keep(1, (top, out), d[:, :half])
-                keep(1, (low, out), d[:, half:])
-        fa[...] = by_left(0, 0)
-        fb[...] = by_left(1, 2)
+                t, u = ref[b, top, :], ref[b, low, :]
+                s, d = t + u, t - u
+                keep(b, 0, (top, out), s[:, :half])
+                keep(b, 0, (low, out), s[:, half:])
+                keep(b, 1, (top, out), d[:, :half])
+                keep(b, 1, (low, out), d[:, half:])
+
+    def left_forward(b):
+        fa[b] = by_left(b, 0, 0)
+        fb[b] = by_left(b, 1, 2)
+
+    def correct(b, frame, live):
         for i in range(steps):
             top = slice(i * BLOCK, (i + 1) * BLOCK)
             low = slice(half + i * BLOCK, half + (i + 1) * BLOCK)
             for which, ref in ((0, fa), (1, fb)):
-                re, im = ref[top, :], ref[low, :]
+                re, im = ref[b, top, :], ref[b, low, :]
                 a = amp[frame, pl.ds(which * half + i * BLOCK, BLOCK), :]
                 factor = 1.0 - a * lax.rsqrt(re * re + im * im + 0.25)
-                keep(which, (top, slice(0, size)), re * factor)
-                keep(which, (low, slice(0, size)), im * factor)
-        fa[...] = by_left(0, 1)
-        fb[...] = by_left(1, 3)
+                factor = jnp.where(live, factor, 0.0)
+                keep(b, which, (top, slice(0, size)), re * factor)
+                keep(b, which, (low, slice(0, size)), im * factor)
+
+    def left_back(b):
+        fa[b] = by_left(b, 0, 1)
+        fb[b] = by_left(b, 1, 3)
+
+    def unfold_rows(b):
         for i in range(steps):
             top = slice(i * BLOCK, (i + 1) * BLOCK)
             low = slice(half + i * BLOCK, half + (i + 1) * BLOCK)
             for part, out in ((top, slice(0, half)), (low, slice(half, size))):
-                p, q = fa[part, :], fb[part, :]
+                p, q = fa[b, part, :], fb[b, part, :]
                 s, d = p + q, p - q
                 for place, v in ((top, s), (low, d)):
-                    keep(0, (place, out), v[:, :half])
-                    keep(1, (place, out), v[:, half:])
-        fa[...] = by_right(0, 0)
-        fb[...] = by_right(1, 2)
+                    keep(b, 0, (place, out), v[:, :half])
+                    keep(b, 1, (place, out), v[:, half:])
+
+    def right_back(b):
+        fa[b] = by_right(b, 0, 0)
+        fb[b] = by_right(b, 1, 2)
+
+    def spread(b, place):
+        start, rest_row, base, rest_col = place
         before = [jnp.zeros((1, 8, 384), jnp.float32)] * 2
         for i in range(size // BLOCK):
             row = slice(i * BLOCK, (i + 1) * BLOCK)
-            p, q = fa[row, :], fb[row, :]
+            p, q = fa[b, row, :], fb[b, row, :]
             s, d = p + q, p - q
             br = jnp.concatenate([s[:, :half], d[:, :half]], axis=1)
             bi = jnp.concatenate([s[:, half:], d[:, half:]], axis=1)
-            wr, wi = win[0, row, :], win[1, row, :]
+            wr, wi = win[b, 0, row, :], win[b, 1, row, :]
             grad[0, row, :] = grad[0, row, :] + (wr * br + wi * bi)
             grad[1, row, :] = grad[1, row, :] + (wr * bi - wi * br)
-            pr, pi = probe_ref[0, row, :], probe_ref[1, row, :]
+            pr, pi = probe[0, row, :], probe[1, row, :]
             for c, v in ((0, pr * br + pi * bi), (1, pr * bi - pi * br)):
                 part, before[c] = moved_rows(moved_columns(v, rest_col), before[c], rest_row)
-                place = (c, pl.ds(start + i * BLOCK, BLOCK), pl.ds(base, 384))
-                total[place] = total[place] + part
+                at = (c, pl.ds(start + i * BLOCK, BLOCK), pl.ds(base, 384))
+                total[at] = total[at] + part
         for c in (0, 1):
-            place = (c, pl.ds(start + size, 8), pl.ds(base, 384))
-            total[place] = total[place] + last_rows(before[c], rest_row)
+            at = (c, pl.ds(start + size, 8), pl.ds(base, 384))
+            total[at] = total[at] + last_rows(before[c], rest_row)
+
+    def two_frames(pair, carry):
+        frames = (2 * pair, 2 * pair + 1)
+        places = [placed(*corner(facts, 0, frame)) for frame in frames]
+        both = (0, 1)
+        cut(0, places[0])
+
+        @pl.when(pair == 0)
+        def _():
+            for load in loads[urgent + 2 :]:
+                load.wait()
+
+        right_forward(0)
+        cut(1, places[1])
+        right_forward(1)
+        for elementwise, product in (
+            (lambda b: fold_rows(b), left_forward),
+            (lambda b: correct(b, frames[b], frames[b] < count), left_back),
+            (lambda b: unfold_rows(b), right_back),
+        ):
+            for b in both:
+                elementwise(b)
+                product(b)
+        for b in both:
+            spread(b, places[b])
         return carry
 
-    lax.fori_loop(0, counts[0], one_frame, 0)
-    stores = [
-        pltpu.make_async_copy(total.at[:, band:], over_ref, sems.at[0]),
-        pltpu.make_async_copy(total.at[:, :band], own_ref, sems.at[1]),
-    ]
+    lax.fori_loop(0, (count + 1) // 2, two_frames, 0)
+    stores = []
+    for c in (0, 1):
+        for j in (0, 1):
+            rows = slice(j * half, (j + 1) * half)
+            stores.append((total.at[c, band + j * half : band + (j + 1) * half], over_ref.at[c, rows]))
+            stores.append((total.at[c, rows], own_ref.at[c, rows]))
+    stores = [pltpu.make_async_copy(src, dst, out_sems.at[k]) for k, (src, dst) in enumerate(stores)]
     for store in stores:
         store.start()
-    first = counts[2] == 0
+    first = facts[0, CORE] == 0
     for i in range(size // BLOCK):
         row = slice(i * BLOCK, (i + 1) * BLOCK)
         re, im = grad[0, row, :], grad[1, row, :]
@@ -311,6 +366,16 @@
         other_ref[row, :] = jnp.where(first, im, re)
     for store in stores:
         store.wait()
+
+
+def update_kernel(facts, mine_ref, other_ref, probe_ref, out_ref):
+    size = mine_ref.shape[0]
+    mine, other = mine_ref[...], other_ref[...]
+    squares = jnp.sum(mine * mine + other * other)
+    step = 0.25 * lax.rsqrt(jnp.full((1, 1), squares / (2 * size * size) + 1e-06, jnp.float32))
+    first = facts[0, CORE] == 0
+    out_ref[0] = probe_ref[0] - step * jnp.where(first, mine, other)
+    out_ref[1] = probe_ref[1] - step * jnp.where(first, other, mine)
 
 
 def place_of(device):
@@ -352,12 +417,10 @@
     peers = lax.axis_size("dev")
 
     rim = lax.ppermute(object_field, "dev", [(i, i - 1) for i in range(1, peers)])
-    facts = jnp.concatenate([row_offset[0, 0], col_offset[0, 0], frame_count[0]])
+    core = (lax.axis_index("dev") % 2).astype(jnp.int32)
+    facts = jnp.concatenate([row_offset[0, 0], col_offset[0, 0], frame_count[0], core[None]])
     facts_before = lax.ppermute(facts, "dev", [(i, i + 1) for i in range(peers - 1)])
-    both = jnp.stack([facts, facts_before])
-    rows, cols = both[:, :slots], both[:, slots : 2 * slots]
-    core = lax.axis_index("dev") % 2
-    counts = jnp.concatenate([both[:, 2 * slots], core[None]])
+    facts = jnp.stack([facts, facts_before])
 
     ordered, scale = pl.pallas_call(
         prepare_kernel,
@@ -365,7 +428,7 @@
             jax.ShapeDtypeStruct((slots, size, size), f32),
             jax.ShapeDtypeStruct((band, width), f32),
         ),
-        in_specs=[smem, smem, smem, vmem, vmem, vmem],
+        in_specs=[smem, vmem, vmem, vmem],
         out_specs=(vmem, vmem),
         scratch_shapes=[
             pltpu.VMEM((2 * band + size, width), f32),
@@ -374,7 +437,7 @@
         compiler_params=pltpu.CompilerParams(vmem_limit_bytes=65000 * 1024),
         cost_estimate=pl.CostEstimate(flops=800_000_000, bytes_accessed=3_200_000, transcendentals=0),
         name="prepare",
-    )(rows, cols, counts, amplitudes[0, 0], probe, jnp.asarray(order_table(size)))
+    )(facts, amplitudes[0, 0], probe, jnp.asarray(order_table(size)))
 
     bf16 = jnp.bfloat16
     mine, other, own, over = pl.pallas_call(
@@ -385,28 +448,28 @@
             jax.ShapeDtypeStruct((2, band, width), f32),
             jax.ShapeDtypeStruct((2, size, width), f32),
         ),
-        in_specs=[smem, smem, smem, hbm, hbm, vmem, hbm, hbm],
+        in_specs=[smem, hbm, hbm, hbm, hbm, hbm],
         out_specs=(vmem, vmem, hbm, hbm),
         scratch_shapes=[
             pltpu.VMEM((2, band + size, width), f32),
+            pltpu.VMEM((2, size, size), f32),
             pltpu.VMEM((slots, size, size), f32),
             pltpu.VMEM((4, 2, size, size), bf16),
+            pltpu.VMEM((2, 2, size, size), f32),
+            pltpu.VMEM((2, 2, size, size), bf16),
+            pltpu.VMEM((2, 2, size, size), bf16),
             pltpu.VMEM((2, size, size), f32),
-            pltpu.VMEM((2, size, size), bf16),
-            pltpu.VMEM((2, size, size), bf16),
-            pltpu.VMEM((size, size), f32),
-            pltpu.VMEM((size, size), f32),
+            pltpu.VMEM((2, size, size), f32),
             pltpu.VMEM((2, band + size, width), f32),
             pltpu.VMEM((2, size, size), f32),
-            pltpu.SemaphoreType.DMA((4,)),
+            pltpu.SemaphoreType.DMA((18,)),
+            pltpu.SemaphoreType.DMA((8,)),
         ],
-        compiler_params=pltpu.CompilerParams(vmem_limit_bytes=60 * 1024 * 1024),
+        compiler_params=pltpu.CompilerParams(vmem_limit_bytes=64500 * 1024),
         cost_estimate=pl.CostEstimate(flops=3_300_000_000, bytes_accessed=8_000_000, transcendentals=262144),
         name="frames",
-    )(rows, cols, counts, object_field, rim, probe, ordered, jnp.asarray(frame_tables(size)))
-
-    first = core == 0
-    mine, other, first = lax.optimization_barrier((mine, other, first))
+    )(facts, object_field, rim, probe, ordered, jnp.asarray(frame_tables(size)))
+
     swap = [(i, i ^ 1) for i in range(peers)]
     plane = mine + lax.ppermute(other, "dev", swap)
     parts = exchanged(plane.reshape(32, size // 32, size), WIDE)
@@ -420,11 +483,15 @@
         [own[:, :size] + incoming, own[:, size:]], axis=1
     ) * scale[None]
 
-    squares = jnp.sum(plane * plane + plane_other * plane_other)
-    step = 0.25 * lax.rsqrt(squares / (2 * size * size) + 1e-06)
-    real = jnp.where(first, plane, plane_other)
-    imag = jnp.where(first, plane_other, plane)
-    new_probe = jnp.stack([probe[0] - step * real, probe[1] - step * imag])
+    new_probe = pl.pallas_call(
+        update_kernel,
+        out_shape=jax.ShapeDtypeStruct(probe.shape, f32),
+        in_specs=[smem, vmem, vmem, vmem],
+        out_specs=vmem,
+        compiler_params=pltpu.CompilerParams(vmem_limit_bytes=8 * 1024 * 1024),
+        cost_estimate=pl.CostEstimate(flops=1_000_000, bytes_accessed=1_600_000, transcendentals=1),
+        name="update",
+    )(facts, plane, plane_other, probe)
     return (new_field, new_probe)
 
 

time: 105 us -> 98.8 us (0.941)
  other arithmetic: 6.81 us -> 3.89 us
  Pallas kernels: 16.1 us -> 13.3 us
  starting transfers between devices: 34.6 us -> 37 us
    pallas_call x1, Pallas kernels: 11.7 us -> 7.71 us  [on_device(): pl.pallas_call(frames_kernel, out_shape=(jax.ShapeDtypeStruct((size, size...]
    pallas_call x0 -> x1, Pallas kernels: none -> 1.64 us  [on_device(): pl.pallas_call(update_kernel, out_shape=jax.ShapeDtypeStruct(probe.shape,...]
    all_to_all x1, starting transfers between devices: 16.8 us -> 18.4 us  [exchanged(): lax.all_to_all(parts, AXES, 0, 0, tiled=True, axis_index_groups=groups_al...]
    sub x1, other arithmetic: 2.62 us -> 1.39 us  [on_device(): object_field - jnp.concatenate([own[:, :size] + incoming, own[:, size:]],...]
  transfers between devices with their start and end apart: 6 -> 6, of which waited for: 3 -> 4; matrix products, arithmetic and copies ran while one was open for 4% -> 2% of each run, Pallas kernels for 4% -> 4%
where the time goes in v2:
time: 98.8 us; the launch traced here: 98.3 us
  starting transfers between devices  37 us (37%)
  blocking collectives  31.6 us (32%)
  Pallas kernels  13.3 us (13%)
  waiting for transfers between devices  10.3 us (10%)
  other arithmetic  3.89 us (4%)
  between operations  1.45 us (1%)
    all_to_all x2, blocking collectives, exchanged(): lax.all_to_all(parts, AXES, 0, 0, tiled=True, axis_index_groups=groups_al...  31.6 us
    all_to_all x1, starting transfers between devices, exchanged(): lax.all_to_all(parts, AXES, 0, 0, tiled=True, axis_index_groups=groups_al...  18.4 us
    ppermute x1, starting transfers between devices, on_device(): lax.ppermute(object_field, 'dev', [(i, i - 1) for i in range(1, peers)])  8.79 us
    pallas_call x1, Pallas kernels, on_device(): pl.pallas_call(frames_kernel, out_shape=(jax.ShapeDtypeStruct((size, size...  7.71 us
    all_to_all x1, waiting for transfers between devices, exchanged(): lax.all_to_all(parts, AXES, 0, 0, tiled=True, axis_index_groups=groups_al...  7.08 us
    pallas_call x1, Pallas kernels, on_device(): pl.pallas_call(prepare_kernel, out_shape=(jax.ShapeDtypeStruct((slots, si...  3.95 us
    ppermute x1, starting transfers between devices, on_device(): plane_other = lax.ppermute(plane, 'dev', swap)  3.2 us
    ppermute x1, starting transfers between devices, on_device(): incoming = lax.ppermute(over, 'dev', [(i, i + 1) for i in range(peers - 1)])  2.86 us
  transfers between devices with their start and end apart: 6, of which 4 were waited for; matrix products, arithmetic and copies ran while one was open for 2% of the time, Pallas kernels for 4%

profile of v2, /device:TPU:1, one launch (start us, length us, event | category | flops | bytes accessed | tf_op | source)
XLA Modules:
  0.0 98.3 jit_solution(11434236820888139413)
XLA Ops:
  0.6 8.8 %collective-permute-start.1 = (f32[2,256,512]{2,1,0:T(8,128)}, f32[2,256,512]{2,1,0:T(8,128)}, u32[]{:S(2)}, u32[]{:S(2)}) collective-permute-start(f32[2,256,512]{2,1,0:T(8,128)} %field_ref.1), channel_id=1, source_target_pairs={{1,0},{2,1},{3,2},{4,3},{5,4},{6,5},{7,6},{8,7},{9,8},{10,9},{11,1... | collective-permute-start | bytes 3145736 | tf_op jit(solution)/shard_map/ppermute | solution.py:419
  10.1 0.0 copy-start.5
  10.1 0.0 copy-start.6
  10.1 0.6 copy-done.5
  10.7 0.0 copy-done.6
  10.8 0.1 pad_add_fusion.1
  10.8 1.9 %collective-permute-start = (s32[10]{0:T(128)S(1)}, s32[10]{0:T(128)S(1)}, u32[]{:S(2)}, u32[]{:S(2)}) collective-permute-start(s32[10]{0:T(128)S(1)} %pad_add_fusion.1), channel_id=1, source_target_pairs={{0,1},{1,2},{2,3},{3,4},{4,5},{5,6},{6,7},{7,8},{8,9},{9,10},{10,1... | collective-permute-start | bytes 128 | tf_op jit(solution)/shard_map/ppermute | solution.py:422
  12.8 1.1 %collective-permute-done = s32[10]{0:T(128)S(1)} collective-permute-done((s32[10]{0:T(128)S(1)}, s32[10]{0:T(128)S(1)}, u32[]{:S(2)}, u32[]{:S(2)}) %collective-permute-start) | collective-permute-done | bytes 72 | tf_op jit(solution)/shard_map/ppermute | solution.py:422
  13.8 0.6 pad_add_fusion.facts
  14.4 3.9 %prepare.1 = (f32[4,256,256]{2,1,0:T(8,128)}, f32[256,512]{1,0:T(8,128)}) custom-call(s32[2,10]{1,0:T(2,128)} %pad_add_fusion.facts, f32[4,256,256]{2,1,0:T(8,128)} %bitcast.17, f32[2,256,256]{2,1,0:T(8,128)} %probe_ref.5, bf16[256,256]{1,0:T(8,128)(2,1)} %constant.23.clone.order_ref), custom_call_target="tpu_custom_call" | custom-call | flops 800000000 | bytes 3200000 | tf_op jit(solution)/shard_map/prepare/pallas_call | solution.py:425
  18.4 0.4 collective-permute-done.1.rim_ref
  18.8 7.7 %frames.1 = (f32[256,256]{1,0:T(8,128)}, f32[256,256]{1,0:T(8,128)}, f32[2,256,512]{2,1,0:T(8,128)}, f32[2,256,512]{2,1,0:T(8,128)}) custom-call(s32[2,10]{1,0:T(2,128)} %pad_add_fusion.facts, f32[2,256,512]{2,1,0:T(8,128)} %field_ref.1, f32[2,256,512]{2,1,0:T(8,128)} %collective-permute-done.1.rim_ref, f32[2,256,256]{2,1,0:T(8,128)} %probe_ref.5, ...), custom_call_target="tpu_custom_call" | custom-call | flops 3300000000 | bytes 8000000 | tf_op jit(solution)/shard_map/frames/pallas_call | solution.py:443
  26.5 1.9 %collective-permute-start.3 = (f32[256,256]{1,0:T(8,128)}, f32[256,256]{1,0:T(8,128)S(1)}, u32[]{:S(2)}, u32[]{:S(2)}) collective-permute-start(f32[256,256]{1,0:T(8,128)} %get-tuple-element.13), channel_id=1, source_target_pairs={{0,1},{1,0},{2,3},{3,2},{4,5},{5,4},{6,7},{7,6},{8,9},{9,8},{10,11... | collective-permute-start | bytes 786440 | tf_op jit(solution)/shard_map/ppermute | solution.py:474
  28.5 1.7 %collective-permute-done.3 = f32[256,256]{1,0:T(8,128)S(1)} collective-permute-done((f32[256,256]{1,0:T(8,128)}, f32[256,256]{1,0:T(8,128)S(1)}, u32[]{:S(2)}, u32[]{:S(2)}) %collective-permute-start.3) | collective-permute-done | bytes 262176 | tf_op jit(solution)/shard_map/ppermute | solution.py:474
  30.2 0.0 copy-start.3
  30.2 1.8 %add_bitcast_fusion = f32[32,8,256]{2,1,0:T(8,128)} fusion(f32[256,256]{1,0:T(8,128)} %get-tuple-element.12, f32[256,256]{1,0:T(8,128)S(1)} %collective-permute-done.3), kind=kLoop, calls=%fused_computation.1 | loop fusion | flops 65536 | bytes 786432 | tf_op jit(solution)/shard_map/reshape | solution.py:475
  32.0 0.0 copy-start.2
  32.0 18.4 %all-to-all-start = ((f32[32,8,256]{2,1,0:T(8,128)}), f32[32,8,256]{2,1,0:T(8,128)S(1)}, u32[]{:S(2)}, u32[]{:S(2)}) async-start(f32[32,8,256]{2,1,0:T(8,128)} %add_bitcast_fusion), calls=%async_computation | async-start | bytes 524288 | tf_op jit(solution)/shard_map/all_to_all | solution.py:401
  50.3 2.9 %collective-permute-start.2 = (f32[2,256,512]{2,1,0:T(8,128)}, f32[2,256,512]{2,1,0:T(8,128)S(1)}, u32[]{:S(2)}, u32[]{:S(2)}) collective-permute-start(f32[2,256,512]{2,1,0:T(8,128)} %get-tuple-element.10), channel_id=1, source_target_pairs={{0,1},{1,2},{2,3},{3,4},{4,5},{5,6},{6,7},{7,8},{8,9},{9,10},{10,1... | collective-permute-start | bytes 3145736 | tf_op jit(solution)/shard_map/ppermute | solution.py:481
  53.2 7.1 %all-to-all-done = f32[32,8,256]{2,1,0:T(8,128)S(1)} async-done(((f32[32,8,256]{2,1,0:T(8,128)}), f32[32,8,256]{2,1,0:T(8,128)S(1)}, u32[]{:S(2)}, u32[]{:S(2)}) %all-to-all-start) | async-done | bytes 262176 | tf_op jit(solution)/shard_map/all_to_all | solution.py:401
  60.3 13.9 %all_to_all.15 = f32[8,8,256]{2,1,0:T(8,128)S(1)} all-to-all(f32[8,8,256]{2,1,0:T(8,128)S(1)} %broadcast_in_dim.7), channel_id=1, replica_groups={{0,8,16,24,32,40,48,56},{1,3,5,7,65,67,69,71},{2,10,18,26,34,42,50,58},..., dimensions={0} | all-to-all | bytes 131072 | tf_op jit(solution)/shard_map/all_to_all | solution.py:401
  74.2 0.0 copy-start.4
  74.3 17.7 %all_to_all.16 = f32[32,8,256]{2,1,0:T(8,128)S(1)} all-to-all(f32[32,8,256]{2,1,0:T(8,128)S(1)} %broadcast_in_dim.8), channel_id=1, replica_groups={{0,2,4,6,64,66,68,70,128,130,132,134,192,194,196,198,256,258,260,262,32..., dimensions={0} | all-to-all | bytes 524288 | tf_op jit(solution)/shard_map/all_to_all | solution.py:401
  92.0 3.2 %collective-permute-start.4 = (f32[256,256]{1,0:T(8,128)S(1)}, f32[256,256]{1,0:T(8,128)S(1)}, u32[]{:S(2)}, u32[]{:S(2)}) collective-permute-start(f32[256,256]{1,0:T(8,128)S(1)} %bitcast.11), channel_id=1, source_target_pairs={{0,1},{1,0},{2,3},{3,2},{4,5},{5,4},{6,7},{7,6},{8,9},{9,8},{10,11... | collective-permute-start | bytes 786440 | tf_op jit(solution)/shard_map/ppermute | solution.py:479
  95.2 0.0 collective-permute-done.2
  95.2 0.0 copy-done.3
  95.2 0.0 copy-done.2
  95.2 0.0 copy-done.4
  95.2 0.0 copy-start
  95.2 0.0 copy-start.1
  95.3 1.4 %multiply_subtract_fusion = f32[2,256,512]{2,1,0:T(8,128)} fusion(f32[2,256,512]{2,1,0:T(8,128)S(1)} %copy-done.2, f32[2,256,512]{2,1,0:T(8,128)S(1)} %copy-done.3, f32[2,256,512]{2,1,0:T(8,128)S(1)} %collective-permute-done.2, f32[256,512]{1,0:T(8,128)S(1)} %copy-done.4), kind=kLoop, calls=%fused_computation | loop fusion | flops 786432 | bytes 4718592 | tf_op jit(solution)/shard_map/sub | solution.py:482
  96.7 0.0 collective-permute-done.4.other_ref
  96.7 0.0 copy-done
  96.7 0.0 copy-done.1
  96.7 1.6 %update.1 = f32[2,256,256]{2,1,0:T(8,128)} custom-call(s32[2,10]{1,0:T(2,128)S(1)} %copy-done.1, f32[256,256]{1,0:T(8,128)S(1)} %bitcast.12, f32[256,256]{1,0:T(8,128)S(1)} %collective-permute-done.4.other_ref, f32[2,256,256]{2,1,0:T(8,128)S(1)} %copy-done), custom_call_target="tpu_custom_call" | custom-call | flops 1000000 | bytes 1600000 | tf_op jit(solution)/shard_map/update/pallas_call | solution.py:486
  (4 shorter events, 0.1 us)
Async XLA Ops:
  0.6 18.2 %collective-permute-start.1 = (f32[2,256,512]{2,1,0:T(8,128)}, f32[2,256,512]{2,1,0:T(8,128)}, u32[]{:S(2)}, u32[]{:S(2)}) collective-permute-start(f32[2,256,512]{2,1,0:T(8,128)} %field_ref.1), channel_id=1, source_target_pairs={{1,0},{2,1},{3,2},{4,3},{5,4},{6,5},{7,6},{8,7},{9,8},{10,9},{11,1... | collective-permute-start | bytes 3145736 | tf_op jit(solution)/shard_map/ppermute | solution.py:419
  10.1 0.7 copy-start.5
  10.1 0.7 copy-start.6
  10.8 3.0 %collective-permute-start = (s32[10]{0:T(128)S(1)}, s32[10]{0:T(128)S(1)}, u32[]{:S(2)}, u32[]{:S(2)}) collective-permute-start(s32[10]{0:T(128)S(1)} %pad_add_fusion.1), channel_id=1, source_target_pairs={{0,1},{1,2},{2,3},{3,4},{4,5},{5,6},{6,7},{7,8},{8,9},{9,10},{10,1... | collective-permute-start | bytes 128 | tf_op jit(solution)/shard_map/ppermute | solution.py:422
  26.5 3.6 %collective-permute-start.3 = (f32[256,256]{1,0:T(8,128)}, f32[256,256]{1,0:T(8,128)S(1)}, u32[]{:S(2)}, u32[]{:S(2)}) collective-permute-start(f32[256,256]{1,0:T(8,128)} %get-tuple-element.13), channel_id=1, source_target_pairs={{0,1},{1,0},{2,3},{3,2},{4,5},{5,4},{6,7},{7,6},{8,9},{9,8},{10,11... | collective-permute-start | bytes 786440 | tf_op jit(solution)/shard_map/ppermute | solution.py:474
  30.2 65.0 %copy-start.3 = (f32[2,256,512]{2,1,0:T(8,128)S(1)}, f32[2,256,512]{2,1,0:T(8,128)}, u32[]{:S(2)}) copy-start(f32[2,256,512]{2,1,0:T(8,128)} %get-tuple-element.9) | copy-start | bytes 3145732
  32.0 63.3 %copy-start.2 = (f32[2,256,512]{2,1,0:T(8,128)S(1)}, f32[2,256,512]{2,1,0:T(8,128)}, u32[]{:S(2)}) copy-start(f32[2,256,512]{2,1,0:T(8,128)} %field_ref.1) | copy-start | bytes 3145732
  32.0 28.3 %all-to-all-start = ((f32[32,8,256]{2,1,0:T(8,128)}), f32[32,8,256]{2,1,0:T(8,128)S(1)}, u32[]{:S(2)}, u32[]{:S(2)}) async-start(f32[32,8,256]{2,1,0:T(8,128)} %add_bitcast_fusion), calls=%async_computation | async-start | bytes 524288 | tf_op jit(solution)/shard_map/all_to_all | solution.py:401
  50.3 44.9 %collective-permute-start.2 = (f32[2,256,512]{2,1,0:T(8,128)}, f32[2,256,512]{2,1,0:T(8,128)S(1)}, u32[]{:S(2)}, u32[]{:S(2)}) collective-permute-start(f32[2,256,512]{2,1,0:T(8,128)} %get-tuple-element.10), channel_id=1, source_target_pairs={{0,1},{1,2},{2,3},{3,4},{4,5},{5,6},{6,7},{7,8},{8,9},{9,10},{10,1... | collective-permute-start | bytes 3145736 | tf_op jit(solution)/shard_map/ppermute | solution.py:481
  74.2 21.0 %copy-start.4 = (f32[256,512]{1,0:T(8,128)S(1)}, f32[256,512]{1,0:T(8,128)}, u32[]{:S(2)}) copy-start(f32[256,512]{1,0:T(8,128)} %get-tuple-element.11) | copy-start | bytes 1572868
  92.0 4.7 %collective-permute-start.4 = (f32[256,256]{1,0:T(8,128)S(1)}, f32[256,256]{1,0:T(8,128)S(1)}, u32[]{:S(2)}, u32[]{:S(2)}) collective-permute-start(f32[256,256]{1,0:T(8,128)S(1)} %bitcast.11), channel_id=1, source_target_pairs={{0,1},{1,0},{2,3},{3,2},{4,5},{5,4},{6,7},{7,6},{8,9},{9,8},{10,11... | collective-permute-start | bytes 786440 | tf_op jit(solution)/shard_map/ppermute | solution.py:479
  95.2 1.4 %copy-start = (f32[2,256,256]{2,1,0:T(8,128)S(1)}, f32[2,256,256]{2,1,0:T(8,128)}, u32[]{:S(2)}) copy-start(f32[2,256,256]{2,1,0:T(8,128)} %probe_ref.5) | copy-start | bytes 1572868
  95.2 1.4 %copy-start.1 = (s32[2,10]{1,0:T(2,128)S(1)}, s32[2,10]{1,0:T(2,128)}, u32[]{:S(2)}) copy-start(s32[2,10]{1,0:T(2,128)} %pad_add_fusion.facts) | copy-start | bytes 244

commit v3 on v2

--- a/solution.py
+++ b/solution.py
@@ -176,34 +176,30 @@
 
 
 def frames_kernel(
-    facts, field_ref, rim_ref, probe_ref, amp_ref, tables_ref,
-    mine_ref, other_ref, own_ref, over_ref,
-    ext, probe, amp, tables, win, xh, xl, fa, fb, total, grad, sems, out_sems,
+    facts, field_ref, rim_ref, probe, amp, tables,
+    mine_ref, other_ref, total,
+    ext, win, xh, xl, fa, fb, grad, sems,
 ):
     band = field_ref.shape[1]
-    size = probe_ref.shape[1]
+    size = probe.shape[1]
     half = size // 2
     steps = half // BLOCK
     count = facts[0, COUNT]
 
-    pieces = []
+    loads = []
     for c in (0, 1):
         for j in (0, 1):
             rows = slice(j * half, (j + 1) * half)
-            pieces.append((field_ref.at[c, rows], ext.at[c, rows]))
-            pieces.append((rim_ref.at[c, rows], ext.at[c, band + j * half : band + (j + 1) * half]))
-    urgent = len(pieces)
-    for c in (0, 1):
-        pieces.append((probe_ref.at[c], probe.at[c]))
-    for k in range(4):
-        pieces.append((tables_ref.at[k], tables.at[k]))
-        pieces.append((amp_ref.at[k], amp.at[k]))
-    loads = [pltpu.make_async_copy(src, dst, sems.at[k]) for k, (src, dst) in enumerate(pieces)]
+            under = slice(band + j * half, band + (j + 1) * half)
+            loads.append(
+                pltpu.make_async_copy(rim_ref.at[c, rows], ext.at[c, under], sems.at[2 * c + j])
+            )
     for load in loads:
         load.start()
+    ext[:, :band] = field_ref[...]
     total[...] = jnp.zeros_like(total)
     grad[...] = jnp.zeros_like(grad)
-    for load in loads[: urgent + 2]:
+    for load in loads:
         load.wait()
 
     def keep(b, which, place, value):
@@ -327,12 +323,6 @@
         places = [placed(*corner(facts, 0, frame)) for frame in frames]
         both = (0, 1)
         cut(0, places[0])
-
-        @pl.when(pair == 0)
-        def _():
-            for load in loads[urgent + 2 :]:
-                load.wait()
-
         right_forward(0)
         cut(1, places[1])
         right_forward(1)
@@ -349,23 +339,12 @@
         return carry
 
     lax.fori_loop(0, (count + 1) // 2, two_frames, 0)
-    stores = []
-    for c in (0, 1):
-        for j in (0, 1):
-            rows = slice(j * half, (j + 1) * half)
-            stores.append((total.at[c, band + j * half : band + (j + 1) * half], over_ref.at[c, rows]))
-            stores.append((total.at[c, rows], own_ref.at[c, rows]))
-    stores = [pltpu.make_async_copy(src, dst, out_sems.at[k]) for k, (src, dst) in enumerate(stores)]
-    for store in stores:
-        store.start()
     first = facts[0, CORE] == 0
     for i in range(size // BLOCK):
         row = slice(i * BLOCK, (i + 1) * BLOCK)
         re, im = grad[0, row, :], grad[1, row, :]
         mine_ref[row, :] = jnp.where(first, re, im)
         other_ref[row, :] = jnp.where(first, im, re)
-    for store in stores:
-        store.wait()
 
 
 def update_kernel(facts, mine_ref, other_ref, probe_ref, out_ref):
@@ -417,6 +396,7 @@
     peers = lax.axis_size("dev")
 
     rim = lax.ppermute(object_field, "dev", [(i, i - 1) for i in range(1, peers)])
+    rim = pltpu.with_memory_space_constraint(rim, pltpu.HBM)
     core = (lax.axis_index("dev") % 2).astype(jnp.int32)
     facts = jnp.concatenate([row_offset[0, 0], col_offset[0, 0], frame_count[0], core[None]])
     facts_before = lax.ppermute(facts, "dev", [(i, i + 1) for i in range(peers - 1)])
@@ -434,41 +414,36 @@
             pltpu.VMEM((2 * band + size, width), f32),
             pltpu.VMEM((size, size // 2), f32),
         ],
-        compiler_params=pltpu.CompilerParams(vmem_limit_bytes=65000 * 1024),
+        compiler_params=pltpu.CompilerParams(vmem_limit_bytes=24000 * 1024),
         cost_estimate=pl.CostEstimate(flops=800_000_000, bytes_accessed=3_200_000, transcendentals=0),
         name="prepare",
     )(facts, amplitudes[0, 0], probe, jnp.asarray(order_table(size)))
 
     bf16 = jnp.bfloat16
-    mine, other, own, over = pl.pallas_call(
+    mine, other, total = pl.pallas_call(
         frames_kernel,
         out_shape=(
             jax.ShapeDtypeStruct((size, size), f32),
             jax.ShapeDtypeStruct((size, size), f32),
-            jax.ShapeDtypeStruct((2, band, width), f32),
-            jax.ShapeDtypeStruct((2, size, width), f32),
+            jax.ShapeDtypeStruct((2, band + size, width), f32),
         ),
-        in_specs=[smem, hbm, hbm, hbm, hbm, hbm],
-        out_specs=(vmem, vmem, hbm, hbm),
+        in_specs=[smem, vmem, hbm, vmem, vmem, vmem],
+        out_specs=(vmem, vmem, vmem),
         scratch_shapes=[
             pltpu.VMEM((2, band + size, width), f32),
-            pltpu.VMEM((2, size, size), f32),
-            pltpu.VMEM((slots, size, size), f32),
-            pltpu.VMEM((4, 2, size, size), bf16),
             pltpu.VMEM((2, 2, size, size), f32),
             pltpu.VMEM((2, 2, size, size), bf16),
             pltpu.VMEM((2, 2, size, size), bf16),
             pltpu.VMEM((2, size, size), f32),
             pltpu.VMEM((2, size, size), f32),
-            pltpu.VMEM((2, band + size, width), f32),
             pltpu.VMEM((2, size, size), f32),
-            pltpu.SemaphoreType.DMA((18,)),
-            pltpu.SemaphoreType.DMA((8,)),
+            pltpu.SemaphoreType.DMA((4,)),
         ],
-        compiler_params=pltpu.CompilerParams(vmem_limit_bytes=64500 * 1024),
+        compiler_params=pltpu.CompilerParams(vmem_limit_bytes=24 * 1024 * 1024),
         cost_estimate=pl.CostEstimate(flops=3_300_000_000, bytes_accessed=8_000_000, transcendentals=262144),
         name="frames",
     )(facts, object_field, rim, probe, ordered, jnp.asarray(frame_tables(size)))
+    own, over = total[:, :band], total[:, band:]
 
     swap = [(i, i ^ 1) for i in range(peers)]
     plane = mine + lax.ppermute(other, "dev", swap)

time: 98.8 us -> 97.2 us (0.984)
  starting transfers between devices: 37 us -> 31.5 us
  local copies, waits for them, and re-layouts: 0.71 us -> 6.01 us
  Pallas kernels: 13.3 us -> 11.8 us
  waiting for transfers between devices: 10.3 us -> 9.09 us
    unnamed x14 -> x18, local copies, waits for them, and re-layouts: 0.68 us -> 4.95 us
    all_to_all x1, starting transfers between devices: 18.4 us -> 14.3 us  [exchanged(): lax.all_to_all(parts, AXES, 0, 0, tiled=True, axis_index_groups=groups_al...]
    sub x1, other arithmetic: 1.39 us -> 2.81 us  [on_device(): object_field - jnp.concatenate([own[:, :size] + incoming, own[:, size:]],...]
    pallas_call x1, Pallas kernels: 3.95 us -> 2.87 us  [on_device(): pl.pallas_call(prepare_kernel, out_shape=(jax.ShapeDtypeStruct((slots, si...]
    slice x0 -> x1, local copies, waits for them, and re-layouts: none -> 1.04 us  [on_device(): own, over = (total[:, :band], total[:, band:])]
    reshape x1, other arithmetic: 1.78 us -> 0.75 us  [on_device(): parts = exchanged(plane.reshape(32, size // 32, size), WIDE)]
  transfers between devices with their start and end apart: 6 -> 6, of which waited for: 4 -> 3; matrix products, arithmetic and copies ran while one was open for 2% -> 5% of each run, Pallas kernels for 4% -> 3%
where the time goes in v3:
time: 97.2 us; the launch traced here: 96.7 us
  blocking collectives  32.5 us (33%)
  starting transfers between devices  31.5 us (32%)
  Pallas kernels  11.8 us (12%)
  waiting for transfers between devices  9.09 us (9%)
  local copies, waits for them, and re-layouts  6.01 us (6%)
  other arithmetic  4.37 us (4%)
  between operations  1.42 us (1%)
    all_to_all x2, blocking collectives, exchanged(): lax.all_to_all(parts, AXES, 0, 0, tiled=True, axis_index_groups=groups_al...  32.5 us
    all_to_all x1, starting transfers between devices, exchanged(): lax.all_to_all(parts, AXES, 0, 0, tiled=True, axis_index_groups=groups_al...  14.3 us
    ppermute x1, starting transfers between devices, on_device(): lax.ppermute(object_field, 'dev', [(i, i - 1) for i in range(1, peers)])  8.92 us
    pallas_call x1, Pallas kernels, on_device(): pl.pallas_call(frames_kernel, out_shape=(jax.ShapeDtypeStruct((size, size...  7.31 us
    all_to_all x1, waiting for transfers between devices, exchanged(): lax.all_to_all(parts, AXES, 0, 0, tiled=True, axis_index_groups=groups_al...  6.49 us
    unnamed x18, local copies, waits for them, and re-layouts  4.95 us
    pallas_call x1, Pallas kernels, on_device(): pl.pallas_call(prepare_kernel, out_shape=(jax.ShapeDtypeStruct((slots, si...  2.87 us
    sub x1, other arithmetic, on_device(): object_field - jnp.concatenate([own[:, :size] + incoming, own[:, size:]],...  2.81 us
  transfers between devices with their start and end apart: 6, of which 3 were waited for; matrix products, arithmetic and copies ran while one was open for 5% of the time, Pallas kernels for 3%

profile of v3, /device:TPU:1, one launch (start us, length us, event | category | flops | bytes accessed | tf_op | source)
XLA Modules:
  0.0 96.7 jit_solution(6337306968137984776)
XLA Ops:
  0.6 0.0 copy-start
  0.6 8.9 %collective-permute-start.1 = (f32[2,256,512]{2,1,0:T(8,128)}, f32[2,256,512]{2,1,0:T(8,128)S(1)}, u32[]{:S(2)}, u32[]{:S(2)}) collective-permute-start(f32[2,256,512]{2,1,0:T(8,128)} %field_ref.1), channel_id=1, source_target_pairs={{1,0},{2,1},{3,2},{4,3},{5,4},{6,5},{7,6},{8,7},{9,8},{10,9},{11,1... | collective-permute-start | bytes 3145736 | tf_op jit(solution)/shard_map/ppermute | solution.py:398
  10.2 0.8 pad_add_fusion.1
  11.0 1.9 %collective-permute-start = (s32[10]{0:T(128)S(1)}, s32[10]{0:T(128)S(1)}, u32[]{:S(2)}, u32[]{:S(2)}) collective-permute-start(s32[10]{0:T(128)S(1)} %pad_add_fusion.1), channel_id=1, source_target_pairs={{0,1},{1,2},{2,3},{3,4},{4,5},{5,6},{6,7},{7,8},{8,9},{9,10},{10,1... | collective-permute-start | bytes 128 | tf_op jit(solution)/shard_map/ppermute | solution.py:402
  12.9 1.1 %collective-permute-done = s32[10]{0:T(128)S(1)} collective-permute-done((s32[10]{0:T(128)S(1)}, s32[10]{0:T(128)S(1)}, u32[]{:S(2)}, u32[]{:S(2)}) %collective-permute-start) | collective-permute-done | bytes 72 | tf_op jit(solution)/shard_map/ppermute | solution.py:402
  14.0 0.0 copy-start.2
  14.0 1.0 %copy-done.2 = f32[2,256,256]{2,1,0:T(8,128)S(1)} copy-done((f32[2,256,256]{2,1,0:T(8,128)S(1)}, f32[2,256,256]{2,1,0:T(8,128)}, u32[]{:S(2)}) %copy-start.2) | copy-done | bytes 524312
  15.0 0.0 copy-start.5
  15.0 1.2 %copy-done.5 = f32[1,1,4,256,256]{4,3,2,1,0:T(8,128)S(1)} copy-done((f32[1,1,4,256,256]{4,3,2,1,0:T(8,128)S(1)}, f32[1,1,4,256,256]{4,3,2,1,0:T(8,128)}, u32[]{:S(2)}) %copy-start.5) | copy-done | bytes 1048600
  16.3 0.0 copy-start.7
  16.3 0.9 copy-done.7
  17.2 0.0 copy-start.3
  17.2 0.0 copy-start.6
  17.2 2.9 %prepare.1 = (f32[4,256,256]{2,1,0:T(8,128)S(1)}, f32[256,512]{1,0:T(8,128)S(1)}) custom-call(s32[2,10]{1,0:T(2,128)S(1)} %pad_add_fusion.facts, f32[4,256,256]{2,1,0:T(8,128)S(1)} %bitcast.13, f32[2,256,256]{2,1,0:T(8,128)S(1)} %copy-done.2, bf16[256,256]{1,0:T(8,128)(2,1)S(1)} %copy-done.7), custom_call_target="tpu_custom_call" | custom-call | flops 800000000 | bytes 3200000 | tf_op jit(solution)/shard_map/prepare/pallas_call | solution.py:405
  20.0 0.0 copy-start.1
  20.0 0.8 copy-done.1
  20.8 0.0 collective-permute-done.1.rim_ref
  20.8 0.0 copy-start.8
  20.8 1.0 %copy-done.8 = f32[2,256,512]{2,1,0:T(8,128)} copy-done((f32[2,256,512]{2,1,0:T(8,128)}, f32[2,256,512]{2,1,0:T(8,128)S(1)}, u32[]{:S(2)}) %copy-start.8) | copy-done | bytes 1048600
  21.8 0.0 copy-done
  21.8 0.0 copy-done.3
  21.8 0.0 copy-done.6
  21.8 7.3 %frames.1 = (f32[256,256]{1,0:T(8,128)S(1)}, f32[256,256]{1,0:T(8,128)S(1)}, f32[2,512,512]{2,1,0:T(8,128)S(1)}) custom-call(s32[2,10]{1,0:T(2,128)S(1)} %pad_add_fusion.facts, f32[2,256,512]{2,1,0:T(8,128)S(1)} %copy-done, f32[2,256,512]{2,1,0:T(8,128)} %copy-done.8, f32[2,256,256]{2,1,0:T(8,128)S(1)} %copy-done.3, ...), custom_call_target="tpu_custom_call" | custom-call | flops 3300000000 | bytes 8000000 | tf_op jit(solution)/shard_map/frames/pallas_call | solution.py:423
  29.1 1.9 %collective-permute-start.3 = (f32[256,256]{1,0:T(8,128)S(1)}, f32[256,256]{1,0:T(8,128)S(1)}, u32[]{:S(2)}, u32[]{:S(2)}) collective-permute-start(f32[256,256]{1,0:T(8,128)S(1)} %get-tuple-element.11), channel_id=1, source_target_pairs={{0,1},{1,0},{2,3},{3,2},{4,5},{5,4},{6,7},{7,6},{8,9},{9,8},{10,11... | collective-permute-start | bytes 786440 | tf_op jit(solution)/shard_map/ppermute | solution.py:449
  31.1 1.5 %collective-permute-done.3 = f32[256,256]{1,0:T(8,128)S(1)} collective-permute-done((f32[256,256]{1,0:T(8,128)S(1)}, f32[256,256]{1,0:T(8,128)S(1)}, u32[]{:S(2)}, u32[]{:S(2)}) %collective-permute-start.3) | collective-permute-done | bytes 262176 | tf_op jit(solution)/shard_map/ppermute | solution.py:449
  32.6 0.8 add_bitcast_fusion
  33.3 14.3 %all-to-all-start = ((f32[32,8,256]{2,1,0:T(8,128)}), f32[32,8,256]{2,1,0:T(8,128)S(1)}, u32[]{:S(2)}, u32[]{:S(2)}) async-start(f32[32,8,256]{2,1,0:T(8,128)} %add_bitcast_fusion), calls=%async_computation | async-start | bytes 524288 | tf_op jit(solution)/shard_map/all_to_all | solution.py:380
  47.6 1.0 %slice.7 = f32[2,256,512]{2,1,0:T(8,128)} slice(f32[2,512,512]{2,1,0:T(8,128)S(1)} %get-tuple-element.8), slice={[0:2], [256:512], [0:512]} | slice | bytes 2097152 | tf_op jit(solution)/shard_map/slice | solution.py:446
  48.6 2.1 %collective-permute-start.2 = (f32[2,256,512]{2,1,0:T(8,128)}, f32[2,256,512]{2,1,0:T(8,128)}, u32[]{:S(2)}, u32[]{:S(2)}) collective-permute-start(f32[2,256,512]{2,1,0:T(8,128)} %slice.7), channel_id=1, source_target_pairs={{0,1},{1,2},{2,3},{3,4},{4,5},{5,6},{6,7},{7,8},{8,9},{9,10},{10,1... | collective-permute-start | bytes 3145736 | tf_op jit(solution)/shard_map/ppermute | solution.py:456
  50.7 6.5 %all-to-all-done = f32[32,8,256]{2,1,0:T(8,128)S(1)} async-done(((f32[32,8,256]{2,1,0:T(8,128)}), f32[32,8,256]{2,1,0:T(8,128)S(1)}, u32[]{:S(2)}, u32[]{:S(2)}) %all-to-all-start) | async-done | bytes 262176 | tf_op jit(solution)/shard_map/all_to_all | solution.py:380
  57.3 14.2 %all_to_all.15 = f32[8,8,256]{2,1,0:T(8,128)S(1)} all-to-all(f32[8,8,256]{2,1,0:T(8,128)S(1)} %broadcast_in_dim.7), channel_id=1, replica_groups={{0,8,16,24,32,40,48,56},{1,3,5,7,65,67,69,71},{2,10,18,26,34,42,50,58},..., dimensions={0} | all-to-all | bytes 131072 | tf_op jit(solution)/shard_map/all_to_all | solution.py:380
  71.5 18.3 %all_to_all.16 = f32[32,8,256]{2,1,0:T(8,128)S(1)} all-to-all(f32[32,8,256]{2,1,0:T(8,128)S(1)} %broadcast_in_dim.8), channel_id=1, replica_groups={{0,2,4,6,64,66,68,70,128,130,132,134,192,194,196,198,256,258,260,262,32..., dimensions={0} | all-to-all | bytes 524288 | tf_op jit(solution)/shard_map/all_to_all | solution.py:380
  89.8 2.4 %collective-permute-start.4 = (f32[256,256]{1,0:T(8,128)S(1)}, f32[256,256]{1,0:T(8,128)S(1)}, u32[]{:S(2)}, u32[]{:S(2)}) collective-permute-start(f32[256,256]{1,0:T(8,128)S(1)} %bitcast.11), channel_id=1, source_target_pairs={{0,1},{1,0},{2,3},{3,2},{4,5},{5,4},{6,7},{7,6},{8,9},{9,8},{10,11... | collective-permute-start | bytes 786440 | tf_op jit(solution)/shard_map/ppermute | solution.py:454
  92.2 0.0 collective-permute-done.2
  92.2 0.0 copy-start.4
  92.2 2.8 %multiply_subtract_fusion = f32[2,256,512]{2,1,0:T(8,128)} fusion(f32[2,256,512]{2,1,0:T(8,128)S(1)} %copy-done, f32[2,256,512]{2,1,0:T(8,128)} %collective-permute-done.2, f32[2,512,512]{2,1,0:T(8,128)S(1)} %get-tuple-element.8, f32[256,512]{1,0:T(8,128)} %copy-done.1), kind=kLoop, calls=%fused_computation | loop fusion | flops 786432 | bytes 4718592 | tf_op jit(solution)/shard_map/sub | solution.py:457
  95.0 0.0 collective-permute-done.4.other_ref
  95.1 0.0 copy-done.4
  95.1 1.6 %update.1 = f32[2,256,256]{2,1,0:T(8,128)} custom-call(s32[2,10]{1,0:T(2,128)S(1)} %pad_add_fusion.facts, f32[256,256]{1,0:T(8,128)S(1)} %bitcast.12, f32[256,256]{1,0:T(8,128)S(1)} %collective-permute-done.4.other_ref, f32[2,256,256]{2,1,0:T(8,128)S(1)} %copy-done.4), custom_call_target="tpu_custom_call" | custom-call | flops 1000000 | bytes 1600000 | tf_op jit(solution)/shard_map/update/pallas_call | solution.py:461
  (5 shorter events, 0.1 us)
Async XLA Ops:
  0.6 21.2 %copy-start = (f32[2,256,512]{2,1,0:T(8,128)S(1)}, f32[2,256,512]{2,1,0:T(8,128)}, u32[]{:S(2)}) copy-start(f32[2,256,512]{2,1,0:T(8,128)} %field_ref.1) | copy-start | bytes 3145732
  0.6 20.2 %collective-permute-start.1 = (f32[2,256,512]{2,1,0:T(8,128)}, f32[2,256,512]{2,1,0:T(8,128)S(1)}, u32[]{:S(2)}, u32[]{:S(2)}) collective-permute-start(f32[2,256,512]{2,1,0:T(8,128)} %field_ref.1), channel_id=1, source_target_pairs={{1,0},{2,1},{3,2},{4,3},{5,4},{6,5},{7,6},{8,7},{9,8},{10,9},{11,1... | collective-permute-start | bytes 3145736 | tf_op jit(solution)/shard_map/ppermute | solution.py:398
  11.0 3.0 %collective-permute-start = (s32[10]{0:T(128)S(1)}, s32[10]{0:T(128)S(1)}, u32[]{:S(2)}, u32[]{:S(2)}) collective-permute-start(s32[10]{0:T(128)S(1)} %pad_add_fusion.1), channel_id=1, source_target_pairs={{0,1},{1,2},{2,3},{3,4},{4,5},{5,6},{6,7},{7,8},{8,9},{9,10},{10,1... | collective-permute-start | bytes 128 | tf_op jit(solution)/shard_map/ppermute | solution.py:402
  14.0 1.0 %copy-start.2 = (f32[2,256,256]{2,1,0:T(8,128)S(1)}, f32[2,256,256]{2,1,0:T(8,128)}, u32[]{:S(2)}) copy-start(f32[2,256,256]{2,1,0:T(8,128)} %probe_ref.3) | copy-start | bytes 1572868
  15.0 1.2 %copy-start.5 = (f32[1,1,4,256,256]{4,3,2,1,0:T(8,128)S(1)}, f32[1,1,4,256,256]{4,3,2,1,0:T(8,128)}, u32[]{:S(2)}) copy-start(f32[1,1,4,256,256]{4,3,2,1,0:T(8,128)} %param.10) | copy-start | bytes 3145732
  16.3 0.9 copy-start.7
  17.2 4.7 %copy-start.3 = (f32[2,256,256]{2,1,0:T(8,128)S(1)}, f32[2,256,256]{2,1,0:T(8,128)}, u32[]{:S(2)}) copy-start(f32[2,256,256]{2,1,0:T(8,128)} %probe_ref.3) | copy-start | bytes 1572868
  17.2 4.7 %copy-start.6 = (bf16[4,2,256,256]{3,2,1,0:T(8,128)(2,1)S(1)}, bf16[4,2,256,256]{3,2,1,0:T(8,128)(2,1)}, u32[]{:S(2)}) copy-start(bf16[4,2,256,256]{3,2,1,0:T(8,128)(2,1)} %constant.24.clone.tables) | copy-start | bytes 3145732
  20.0 0.8 copy-start.1
  20.8 1.0 %copy-start.8 = (f32[2,256,512]{2,1,0:T(8,128)}, f32[2,256,512]{2,1,0:T(8,128)S(1)}, u32[]{:S(2)}) copy-start(f32[2,256,512]{2,1,0:T(8,128)S(1)} %collective-permute-done.1.rim_ref) | copy-start | bytes 3145732
  29.1 3.4 %collective-permute-start.3 = (f32[256,256]{1,0:T(8,128)S(1)}, f32[256,256]{1,0:T(8,128)S(1)}, u32[]{:S(2)}, u32[]{:S(2)}) collective-permute-start(f32[256,256]{1,0:T(8,128)S(1)} %get-tuple-element.11), channel_id=1, source_target_pairs={{0,1},{1,0},{2,3},{3,2},{4,5},{5,4},{6,7},{7,6},{8,9},{9,8},{10,11... | collective-permute-start | bytes 786440 | tf_op jit(solution)/shard_map/ppermute | solution.py:449
  33.3 23.9 %all-to-all-start = ((f32[32,8,256]{2,1,0:T(8,128)}), f32[32,8,256]{2,1,0:T(8,128)S(1)}, u32[]{:S(2)}, u32[]{:S(2)}) async-start(f32[32,8,256]{2,1,0:T(8,128)} %add_bitcast_fusion), calls=%async_computation | async-start | bytes 524288 | tf_op jit(solution)/shard_map/all_to_all | solution.py:380
  48.6 43.6 %collective-permute-start.2 = (f32[2,256,512]{2,1,0:T(8,128)}, f32[2,256,512]{2,1,0:T(8,128)}, u32[]{:S(2)}, u32[]{:S(2)}) collective-permute-start(f32[2,256,512]{2,1,0:T(8,128)} %slice.7), channel_id=1, source_target_pairs={{0,1},{1,2},{2,3},{3,4},{4,5},{5,6},{6,7},{7,8},{8,9},{9,10},{10,1... | collective-permute-start | bytes 3145736 | tf_op jit(solution)/shard_map/ppermute | solution.py:456
  89.8 5.2 %collective-permute-start.4 = (f32[256,256]{1,0:T(8,128)S(1)}, f32[256,256]{1,0:T(8,128)S(1)}, u32[]{:S(2)}, u32[]{:S(2)}) collective-permute-start(f32[256,256]{1,0:T(8,128)S(1)} %bitcast.11), channel_id=1, source_target_pairs={{0,1},{1,0},{2,3},{3,2},{4,5},{5,4},{6,7},{7,6},{8,9},{9,8},{10,11... | collective-permute-start | bytes 786440 | tf_op jit(solution)/shard_map/ppermute | solution.py:454
  92.2 2.8 %copy-start.4 = (f32[2,256,256]{2,1,0:T(8,128)S(1)}, f32[2,256,256]{2,1,0:T(8,128)}, u32[]{:S(2)}) copy-start(f32[2,256,256]{2,1,0:T(8,128)} %probe_ref.3) | copy-start | bytes 1572868

commit v4 on v3

--- a/solution.py
+++ b/solution.py
@@ -176,31 +176,17 @@
 
 
 def frames_kernel(
-    facts, field_ref, rim_ref, probe, amp, tables,
+    facts, ext, probe, amp, tables,
     mine_ref, other_ref, total,
-    ext, win, xh, xl, fa, fb, grad, sems,
+    win, xh, xl, fa, fb, grad,
 ):
-    band = field_ref.shape[1]
     size = probe.shape[1]
     half = size // 2
     steps = half // BLOCK
     count = facts[0, COUNT]
 
-    loads = []
-    for c in (0, 1):
-        for j in (0, 1):
-            rows = slice(j * half, (j + 1) * half)
-            under = slice(band + j * half, band + (j + 1) * half)
-            loads.append(
-                pltpu.make_async_copy(rim_ref.at[c, rows], ext.at[c, under], sems.at[2 * c + j])
-            )
-    for load in loads:
-        load.start()
-    ext[:, :band] = field_ref[...]
     total[...] = jnp.zeros_like(total)
     grad[...] = jnp.zeros_like(grad)
-    for load in loads:
-        load.wait()
 
     def keep(b, which, place, value):
         high, low = split2(value)
@@ -396,7 +382,6 @@
     peers = lax.axis_size("dev")
 
     rim = lax.ppermute(object_field, "dev", [(i, i - 1) for i in range(1, peers)])
-    rim = pltpu.with_memory_space_constraint(rim, pltpu.HBM)
     core = (lax.axis_index("dev") % 2).astype(jnp.int32)
     facts = jnp.concatenate([row_offset[0, 0], col_offset[0, 0], frame_count[0], core[None]])
     facts_before = lax.ppermute(facts, "dev", [(i, i + 1) for i in range(peers - 1)])
@@ -420,6 +405,9 @@
     )(facts, amplitudes[0, 0], probe, jnp.asarray(order_table(size)))
 
     bf16 = jnp.bfloat16
+    ext = jnp.pad(object_field, ((0, 0), (0, size), (0, 0)))
+    ext, rim = lax.optimization_barrier((ext, rim))
+    ext = lax.dynamic_update_slice(ext, rim[:, :size], (0, band, 0))
     mine, other, total = pl.pallas_call(
         frames_kernel,
         out_shape=(
@@ -427,36 +415,36 @@
             jax.ShapeDtypeStruct((size, size), f32),
             jax.ShapeDtypeStruct((2, band + size, width), f32),
         ),
-        in_specs=[smem, vmem, hbm, vmem, vmem, vmem],
+        in_specs=[smem, vmem, vmem, vmem, vmem],
         out_specs=(vmem, vmem, vmem),
         scratch_shapes=[
-            pltpu.VMEM((2, band + size, width), f32),
             pltpu.VMEM((2, 2, size, size), f32),
             pltpu.VMEM((2, 2, size, size), bf16),
             pltpu.VMEM((2, 2, size, size), bf16),
             pltpu.VMEM((2, size, size), f32),
             pltpu.VMEM((2, size, size), f32),
             pltpu.VMEM((2, size, size), f32),
-            pltpu.SemaphoreType.DMA((4,)),
         ],
         compiler_params=pltpu.CompilerParams(vmem_limit_bytes=24 * 1024 * 1024),
         cost_estimate=pl.CostEstimate(flops=3_300_000_000, bytes_accessed=8_000_000, transcendentals=262144),
         name="frames",
-    )(facts, object_field, rim, probe, ordered, jnp.asarray(frame_tables(size)))
-    own, over = total[:, :band], total[:, band:]
-
+    )(facts, ext, probe, ordered, jnp.asarray(frame_tables(size)))
+    over = total[:, band:]
+    steps = [(i, i + 1) for i in range(peers - 1)]
     swap = [(i, i ^ 1) for i in range(peers)]
     plane = mine + lax.ppermute(other, "dev", swap)
+    incoming = lax.ppermute(over, "dev", steps)
     parts = exchanged(plane.reshape(32, size // 32, size), WIDE)
     share = jnp.sum(parts, axis=0)
     share = jnp.sum(copies(share, LINE), axis=0)
-    plane = copies(share, WIDE).reshape(size, size)
-    plane_other = lax.ppermute(plane, "dev", swap)
-
-    incoming = lax.ppermute(over, "dev", [(i, i + 1) for i in range(peers - 1)])
+    share, total = lax.optimization_barrier((share, total))
+    own = total[:, :band]
     new_field = object_field - jnp.concatenate(
         [own[:, :size] + incoming, own[:, size:]], axis=1
     ) * scale[None]
+    plane = copies(share, WIDE).reshape(size, size)
+    plane, new_field = lax.optimization_barrier((plane, new_field))
+    plane_other = lax.ppermute(plane, "dev", swap)
 
     new_probe = pl.pallas_call(
         update_kernel,

time: 97.2 us -> 97.9 us (level)
  blocking collectives: 32.5 us -> 39.6 us
  Pallas kernels: 11.8 us -> 7.26 us
  local copies, waits for them, and re-layouts: 6.01 us -> 3.36 us
    all_to_all x1, starting transfers between devices: 14.3 us -> 4.88 us  [exchanged(): lax.all_to_all(parts, AXES, 0, 0, tiled=True, axis_index_groups=groups_al...]
    all_to_all x2, blocking collectives: 32.5 us -> 39.6 us  [exchanged(): lax.all_to_all(parts, AXES, 0, 0, tiled=True, axis_index_groups=groups_al...]
    ppermute x1, starting transfers between devices: 2.37 us -> 7.42 us  [on_device(): plane_other = lax.ppermute(plane, 'dev', swap)]
    unnamed x18 -> x8, local copies, waits for them, and re-layouts: 4.95 us -> 0.02 us
    pallas_call x1, Pallas kernels: 7.31 us -> 3.38 us  [on_device(): pl.pallas_call(frames_kernel, out_shape=(jax.ShapeDtypeStruct((size, size...]
    ppermute x1, starting transfers between devices: 2.11 us -> 5.7 us  [on_device(): incoming = lax.ppermute(over, 'dev', steps)]
    ppermute x1, waiting for transfers between devices: 0.01 us -> 2.12 us  [on_device(): lax.ppermute(object_field, 'dev', [(i, i - 1) for i in range(1, peers)])]
    ppermute x1, waiting for transfers between devices: 1.5 us -> 0.01 us  [on_device(): plane = mine + lax.ppermute(other, 'dev', swap)]
  transfers between devices with their start and end apart: 6 -> 6, of which waited for: 3 -> 3; matrix products, arithmetic and copies ran while one was open for 5% -> 7% of each run, Pallas kernels for 3% -> 2%
where the time goes in v4:
time: 97.9 us; the launch traced here: 97.5 us
  blocking collectives  39.6 us (40%)
  starting transfers between devices  32 us (33%)
  waiting for transfers between devices  9.97 us (10%)
  Pallas kernels  7.26 us (7%)
  other arithmetic  3.79 us (4%)
  local copies, waits for them, and re-layouts  3.36 us (3%)
  between operations  1.48 us (2%)
    all_to_all x2, blocking collectives, exchanged(): lax.all_to_all(parts, AXES, 0, 0, tiled=True, axis_index_groups=groups_al...  39.6 us
    ppermute x1, starting transfers between devices, on_device(): lax.ppermute(object_field, 'dev', [(i, i - 1) for i in range(1, peers)])  8.92 us
    ppermute x1, starting transfers between devices, on_device(): plane_other = lax.ppermute(plane, 'dev', swap)  7.42 us
    all_to_all x1, waiting for transfers between devices, exchanged(): lax.all_to_all(parts, AXES, 0, 0, tiled=True, axis_index_groups=groups_al...  6.7 us
    ppermute x1, starting transfers between devices, on_device(): incoming = lax.ppermute(over, 'dev', steps)  5.7 us
    all_to_all x1, starting transfers between devices, exchanged(): lax.all_to_all(parts, AXES, 0, 0, tiled=True, axis_index_groups=groups_al...  4.88 us
    pallas_call x1, Pallas kernels, on_device(): pl.pallas_call(frames_kernel, out_shape=(jax.ShapeDtypeStruct((size, size...  3.38 us
    ppermute x1, starting transfers between devices, on_device(): plane = mine + lax.ppermute(other, 'dev', swap)  3.18 us
  transfers between devices with their start and end apart: 6, of which 3 were waited for; matrix products, arithmetic and copies ran while one was open for 7% of the time, Pallas kernels for 2%

profile of v4, /device:TPU:1, one launch (start us, length us, event | category | flops | bytes accessed | tf_op | source)
XLA Modules:
  0.0 97.5 jit_solution(9057665443869960471)
XLA Ops:
  0.6 0.0 copy-start.3
  0.6 0.0 copy-start
  0.7 0.0 copy-start.1
  0.7 8.9 %collective-permute-start.1 = (f32[2,256,512]{2,1,0:T(8,128)}, f32[2,256,512]{2,1,0:T(8,128)S(1)}, u32[]{:S(2)}, u32[]{:S(2)}) collective-permute-start(f32[2,256,512]{2,1,0:T(8,128)} %param.8), channel_id=1, source_target_pairs={{1,0},{2,1},{3,2},{4,3},{5,4},{6,5},{7,6},{8,7},{9,8},{10,9},{11,1... | collective-permute-start | bytes 3145736 | tf_op jit(solution)/shard_map/ppermute | solution.py:384
  10.2 0.8 pad_add_fusion.1
  11.0 1.9 %collective-permute-start = (s32[10]{0:T(128)S(1)}, s32[10]{0:T(128)S(1)}, u32[]{:S(2)}, u32[]{:S(2)}) collective-permute-start(s32[10]{0:T(128)S(1)} %pad_add_fusion.1), channel_id=1, source_target_pairs={{0,1},{1,2},{2,3},{3,4},{4,5},{5,6},{6,7},{7,8},{8,9},{9,10},{10,1... | collective-permute-start | bytes 128 | tf_op jit(solution)/shard_map/ppermute | solution.py:387
  12.9 1.5 %pad.4 = f32[2,512,512]{2,1,0:T(8,128)S(1)} pad(f32[2,256,512]{2,1,0:T(8,128)} %param.8, f32[]{:T(128)} %constant.25.clone.1), padding=0_0x0_256x0_0 | pad | bytes 3145732 | tf_op jit(solution)/shard_map/jit(_pad)/pad | solution.py:408
  14.4 0.0 collective-permute-done
  14.4 0.0 copy-done.3
  14.5 0.0 copy-done
  14.5 0.0 copy-done.1
  14.5 0.0 copy-start.2
  14.5 2.3 %prepare.1 = (f32[4,256,256]{2,1,0:T(8,128)S(1)}, f32[256,512]{1,0:T(8,128)S(1)}) custom-call(s32[2,10]{1,0:T(2,128)S(1)} %pad_add_fusion.facts, f32[4,256,256]{2,1,0:T(8,128)S(1)} %bitcast.13, f32[2,256,256]{2,1,0:T(8,128)S(1)} %copy-done, bf16[256,256]{1,0:T(8,128)(2,1)S(1)} %copy-done.3), custom_call_target="tpu_custom_call" | custom-call | flops 800000000 | bytes 3200000 | tf_op jit(solution)/shard_map/prepare/pallas_call | solution.py:390
  16.7 2.1 %collective-permute-done.1 = f32[2,256,512]{2,1,0:T(8,128)S(1)} collective-permute-done((f32[2,256,512]{2,1,0:T(8,128)}, f32[2,256,512]{2,1,0:T(8,128)S(1)}, u32[]{:S(2)}, u32[]{:S(2)}) %collective-permute-start.1) | collective-permute-done | bytes 1048608 | tf_op jit(solution)/shard_map/ppermute | solution.py:384
  18.9 0.1 constant_dynamic-update-slice_fusion.ext
  19.0 0.0 copy-done.2
  19.0 3.4 %frames.1 = (f32[256,256]{1,0:T(8,128)S(1)}, f32[256,256]{1,0:T(8,128)S(1)}, f32[2,512,512]{2,1,0:T(8,128)S(1)}) custom-call(s32[2,10]{1,0:T(2,128)S(1)} %pad_add_fusion.facts, f32[2,512,512]{2,1,0:T(8,128)S(1)} %constant_dynamic-update-slice_fusion.ext, f32[2,256,256]{2,1,0:T(8,128)S(1)} %copy-done, f32[4,256,256]{2,1,0:T(8,128)S(1)} %get-tuple-element.15.amp, ...), custom_call_target="tpu_custom_call" | custom-call | flops 3300000000 | bytes 8000000 | tf_op jit(solution)/shard_map/frames/pallas_call | solution.py:411
  22.3 3.2 %collective-permute-start.2 = (f32[256,256]{1,0:T(8,128)S(1)}, f32[256,256]{1,0:T(8,128)S(1)}, u32[]{:S(2)}, u32[]{:S(2)}) collective-permute-start(f32[256,256]{1,0:T(8,128)S(1)} %get-tuple-element.17), channel_id=1, source_target_pairs={{0,1},{1,0},{2,3},{3,2},{4,5},{5,4},{6,7},{7,6},{8,9},{9,8},{10,11... | collective-permute-start | bytes 786440 | tf_op jit(solution)/shard_map/ppermute | solution.py:435
  25.5 1.0 %slice.7 = f32[2,256,512]{2,1,0:T(8,128)} slice(f32[2,512,512]{2,1,0:T(8,128)S(1)} %get-tuple-element.20), slice={[0:2], [256:512], [0:512]} | slice | bytes 2097152 | tf_op jit(solution)/shard_map/slice | solution.py:432
  26.6 5.7 %collective-permute-start.3 = (f32[2,256,512]{2,1,0:T(8,128)}, f32[2,256,512]{2,1,0:T(8,128)}, u32[]{:S(2)}, u32[]{:S(2)}) collective-permute-start(f32[2,256,512]{2,1,0:T(8,128)} %slice.7), channel_id=1, source_target_pairs={{0,1},{1,2},{2,3},{3,4},{4,5},{5,6},{6,7},{7,8},{8,9},{9,10},{10,1... | collective-permute-start | bytes 3145736 | tf_op jit(solution)/shard_map/ppermute | solution.py:436
  32.3 0.0 collective-permute-done.2
  32.3 20.0 %all_to_all.15 = f32[32,8,256]{2,1,0:T(8,128)S(1)} all-to-all(f32[32,8,256]{2,1,0:T(8,128)S(1)} %add_bitcast_fusion), channel_id=1, replica_groups={{0,2,4,6,64,66,68,70,128,130,132,134,192,194,196,198,256,258,260,262,32..., dimensions={0} | all-to-all | bytes 524288 | tf_op jit(solution)/shard_map/all_to_all | solution.py:366
  52.4 19.6 %all_to_all.16 = f32[8,8,256]{2,1,0:T(8,128)S(1)} all-to-all(f32[8,8,256]{2,1,0:T(8,128)S(1)} %broadcast_in_dim.7), channel_id=1, replica_groups={{0,8,16,24,32,40,48,56},{1,3,5,7,65,67,69,71},{2,10,18,26,34,42,50,58},..., dimensions={0} | all-to-all | bytes 131072 | tf_op jit(solution)/shard_map/all_to_all | solution.py:366
  72.0 0.7 broadcast_in_dim.8
  72.8 4.9 %all-to-all-start.2 = ((f32[32,8,256]{2,1,0:T(8,128)}), f32[32,8,256]{2,1,0:T(8,128)S(1)}, u32[]{:S(2)}, u32[]{:S(2)}) async-start(f32[32,8,256]{2,1,0:T(8,128)} %broadcast_in_dim.8), calls=%async_computation.2 | async-start | bytes 524288 | tf_op jit(solution)/shard_map/all_to_all | solution.py:366
  77.6 0.0 collective-permute-done.3
  77.7 2.9 %multiply_subtract_fusion = f32[2,256,512]{2,1,0:T(8,128)} fusion(f32[2,256,512]{2,1,0:T(8,128)} %param.8, f32[2,256,512]{2,1,0:T(8,128)} %collective-permute-done.3, f32[2,512,512]{2,1,0:T(8,128)S(1)} %get-tuple-element.20, f32[256,512]{1,0:T(8,128)S(1)} %get-tuple-element.21), kind=kLoop, calls=%fused_computation | loop fusion | flops 786432 | bytes 4718592 | tf_op jit(solution)/shard_map/sub | solution.py:442
  80.6 6.7 %all-to-all-done.2 = f32[32,8,256]{2,1,0:T(8,128)S(1)} async-done(((f32[32,8,256]{2,1,0:T(8,128)}), f32[32,8,256]{2,1,0:T(8,128)S(1)}, u32[]{:S(2)}, u32[]{:S(2)}) %all-to-all-start.2) | async-done | bytes 262176 | tf_op jit(solution)/shard_map/all_to_all | solution.py:366
  87.3 7.4 %collective-permute-start.4 = (f32[256,256]{1,0:T(8,128)S(1)}, f32[256,256]{1,0:T(8,128)S(1)}, u32[]{:S(2)}, u32[]{:S(2)}) collective-permute-start(f32[256,256]{1,0:T(8,128)S(1)} %bitcast.11), channel_id=1, source_target_pairs={{0,1},{1,0},{2,3},{3,2},{4,5},{5,4},{6,7},{7,6},{8,9},{9,8},{10,11... | collective-permute-start | bytes 786440 | tf_op jit(solution)/shard_map/ppermute | solution.py:447
  94.7 1.1 %collective-permute-done.4.other_ref = f32[256,256]{1,0:T(8,128)S(1)} collective-permute-done((f32[256,256]{1,0:T(8,128)S(1)}, f32[256,256]{1,0:T(8,128)S(1)}, u32[]{:S(2)}, u32[]{:S(2)}) %collective-permute-start.4) | collective-permute-done | bytes 262176 | tf_op jit(solution)/shard_map/ppermute | solution.py:447
  95.9 1.6 %update.1 = f32[2,256,256]{2,1,0:T(8,128)} custom-call(s32[2,10]{1,0:T(2,128)S(1)} %pad_add_fusion.facts, f32[256,256]{1,0:T(8,128)S(1)} %bitcast.12, f32[256,256]{1,0:T(8,128)S(1)} %collective-permute-done.4.other_ref, f32[2,256,256]{2,1,0:T(8,128)S(1)} %copy-done), custom_call_target="tpu_custom_call" | custom-call | flops 1000000 | bytes 1600000 | tf_op jit(solution)/shard_map/update/pallas_call | solution.py:449
  (5 shorter events, 0.1 us)
Async XLA Ops:
  0.6 13.8 %copy-start.3 = (bf16[256,256]{1,0:T(8,128)(2,1)S(1)}, bf16[256,256]{1,0:T(8,128)(2,1)}, u32[]{:S(2)}) copy-start(bf16[256,256]{1,0:T(8,128)(2,1)} %constant.27.clone.order_ref) | copy-start | bytes 393220
  0.6 13.8 %copy-start = (f32[2,256,256]{2,1,0:T(8,128)S(1)}, f32[2,256,256]{2,1,0:T(8,128)}, u32[]{:S(2)}) copy-start(f32[2,256,256]{2,1,0:T(8,128)} %probe_ref.3) | copy-start | bytes 1572868
  0.7 13.8 %copy-start.1 = (f32[1,1,4,256,256]{4,3,2,1,0:T(8,128)S(1)}, f32[1,1,4,256,256]{4,3,2,1,0:T(8,128)}, u32[]{:S(2)}) copy-start(f32[1,1,4,256,256]{4,3,2,1,0:T(8,128)} %param.10) | copy-start | bytes 3145732
  0.7 18.2 %collective-permute-start.1 = (f32[2,256,512]{2,1,0:T(8,128)}, f32[2,256,512]{2,1,0:T(8,128)S(1)}, u32[]{:S(2)}, u32[]{:S(2)}) collective-permute-start(f32[2,256,512]{2,1,0:T(8,128)} %param.8), channel_id=1, source_target_pairs={{1,0},{2,1},{3,2},{4,3},{5,4},{6,5},{7,6},{8,7},{9,8},{10,9},{11,1... | collective-permute-start | bytes 3145736 | tf_op jit(solution)/shard_map/ppermute | solution.py:384
  11.0 3.4 %collective-permute-start = (s32[10]{0:T(128)S(1)}, s32[10]{0:T(128)S(1)}, u32[]{:S(2)}, u32[]{:S(2)}) collective-permute-start(s32[10]{0:T(128)S(1)} %pad_add_fusion.1), channel_id=1, source_target_pairs={{0,1},{1,2},{2,3},{3,4},{4,5},{5,6},{6,7},{7,8},{8,9},{9,10},{10,1... | collective-permute-start | bytes 128 | tf_op jit(solution)/shard_map/ppermute | solution.py:387
  14.5 4.5 %copy-start.2 = (bf16[4,2,256,256]{3,2,1,0:T(8,128)(2,1)S(1)}, bf16[4,2,256,256]{3,2,1,0:T(8,128)(2,1)}, u32[]{:S(2)}) copy-start(bf16[4,2,256,256]{3,2,1,0:T(8,128)(2,1)} %constant.28.clone.tables) | copy-start | bytes 3145732
  22.3 9.9 %collective-permute-start.2 = (f32[256,256]{1,0:T(8,128)S(1)}, f32[256,256]{1,0:T(8,128)S(1)}, u32[]{:S(2)}, u32[]{:S(2)}) collective-permute-start(f32[256,256]{1,0:T(8,128)S(1)} %get-tuple-element.17), channel_id=1, source_target_pairs={{0,1},{1,0},{2,3},{3,2},{4,5},{5,4},{6,7},{7,6},{8,9},{9,8},{10,11... | collective-permute-start | bytes 786440 | tf_op jit(solution)/shard_map/ppermute | solution.py:435
  26.6 51.1 %collective-permute-start.3 = (f32[2,256,512]{2,1,0:T(8,128)}, f32[2,256,512]{2,1,0:T(8,128)}, u32[]{:S(2)}, u32[]{:S(2)}) collective-permute-start(f32[2,256,512]{2,1,0:T(8,128)} %slice.7), channel_id=1, source_target_pairs={{0,1},{1,2},{2,3},{3,4},{4,5},{5,6},{6,7},{7,8},{8,9},{9,10},{10,1... | collective-permute-start | bytes 3145736 | tf_op jit(solution)/shard_map/ppermute | solution.py:436
  72.8 14.5 %all-to-all-start.2 = ((f32[32,8,256]{2,1,0:T(8,128)}), f32[32,8,256]{2,1,0:T(8,128)S(1)}, u32[]{:S(2)}, u32[]{:S(2)}) async-start(f32[32,8,256]{2,1,0:T(8,128)} %broadcast_in_dim.8), calls=%async_computation.2 | async-start | bytes 524288 | tf_op jit(solution)/shard_map/all_to_all | solution.py:366
  87.3 8.6 %collective-permute-start.4 = (f32[256,256]{1,0:T(8,128)S(1)}, f32[256,256]{1,0:T(8,128)S(1)}, u32[]{:S(2)}, u32[]{:S(2)}) collective-permute-start(f32[256,256]{1,0:T(8,128)S(1)} %bitcast.11), channel_id=1, source_target_pairs={{0,1},{1,0},{2,3},{3,2},{4,5},{5,4},{6,7},{7,6},{8,9},{9,8},{10,11... | collective-permute-start | bytes 786440 | tf_op jit(solution)/shard_map/ppermute | solution.py:447

commit v5 on v4

--- a/solution.py
+++ b/solution.py
@@ -437,14 +437,14 @@
     parts = exchanged(plane.reshape(32, size // 32, size), WIDE)
     share = jnp.sum(parts, axis=0)
     share = jnp.sum(copies(share, LINE), axis=0)
-    share, total = lax.optimization_barrier((share, total))
+    share, incoming = lax.optimization_barrier((share, incoming))
+    plane = copies(share, WIDE).reshape(size, size)
+    plane, total = lax.optimization_barrier((plane, total))
+    plane_other = lax.ppermute(plane, "dev", swap)
     own = total[:, :band]
     new_field = object_field - jnp.concatenate(
         [own[:, :size] + incoming, own[:, size:]], axis=1
     ) * scale[None]
-    plane = copies(share, WIDE).reshape(size, size)
-    plane, new_field = lax.optimization_barrier((plane, new_field))
-    plane_other = lax.ppermute(plane, "dev", swap)
 
     new_probe = pl.pallas_call(
         update_kernel,

time: 97.9 us -> 100 us (1.021)
  blocking collectives: 39.6 us -> 53.7 us
  waiting for transfers between devices: 9.97 us -> 3.01 us
  starting transfers between devices: 32 us -> 27.4 us
    all_to_all x2 -> x3, blocking collectives: 39.6 us -> 53.7 us  [exchanged(): lax.all_to_all(parts, AXES, 0, 0, tiled=True, axis_index_groups=groups_al...]
    all_to_all x1 -> x0, waiting for transfers between devices: 6.7 us -> none  [exchanged(): lax.all_to_all(parts, AXES, 0, 0, tiled=True, axis_index_groups=groups_al...]
    all_to_all x1 -> x0, starting transfers between devices: 4.88 us -> none  [exchanged(): lax.all_to_all(parts, AXES, 0, 0, tiled=True, axis_index_groups=groups_al...]
    ppermute x1, starting transfers between devices: 5.7 us -> 7.1 us  [on_device(): incoming = lax.ppermute(over, 'dev', steps)]
    ppermute x1, starting transfers between devices: 3.18 us -> 1.92 us  [on_device(): plane = mine + lax.ppermute(other, 'dev', swap)]
    dynamic_update_slice x1, local copies, waits for them, and re-layouts: 0.07 us -> 1.29 us  [on_device(): ext = lax.dynamic_update_slice(ext, rim[:, :size], (0, band, 0))]
    ppermute x1, waiting for transfers between devices: 1.14 us -> 0.01 us  [on_device(): plane_other = lax.ppermute(plane, 'dev', swap)]
  transfers between devices with their start and end apart: 6 -> 5, of which waited for: 3 -> 1; matrix products, arithmetic and copies ran while one was open for 7% -> 6% of each run, Pallas kernels for 2% -> 1%
where the time goes in v5:
time: 100 us; the launch traced here: 99.8 us
  blocking collectives  53.7 us (54%)
  starting transfers between devices  27.4 us (27%)
  Pallas kernels  6.59 us (7%)
  local copies, waits for them, and re-layouts  3.88 us (4%)
  other arithmetic  3.78 us (4%)
  waiting for transfers between devices  3.01 us (3%)
  between operations  1.47 us (1%)
    all_to_all x3, blocking collectives, exchanged(): lax.all_to_all(parts, AXES, 0, 0, tiled=True, axis_index_groups=groups_al...  53.7 us
    ppermute x1, starting transfers between devices, on_device(): lax.ppermute(object_field, 'dev', [(i, i - 1) for i in range(1, peers)])  8.92 us
    ppermute x1, starting transfers between devices, on_device(): plane_other = lax.ppermute(plane, 'dev', swap)  7.58 us
    ppermute x1, starting transfers between devices, on_device(): incoming = lax.ppermute(over, 'dev', steps)  7.1 us
    pallas_call x1, Pallas kernels, on_device(): pl.pallas_call(frames_kernel, out_shape=(jax.ShapeDtypeStruct((size, size...  3.47 us
    ppermute x1, waiting for transfers between devices, on_device(): lax.ppermute(object_field, 'dev', [(i, i - 1) for i in range(1, peers)])  3 us
    sub x1, other arithmetic, on_device(): object_field - jnp.concatenate([own[:, :size] + incoming, own[:, size:]],...  2.93 us
  transfers between devices with their start and end apart: 5, of which 1 were waited for; matrix products, arithmetic and copies ran while one was open for 6% of the time, Pallas kernels for 1%

profile of v5, /device:TPU:1, one launch (start us, length us, event | category | flops | bytes accessed | tf_op | source)
XLA Modules:
  0.0 99.8 jit_solution(18060201245369288015)
XLA Ops:
  0.6 0.0 copy-start.3
  0.6 0.0 copy-start
  0.7 0.0 copy-start.1
  0.7 8.9 %collective-permute-start.1 = (f32[2,256,512]{2,1,0:T(8,128)}, f32[2,256,512]{2,1,0:T(8,128)}, u32[]{:S(2)}, u32[]{:S(2)}) collective-permute-start(f32[2,256,512]{2,1,0:T(8,128)} %param.8), channel_id=1, source_target_pairs={{1,0},{2,1},{3,2},{4,3},{5,4},{6,5},{7,6},{8,7},{9,8},{10,9},{11,1... | collective-permute-start | bytes 3145736 | tf_op jit(solution)/shard_map/ppermute | solution.py:384
  10.2 0.8 pad_add_fusion.1
  11.0 1.9 %collective-permute-start = (s32[10]{0:T(128)S(1)}, s32[10]{0:T(128)S(1)}, u32[]{:S(2)}, u32[]{:S(2)}) collective-permute-start(s32[10]{0:T(128)S(1)} %pad_add_fusion.1), channel_id=1, source_target_pairs={{0,1},{1,2},{2,3},{3,4},{4,5},{5,6},{6,7},{7,8},{8,9},{9,10},{10,1... | collective-permute-start | bytes 128 | tf_op jit(solution)/shard_map/ppermute | solution.py:387
  12.9 1.5 %pad.4 = f32[2,512,512]{2,1,0:T(8,128)S(1)} pad(f32[2,256,512]{2,1,0:T(8,128)} %param.8, f32[]{:T(128)} %constant.25.clone.1), padding=0_0x0_256x0_0 | pad | bytes 3145732 | tf_op jit(solution)/shard_map/jit(_pad)/pad | solution.py:408
  14.4 0.0 collective-permute-done
  14.4 0.0 copy-done.3
  14.5 0.0 copy-done
  14.5 0.0 copy-done.1
  14.5 0.0 copy-start.2
  14.5 1.5 %prepare.1 = (f32[4,256,256]{2,1,0:T(8,128)S(1)}, f32[256,512]{1,0:T(8,128)S(1)}) custom-call(s32[2,10]{1,0:T(2,128)S(1)} %pad_add_fusion.facts, f32[4,256,256]{2,1,0:T(8,128)S(1)} %bitcast.13, f32[2,256,256]{2,1,0:T(8,128)S(1)} %copy-done, bf16[256,256]{1,0:T(8,128)(2,1)S(1)} %copy-done.3), custom_call_target="tpu_custom_call" | custom-call | flops 800000000 | bytes 3200000 | tf_op jit(solution)/shard_map/prepare/pallas_call | solution.py:390
  16.0 3.0 %collective-permute-done.1 = f32[2,256,512]{2,1,0:T(8,128)} collective-permute-done((f32[2,256,512]{2,1,0:T(8,128)}, f32[2,256,512]{2,1,0:T(8,128)}, u32[]{:S(2)}, u32[]{:S(2)}) %collective-permute-start.1) | collective-permute-done | bytes 1048608 | tf_op jit(solution)/shard_map/ppermute | solution.py:384
  19.0 1.3 %constant_dynamic-update-slice_fusion.ext = f32[2,512,512]{2,1,0:T(8,128)S(1)} fusion(f32[2,512,512]{2,1,0:T(8,128)S(1)} %pad.4, f32[2,256,512]{2,1,0:T(8,128)} %collective-permute-done.1), kind=kLoop, calls=%fused_computation.4 | loop fusion | bytes 2097152 | tf_op jit(solution)/shard_map/dynamic_update_slice | solution.py:410
  20.3 0.0 copy-done.2
  20.3 3.5 %frames.1 = (f32[256,256]{1,0:T(8,128)S(1)}, f32[256,256]{1,0:T(8,128)S(1)}, f32[2,512,512]{2,1,0:T(8,128)S(1)}) custom-call(s32[2,10]{1,0:T(2,128)S(1)} %pad_add_fusion.facts, f32[2,512,512]{2,1,0:T(8,128)S(1)} %constant_dynamic-update-slice_fusion.ext, f32[2,256,256]{2,1,0:T(8,128)S(1)} %copy-done, f32[4,256,256]{2,1,0:T(8,128)S(1)} %get-tuple-element.15.amp, ...), custom_call_target="tpu_custom_call" | custom-call | flops 3300000000 | bytes 8000000 | tf_op jit(solution)/shard_map/frames/pallas_call | solution.py:411
  23.8 1.9 %collective-permute-start.2 = (f32[256,256]{1,0:T(8,128)S(1)}, f32[256,256]{1,0:T(8,128)S(1)}, u32[]{:S(2)}, u32[]{:S(2)}) collective-permute-start(f32[256,256]{1,0:T(8,128)S(1)} %get-tuple-element.17), channel_id=1, source_target_pairs={{0,1},{1,0},{2,3},{3,2},{4,5},{5,4},{6,7},{7,6},{8,9},{9,8},{10,11... | collective-permute-start | bytes 786440 | tf_op jit(solution)/shard_map/ppermute | solution.py:435
  25.7 1.0 %slice.6 = f32[2,256,512]{2,1,0:T(8,128)} slice(f32[2,512,512]{2,1,0:T(8,128)S(1)} %get-tuple-element.20), slice={[0:2], [256:512], [0:512]} | slice | bytes 2097152 | tf_op jit(solution)/shard_map/slice | solution.py:432
  26.7 7.1 %collective-permute-start.3 = (f32[2,256,512]{2,1,0:T(8,128)}, f32[2,256,512]{2,1,0:T(8,128)}, u32[]{:S(2)}, u32[]{:S(2)}) collective-permute-start(f32[2,256,512]{2,1,0:T(8,128)} %slice.6), channel_id=1, source_target_pairs={{0,1},{1,2},{2,3},{3,4},{4,5},{5,6},{6,7},{7,8},{8,9},{9,10},{10,1... | collective-permute-start | bytes 3145736 | tf_op jit(solution)/shard_map/ppermute | solution.py:436
  33.8 0.0 collective-permute-done.2
  33.9 20.0 %all_to_all.15 = f32[32,8,256]{2,1,0:T(8,128)S(1)} all-to-all(f32[32,8,256]{2,1,0:T(8,128)S(1)} %add_bitcast_fusion), channel_id=1, replica_groups={{0,2,4,6,64,66,68,70,128,130,132,134,192,194,196,198,256,258,260,262,32..., dimensions={0} | all-to-all | bytes 524288 | tf_op jit(solution)/shard_map/all_to_all | solution.py:366
  53.9 19.4 %all_to_all.16 = f32[8,8,256]{2,1,0:T(8,128)S(1)} all-to-all(f32[8,8,256]{2,1,0:T(8,128)S(1)} %broadcast_in_dim.7), channel_id=1, replica_groups={{0,8,16,24,32,40,48,56},{1,3,5,7,65,67,69,71},{2,10,18,26,34,42,50,58},..., dimensions={0} | all-to-all | bytes 131072 | tf_op jit(solution)/shard_map/all_to_all | solution.py:366
  73.4 0.0 collective-permute-done.3
  73.4 14.3 %all_to_all.17 = f32[32,8,256]{2,1,0:T(8,128)S(1)} all-to-all(f32[32,8,256]{2,1,0:T(8,128)S(1)} %broadcast_in_dim.8), channel_id=1, replica_groups={{0,2,4,6,64,66,68,70,128,130,132,134,192,194,196,198,256,258,260,262,32..., dimensions={0} | all-to-all | bytes 524288 | tf_op jit(solution)/shard_map/all_to_all | solution.py:366
  87.7 7.6 %collective-permute-start.4 = (f32[256,256]{1,0:T(8,128)S(1)}, f32[256,256]{1,0:T(8,128)S(1)}, u32[]{:S(2)}, u32[]{:S(2)}) collective-permute-start(f32[256,256]{1,0:T(8,128)S(1)} %bitcast.11), channel_id=1, source_target_pairs={{0,1},{1,0},{2,3},{3,2},{4,5},{5,4},{6,7},{7,6},{8,9},{9,8},{10,11... | collective-permute-start | bytes 786440 | tf_op jit(solution)/shard_map/ppermute | solution.py:443
  95.3 2.9 %multiply_subtract_fusion = f32[2,256,512]{2,1,0:T(8,128)} fusion(f32[2,256,512]{2,1,0:T(8,128)} %param.8, f32[2,256,512]{2,1,0:T(8,128)} %collective-permute-done.3, f32[2,512,512]{2,1,0:T(8,128)S(1)} %get-tuple-element.20, f32[256,512]{1,0:T(8,128)S(1)} %get-tuple-element.22), kind=kLoop, calls=%fused_computation | loop fusion | flops 786432 | bytes 4718592 | tf_op jit(solution)/shard_map/sub | solution.py:445
  98.2 0.0 collective-permute-done.4.other_ref
  98.2 1.6 %update.1 = f32[2,256,256]{2,1,0:T(8,128)} custom-call(s32[2,10]{1,0:T(2,128)S(1)} %pad_add_fusion.facts, f32[256,256]{1,0:T(8,128)S(1)} %bitcast.12, f32[256,256]{1,0:T(8,128)S(1)} %collective-permute-done.4.other_ref, f32[2,256,256]{2,1,0:T(8,128)S(1)} %copy-done), custom_call_target="tpu_custom_call" | custom-call | flops 1000000 | bytes 1600000 | tf_op jit(solution)/shard_map/update/pallas_call | solution.py:449
  (6 shorter events, 0.1 us)
Async XLA Ops:
  0.6 13.8 %copy-start.3 = (bf16[256,256]{1,0:T(8,128)(2,1)S(1)}, bf16[256,256]{1,0:T(8,128)(2,1)}, u32[]{:S(2)}) copy-start(bf16[256,256]{1,0:T(8,128)(2,1)} %constant.27.clone.order_ref) | copy-start | bytes 393220
  0.6 13.8 %copy-start = (f32[2,256,256]{2,1,0:T(8,128)S(1)}, f32[2,256,256]{2,1,0:T(8,128)}, u32[]{:S(2)}) copy-start(f32[2,256,256]{2,1,0:T(8,128)} %probe_ref.3) | copy-start | bytes 1572868
  0.7 13.8 %copy-start.1 = (f32[1,1,4,256,256]{4,3,2,1,0:T(8,128)S(1)}, f32[1,1,4,256,256]{4,3,2,1,0:T(8,128)}, u32[]{:S(2)}) copy-start(f32[1,1,4,256,256]{4,3,2,1,0:T(8,128)} %param.10) | copy-start | bytes 3145732
  0.7 18.3 %collective-permute-start.1 = (f32[2,256,512]{2,1,0:T(8,128)}, f32[2,256,512]{2,1,0:T(8,128)}, u32[]{:S(2)}, u32[]{:S(2)}) collective-permute-start(f32[2,256,512]{2,1,0:T(8,128)} %param.8), channel_id=1, source_target_pairs={{1,0},{2,1},{3,2},{4,3},{5,4},{6,5},{7,6},{8,7},{9,8},{10,9},{11,1... | collective-permute-start | bytes 3145736 | tf_op jit(solution)/shard_map/ppermute | solution.py:384
  11.0 3.4 %collective-permute-start = (s32[10]{0:T(128)S(1)}, s32[10]{0:T(128)S(1)}, u32[]{:S(2)}, u32[]{:S(2)}) collective-permute-start(s32[10]{0:T(128)S(1)} %pad_add_fusion.1), channel_id=1, source_target_pairs={{0,1},{1,2},{2,3},{3,4},{4,5},{5,6},{6,7},{7,8},{8,9},{9,10},{10,1... | collective-permute-start | bytes 128 | tf_op jit(solution)/shard_map/ppermute | solution.py:387
  14.5 5.8 %copy-start.2 = (bf16[4,2,256,256]{3,2,1,0:T(8,128)(2,1)S(1)}, bf16[4,2,256,256]{3,2,1,0:T(8,128)(2,1)}, u32[]{:S(2)}) copy-start(bf16[4,2,256,256]{3,2,1,0:T(8,128)(2,1)} %constant.28.clone.tables) | copy-start | bytes 3145732
  23.8 10.1 %collective-permute-start.2 = (f32[256,256]{1,0:T(8,128)S(1)}, f32[256,256]{1,0:T(8,128)S(1)}, u32[]{:S(2)}, u32[]{:S(2)}) collective-permute-start(f32[256,256]{1,0:T(8,128)S(1)} %get-tuple-element.17), channel_id=1, source_target_pairs={{0,1},{1,0},{2,3},{3,2},{4,5},{5,4},{6,7},{7,6},{8,9},{9,8},{10,11... | collective-permute-start | bytes 786440 | tf_op jit(solution)/shard_map/ppermute | solution.py:435
  26.7 46.6 %collective-permute-start.3 = (f32[2,256,512]{2,1,0:T(8,128)}, f32[2,256,512]{2,1,0:T(8,128)}, u32[]{:S(2)}, u32[]{:S(2)}) collective-permute-start(f32[2,256,512]{2,1,0:T(8,128)} %slice.6), channel_id=1, source_target_pairs={{0,1},{1,2},{2,3},{3,4},{4,5},{5,6},{6,7},{7,8},{8,9},{9,10},{10,1... | collective-permute-start | bytes 3145736 | tf_op jit(solution)/shard_map/ppermute | solution.py:436
  87.7 10.5 %collective-permute-start.4 = (f32[256,256]{1,0:T(8,128)S(1)}, f32[256,256]{1,0:T(8,128)S(1)}, u32[]{:S(2)}, u32[]{:S(2)}) collective-permute-start(f32[256,256]{1,0:T(8,128)S(1)} %bitcast.11), channel_id=1, source_target_pairs={{0,1},{1,0},{2,3},{3,2},{4,5},{5,4},{6,7},{7,6},{8,9},{9,8},{10,11... | collective-permute-start | bytes 786440 | tf_op jit(solution)/shard_map/ppermute | solution.py:443

commit v6 on v4

--- a/solution.py
+++ b/solution.py
@@ -12,8 +12,8 @@
 SLOTS = 4
 COUNT, CORE = 2 * SLOTS, 2 * SLOTS + 1
 BLOCK = 32
-WIDE = (("x", "z"), ("x", "y"))
-LINE = (("y",), ("z",))
+WIDE = (("x_lo", "z"), ("x_lo", "y"))
+LINE = (("x_hi", "y"), ("x_hi", "z"))
 
 
 def in_two(table):
@@ -346,7 +346,8 @@
 def place_of(device):
     region, dev = divmod(device, 64)
     return {
-        "x": region // 2,
+        "x_hi": region // 4,
+        "x_lo": region // 2 % 2,
         "z": (region % 2) * 4 + (dev // 2) % 4,
         "y": dev // 8,
         "core": dev % 2,
@@ -434,7 +435,7 @@
     swap = [(i, i ^ 1) for i in range(peers)]
     plane = mine + lax.ppermute(other, "dev", swap)
     incoming = lax.ppermute(over, "dev", steps)
-    parts = exchanged(plane.reshape(32, size // 32, size), WIDE)
+    parts = exchanged(plane.reshape(16, size // 16, size), WIDE)
     share = jnp.sum(parts, axis=0)
     share = jnp.sum(copies(share, LINE), axis=0)
     share, total = lax.optimization_barrier((share, total))

time: 97.9 us -> 89.7 us (0.916)
  blocking collectives: 39.6 us -> 18.9 us
  starting transfers between devices: 32 us -> 42.4 us
  waiting for transfers between devices: 9.97 us -> 11 us
    all_to_all x2 -> x1, blocking collectives: 39.6 us -> 18.9 us  [exchanged(): lax.all_to_all(parts, AXES, 0, 0, tiled=True, axis_index_groups=groups_al...]
    all_to_all x1 -> x2, starting transfers between devices: 4.88 us -> 19.7 us  [exchanged(): lax.all_to_all(parts, AXES, 0, 0, tiled=True, axis_index_groups=groups_al...]
    ppermute x1, starting transfers between devices: 7.42 us -> 3.64 us  [on_device(): plane_other = lax.ppermute(plane, 'dev', swap)]
    ppermute x1, waiting for transfers between devices: 0.01 us -> 1.14 us  [on_device(): plane = mine + lax.ppermute(other, 'dev', swap)]
    all_to_all x1 -> x2, waiting for transfers between devices: 6.7 us -> 6.44 us  [exchanged(): lax.all_to_all(parts, AXES, 0, 0, tiled=True, axis_index_groups=groups_al...]
  transfers between devices with their start and end apart: 6 -> 7, of which waited for: 3 -> 5; matrix products, arithmetic and copies ran while one was open for 7% -> 8% of each run, Pallas kernels for 2% -> 2%
where the time goes in v6:
time: 89.7 us; the launch traced here: 88.7 us
  starting transfers between devices  42.4 us (47%)
  blocking collectives  18.9 us (21%)
  waiting for transfers between devices  11 us (12%)
  Pallas kernels  7.08 us (8%)
  other arithmetic  4.48 us (5%)
  local copies, waits for them, and re-layouts  3.38 us (4%)
  between operations  1.47 us (2%)
    all_to_all x2, starting transfers between devices, exchanged(): lax.all_to_all(parts, AXES, 0, 0, tiled=True, axis_index_groups=groups_al...  19.7 us
    all_to_all x1, blocking collectives, exchanged(): lax.all_to_all(parts, AXES, 0, 0, tiled=True, axis_index_groups=groups_al...  18.9 us
    ppermute x1, starting transfers between devices, on_device(): lax.ppermute(object_field, 'dev', [(i, i - 1) for i in range(1, peers)])  8.92 us
    all_to_all x2, waiting for transfers between devices, exchanged(): lax.all_to_all(parts, AXES, 0, 0, tiled=True, axis_index_groups=groups_al...  6.44 us
    ppermute x1, starting transfers between devices, on_device(): incoming = lax.ppermute(over, 'dev', steps)  5.48 us
    ppermute x1, starting transfers between devices, on_device(): plane_other = lax.ppermute(plane, 'dev', swap)  3.64 us
    pallas_call x1, Pallas kernels, on_device(): pl.pallas_call(frames_kernel, out_shape=(jax.ShapeDtypeStruct((size, size...  3.36 us
    sub x1, other arithmetic, on_device(): object_field - jnp.concatenate([own[:, :size] + incoming, own[:, size:]],...  2.95 us
  transfers between devices with their start and end apart: 7, of which 5 were waited for; matrix products, arithmetic and copies ran while one was open for 8% of the time, Pallas kernels for 2%

profile of v6, /device:TPU:1, one launch (start us, length us, event | category | flops | bytes accessed | tf_op | source)
XLA Modules:
  0.0 88.7 jit_solution(5760009942317112262)
XLA Ops:
  0.6 0.0 copy-start.3
  0.6 0.0 copy-start
  0.7 0.0 copy-start.1
  0.7 8.9 %collective-permute-start.1 = (f32[2,256,512]{2,1,0:T(8,128)}, f32[2,256,512]{2,1,0:T(8,128)S(1)}, u32[]{:S(2)}, u32[]{:S(2)}) collective-permute-start(f32[2,256,512]{2,1,0:T(8,128)} %param.8), channel_id=1, source_target_pairs={{1,0},{2,1},{3,2},{4,3},{5,4},{6,5},{7,6},{8,7},{9,8},{10,9},{11,1... | collective-permute-start | bytes 3145736 | tf_op jit(solution)/shard_map/ppermute | solution.py:385
  10.2 0.8 pad_add_fusion.1
  11.0 1.9 %collective-permute-start = (s32[10]{0:T(128)S(1)}, s32[10]{0:T(128)S(1)}, u32[]{:S(2)}, u32[]{:S(2)}) collective-permute-start(s32[10]{0:T(128)S(1)} %pad_add_fusion.1), channel_id=1, source_target_pairs={{0,1},{1,2},{2,3},{3,4},{4,5},{5,6},{6,7},{7,8},{8,9},{9,10},{10,1... | collective-permute-start | bytes 128 | tf_op jit(solution)/shard_map/ppermute | solution.py:388
  12.9 1.5 %pad.4 = f32[2,512,512]{2,1,0:T(8,128)S(1)} pad(f32[2,256,512]{2,1,0:T(8,128)} %param.8, f32[]{:T(128)} %constant.25.clone.1), padding=0_0x0_256x0_0 | pad | bytes 3145732 | tf_op jit(solution)/shard_map/jit(_pad)/pad | solution.py:409
  14.4 0.0 collective-permute-done
  14.4 0.0 copy-done.3
  14.5 0.0 copy-done
  14.5 0.0 copy-done.1
  14.5 0.0 copy-start.2
  14.5 2.1 %prepare.1 = (f32[4,256,256]{2,1,0:T(8,128)S(1)}, f32[256,512]{1,0:T(8,128)S(1)}) custom-call(s32[2,10]{1,0:T(2,128)S(1)} %pad_add_fusion.facts, f32[4,256,256]{2,1,0:T(8,128)S(1)} %bitcast.12, f32[2,256,256]{2,1,0:T(8,128)S(1)} %copy-done, bf16[256,256]{1,0:T(8,128)(2,1)S(1)} %copy-done.3), custom_call_target="tpu_custom_call" | custom-call | flops 800000000 | bytes 3200000 | tf_op jit(solution)/shard_map/prepare/pallas_call | solution.py:391
  16.6 2.3 %collective-permute-done.1 = f32[2,256,512]{2,1,0:T(8,128)S(1)} collective-permute-done((f32[2,256,512]{2,1,0:T(8,128)}, f32[2,256,512]{2,1,0:T(8,128)S(1)}, u32[]{:S(2)}, u32[]{:S(2)}) %collective-permute-start.1) | collective-permute-done | bytes 1048608 | tf_op jit(solution)/shard_map/ppermute | solution.py:385
  18.9 0.1 constant_dynamic-update-slice_fusion.ext
  19.0 0.0 copy-done.2
  19.0 3.4 %frames.1 = (f32[256,256]{1,0:T(8,128)S(1)}, f32[256,256]{1,0:T(8,128)S(1)}, f32[2,512,512]{2,1,0:T(8,128)S(1)}) custom-call(s32[2,10]{1,0:T(2,128)S(1)} %pad_add_fusion.facts, f32[2,512,512]{2,1,0:T(8,128)S(1)} %constant_dynamic-update-slice_fusion.ext, f32[2,256,256]{2,1,0:T(8,128)S(1)} %copy-done, f32[4,256,256]{2,1,0:T(8,128)S(1)} %get-tuple-element.15.amp, ...), custom_call_target="tpu_custom_call" | custom-call | flops 3300000000 | bytes 8000000 | tf_op jit(solution)/shard_map/frames/pallas_call | solution.py:412
  22.3 2.8 %collective-permute-start.2 = (f32[256,256]{1,0:T(8,128)S(1)}, f32[256,256]{1,0:T(8,128)S(1)}, u32[]{:S(2)}, u32[]{:S(2)}) collective-permute-start(f32[256,256]{1,0:T(8,128)S(1)} %get-tuple-element.17), channel_id=1, source_target_pairs={{0,1},{1,0},{2,3},{3,2},{4,5},{5,4},{6,7},{7,6},{8,9},{9,8},{10,11... | collective-permute-start | bytes 786440 | tf_op jit(solution)/shard_map/ppermute | solution.py:436
  25.1 1.1 %collective-permute-done.2 = f32[256,256]{1,0:T(8,128)S(1)} collective-permute-done((f32[256,256]{1,0:T(8,128)S(1)}, f32[256,256]{1,0:T(8,128)S(1)}, u32[]{:S(2)}, u32[]{:S(2)}) %collective-permute-start.2) | collective-permute-done | bytes 262176 | tf_op jit(solution)/shard_map/ppermute | solution.py:436
  26.2 0.7 add.13
  27.0 13.4 %all-to-all-start = ((f32[16,16,256]{2,1,0:T(8,128)}), f32[16,16,256]{2,1,0:T(8,128)S(1)}, u32[]{:S(2)}, u32[]{:S(2)}) async-start(f32[16,16,256]{2,1,0:T(8,128)} %bitcast.7), calls=%async_computation | async-start | bytes 524288 | tf_op jit(solution)/shard_map/all_to_all | solution.py:367
  40.3 1.0 %slice.7 = f32[2,256,512]{2,1,0:T(8,128)} slice(f32[2,512,512]{2,1,0:T(8,128)S(1)} %get-tuple-element.20), slice={[0:2], [256:512], [0:512]} | slice | bytes 2097152 | tf_op jit(solution)/shard_map/slice | solution.py:433
  41.4 5.5 %collective-permute-start.3 = (f32[2,256,512]{2,1,0:T(8,128)}, f32[2,256,512]{2,1,0:T(8,128)}, u32[]{:S(2)}, u32[]{:S(2)}) collective-permute-start(f32[2,256,512]{2,1,0:T(8,128)} %slice.7), channel_id=1, source_target_pairs={{0,1},{1,2},{2,3},{3,4},{4,5},{5,6},{6,7},{7,8},{8,9},{9,10},{10,1... | collective-permute-start | bytes 3145736 | tf_op jit(solution)/shard_map/ppermute | solution.py:437
  46.9 1.3 %all-to-all-done = f32[16,16,256]{2,1,0:T(8,128)S(1)} async-done(((f32[16,16,256]{2,1,0:T(8,128)}), f32[16,16,256]{2,1,0:T(8,128)S(1)}, u32[]{:S(2)}, u32[]{:S(2)}) %all-to-all-start) | async-done | bytes 262176 | tf_op jit(solution)/shard_map/all_to_all | solution.py:367
  48.3 18.9 %all_to_all.15 = f32[16,16,256]{2,1,0:T(8,128)S(1)} all-to-all(f32[16,16,256]{2,1,0:T(8,128)S(1)} %broadcast_in_dim.7), channel_id=1, replica_groups={{0,8,16,24,32,40,48,56,256,264,272,280,288,296,304,312},{1,3,5,7,65,67,..., dimensions={0} | all-to-all | bytes 524288 | tf_op jit(solution)/shard_map/all_to_all | solution.py:367
  67.2 0.7 broadcast_in_dim.8
  67.9 6.3 %all-to-all-start.2 = ((f32[16,16,256]{2,1,0:T(8,128)}), f32[16,16,256]{2,1,0:T(8,128)S(1)}, u32[]{:S(2)}, u32[]{:S(2)}) async-start(f32[16,16,256]{2,1,0:T(8,128)} %broadcast_in_dim.8), calls=%async_computation.2 | async-start | bytes 524288 | tf_op jit(solution)/shard_map/all_to_all | solution.py:367
  74.3 0.0 collective-permute-done.3
  74.3 2.9 %multiply_subtract_fusion = f32[2,256,512]{2,1,0:T(8,128)} fusion(f32[2,256,512]{2,1,0:T(8,128)} %param.8, f32[2,256,512]{2,1,0:T(8,128)} %collective-permute-done.3, f32[2,512,512]{2,1,0:T(8,128)S(1)} %get-tuple-element.20, f32[256,512]{1,0:T(8,128)S(1)} %get-tuple-element.21), kind=kLoop, calls=%fused_computation | loop fusion | flops 786432 | bytes 4718592 | tf_op jit(solution)/shard_map/sub | solution.py:443
  77.2 5.1 %all-to-all-done.2 = f32[16,16,256]{2,1,0:T(8,128)S(1)} async-done(((f32[16,16,256]{2,1,0:T(8,128)}), f32[16,16,256]{2,1,0:T(8,128)S(1)}, u32[]{:S(2)}, u32[]{:S(2)}) %all-to-all-start.2) | async-done | bytes 262176 | tf_op jit(solution)/shard_map/all_to_all | solution.py:367
  82.3 3.6 %collective-permute-start.4 = (f32[256,256]{1,0:T(8,128)S(1)}, f32[256,256]{1,0:T(8,128)S(1)}, u32[]{:S(2)}, u32[]{:S(2)}) collective-permute-start(f32[256,256]{1,0:T(8,128)S(1)} %bitcast.10), channel_id=1, source_target_pairs={{0,1},{1,0},{2,3},{3,2},{4,5},{5,4},{6,7},{7,6},{8,9},{9,8},{10,11... | collective-permute-start | bytes 786440 | tf_op jit(solution)/shard_map/ppermute | solution.py:448
  86.0 1.1 %collective-permute-done.4.other_ref = f32[256,256]{1,0:T(8,128)S(1)} collective-permute-done((f32[256,256]{1,0:T(8,128)S(1)}, f32[256,256]{1,0:T(8,128)S(1)}, u32[]{:S(2)}, u32[]{:S(2)}) %collective-permute-start.4) | collective-permute-done | bytes 262176 | tf_op jit(solution)/shard_map/ppermute | solution.py:448
  87.1 1.6 %update.1 = f32[2,256,256]{2,1,0:T(8,128)} custom-call(s32[2,10]{1,0:T(2,128)S(1)} %pad_add_fusion.facts, f32[256,256]{1,0:T(8,128)S(1)} %bitcast.11, f32[256,256]{1,0:T(8,128)S(1)} %collective-permute-done.4.other_ref, f32[2,256,256]{2,1,0:T(8,128)S(1)} %copy-done), custom_call_target="tpu_custom_call" | custom-call | flops 1000000 | bytes 1600000 | tf_op jit(solution)/shard_map/update/pallas_call | solution.py:450
  (4 shorter events, 0.1 us)
Async XLA Ops:
  0.6 13.8 %copy-start.3 = (bf16[256,256]{1,0:T(8,128)(2,1)S(1)}, bf16[256,256]{1,0:T(8,128)(2,1)}, u32[]{:S(2)}) copy-start(bf16[256,256]{1,0:T(8,128)(2,1)} %constant.27.clone.order_ref) | copy-start | bytes 393220
  0.6 13.8 %copy-start = (f32[2,256,256]{2,1,0:T(8,128)S(1)}, f32[2,256,256]{2,1,0:T(8,128)}, u32[]{:S(2)}) copy-start(f32[2,256,256]{2,1,0:T(8,128)} %probe_ref.3) | copy-start | bytes 1572868
  0.7 13.8 %copy-start.1 = (f32[1,1,4,256,256]{4,3,2,1,0:T(8,128)S(1)}, f32[1,1,4,256,256]{4,3,2,1,0:T(8,128)}, u32[]{:S(2)}) copy-start(f32[1,1,4,256,256]{4,3,2,1,0:T(8,128)} %param.10) | copy-start | bytes 3145732
  0.7 18.2 %collective-permute-start.1 = (f32[2,256,512]{2,1,0:T(8,128)}, f32[2,256,512]{2,1,0:T(8,128)S(1)}, u32[]{:S(2)}, u32[]{:S(2)}) collective-permute-start(f32[2,256,512]{2,1,0:T(8,128)} %param.8), channel_id=1, source_target_pairs={{1,0},{2,1},{3,2},{4,3},{5,4},{6,5},{7,6},{8,7},{9,8},{10,9},{11,1... | collective-permute-start | bytes 3145736 | tf_op jit(solution)/shard_map/ppermute | solution.py:385
  11.0 3.4 %collective-permute-start = (s32[10]{0:T(128)S(1)}, s32[10]{0:T(128)S(1)}, u32[]{:S(2)}, u32[]{:S(2)}) collective-permute-start(s32[10]{0:T(128)S(1)} %pad_add_fusion.1), channel_id=1, source_target_pairs={{0,1},{1,2},{2,3},{3,4},{4,5},{5,6},{6,7},{7,8},{8,9},{9,10},{10,1... | collective-permute-start | bytes 128 | tf_op jit(solution)/shard_map/ppermute | solution.py:388
  14.5 4.5 %copy-start.2 = (bf16[4,2,256,256]{3,2,1,0:T(8,128)(2,1)S(1)}, bf16[4,2,256,256]{3,2,1,0:T(8,128)(2,1)}, u32[]{:S(2)}) copy-start(bf16[4,2,256,256]{3,2,1,0:T(8,128)(2,1)} %constant.28.clone.tables) | copy-start | bytes 3145732
  22.3 3.9 %collective-permute-start.2 = (f32[256,256]{1,0:T(8,128)S(1)}, f32[256,256]{1,0:T(8,128)S(1)}, u32[]{:S(2)}, u32[]{:S(2)}) collective-permute-start(f32[256,256]{1,0:T(8,128)S(1)} %get-tuple-element.17), channel_id=1, source_target_pairs={{0,1},{1,0},{2,3},{3,2},{4,5},{5,4},{6,7},{7,6},{8,9},{9,8},{10,11... | collective-permute-start | bytes 786440 | tf_op jit(solution)/shard_map/ppermute | solution.py:436
  27.0 21.2 %all-to-all-start = ((f32[16,16,256]{2,1,0:T(8,128)}), f32[16,16,256]{2,1,0:T(8,128)S(1)}, u32[]{:S(2)}, u32[]{:S(2)}) async-start(f32[16,16,256]{2,1,0:T(8,128)} %bitcast.7), calls=%async_computation | async-start | bytes 524288 | tf_op jit(solution)/shard_map/all_to_all | solution.py:367
  41.4 32.9 %collective-permute-start.3 = (f32[2,256,512]{2,1,0:T(8,128)}, f32[2,256,512]{2,1,0:T(8,128)}, u32[]{:S(2)}, u32[]{:S(2)}) collective-permute-start(f32[2,256,512]{2,1,0:T(8,128)} %slice.7), channel_id=1, source_target_pairs={{0,1},{1,2},{2,3},{3,4},{4,5},{5,6},{6,7},{7,8},{8,9},{9,10},{10,1... | collective-permute-start | bytes 3145736 | tf_op jit(solution)/shard_map/ppermute | solution.py:437
  67.9 14.4 %all-to-all-start.2 = ((f32[16,16,256]{2,1,0:T(8,128)}), f32[16,16,256]{2,1,0:T(8,128)S(1)}, u32[]{:S(2)}, u32[]{:S(2)}) async-start(f32[16,16,256]{2,1,0:T(8,128)} %broadcast_in_dim.8), calls=%async_computation.2 | async-start | bytes 524288 | tf_op jit(solution)/shard_map/all_to_all | solution.py:367
  82.3 4.8 %collective-permute-start.4 = (f32[256,256]{1,0:T(8,128)S(1)}, f32[256,256]{1,0:T(8,128)S(1)}, u32[]{:S(2)}, u32[]{:S(2)}) collective-permute-start(f32[256,256]{1,0:T(8,128)S(1)} %bitcast.10), channel_id=1, source_target_pairs={{0,1},{1,0},{2,3},{3,2},{4,5},{5,4},{6,7},{7,6},{8,9},{9,8},{10,11... | collective-permute-start | bytes 786440 | tf_op jit(solution)/shard_map/ppermute | solution.py:448

commit v7 on v6

--- a/solution.py
+++ b/solution.py
@@ -438,7 +438,7 @@
     parts = exchanged(plane.reshape(16, size // 16, size), WIDE)
     share = jnp.sum(parts, axis=0)
     share = jnp.sum(copies(share, LINE), axis=0)
-    share, total = lax.optimization_barrier((share, total))
+    share, total, incoming = lax.optimization_barrier((share, total, incoming))
     own = total[:, :band]
     new_field = object_field - jnp.concatenate(
         [own[:, :size] + incoming, own[:, size:]], axis=1

time: 89.7 us -> 97 us (1.081)
  blocking collectives: 18.9 us -> 44 us
  starting transfers between devices: 42.4 us -> 28.5 us
  waiting for transfers between devices: 11 us -> 8.7 us
    all_to_all x1 -> x2, blocking collectives: 18.9 us -> 44 us  [exchanged(): lax.all_to_all(parts, AXES, 0, 0, tiled=True, axis_index_groups=groups_al...]
    all_to_all x2 -> x1, starting transfers between devices: 19.7 us -> 4.53 us  [exchanged(): lax.all_to_all(parts, AXES, 0, 0, tiled=True, axis_index_groups=groups_al...]
    ppermute x1, starting transfers between devices: 3.64 us -> 6.87 us  [on_device(): plane_other = lax.ppermute(plane, 'dev', swap)]
    ppermute x1, starting transfers between devices: 5.48 us -> 3.53 us  [on_device(): incoming = lax.ppermute(over, 'dev', steps)]
    all_to_all x2 -> x1, waiting for transfers between devices: 6.44 us -> 4.81 us  [exchanged(): lax.all_to_all(parts, AXES, 0, 0, tiled=True, axis_index_groups=groups_al...]
    ppermute x1, waiting for transfers between devices: 1.14 us -> 0.01 us  [on_device(): plane = mine + lax.ppermute(other, 'dev', swap)]
  transfers between devices with their start and end apart: 7 -> 6, of which waited for: 5 -> 3; matrix products, arithmetic and copies ran while one was open for 8% -> 7% of each run, Pallas kernels for 2% -> 2%
where the time goes in v7:
time: 97 us; the launch traced here: 96.5 us
  blocking collectives  44 us (45%)
  starting transfers between devices  28.5 us (29%)
  waiting for transfers between devices  8.7 us (9%)
  Pallas kernels  6.63 us (7%)
  other arithmetic  3.78 us (4%)
  local copies, waits for them, and re-layouts  3.38 us (3%)
  between operations  1.48 us (2%)
    all_to_all x2, blocking collectives, exchanged(): lax.all_to_all(parts, AXES, 0, 0, tiled=True, axis_index_groups=groups_al...  44 us
    ppermute x1, starting transfers between devices, on_device(): lax.ppermute(object_field, 'dev', [(i, i - 1) for i in range(1, peers)])  8.92 us
    ppermute x1, starting transfers between devices, on_device(): plane_other = lax.ppermute(plane, 'dev', swap)  6.87 us
    all_to_all x1, waiting for transfers between devices, exchanged(): lax.all_to_all(parts, AXES, 0, 0, tiled=True, axis_index_groups=groups_al...  4.81 us
    all_to_all x1, starting transfers between devices, exchanged(): lax.all_to_all(parts, AXES, 0, 0, tiled=True, axis_index_groups=groups_al...  4.53 us
    ppermute x1, starting transfers between devices, on_device(): incoming = lax.ppermute(over, 'dev', steps)  3.53 us
    pallas_call x1, Pallas kernels, on_device(): pl.pallas_call(frames_kernel, out_shape=(jax.ShapeDtypeStruct((size, size...  3.37 us
    sub x1, other arithmetic, on_device(): object_field - jnp.concatenate([own[:, :size] + incoming, own[:, size:]],...  2.95 us
  transfers between devices with their start and end apart: 6, of which 3 were waited for; matrix products, arithmetic and copies ran while one was open for 7% of the time, Pallas kernels for 2%

profile of v7, /device:TPU:1, one launch (start us, length us, event | category | flops | bytes accessed | tf_op | source)
XLA Modules:
  0.0 96.5 jit_solution(707730782708421462)
XLA Ops:
  0.6 0.0 copy-start.3
  0.6 0.0 copy-start
  0.7 0.0 copy-start.1
  0.7 8.9 %collective-permute-start.1 = (f32[2,256,512]{2,1,0:T(8,128)}, f32[2,256,512]{2,1,0:T(8,128)S(1)}, u32[]{:S(2)}, u32[]{:S(2)}) collective-permute-start(f32[2,256,512]{2,1,0:T(8,128)} %param.8), channel_id=1, source_target_pairs={{1,0},{2,1},{3,2},{4,3},{5,4},{6,5},{7,6},{8,7},{9,8},{10,9},{11,1... | collective-permute-start | bytes 3145736 | tf_op jit(solution)/shard_map/ppermute | solution.py:385
  10.2 0.8 pad_add_fusion.1
  11.0 1.9 %collective-permute-start = (s32[10]{0:T(128)S(1)}, s32[10]{0:T(128)S(1)}, u32[]{:S(2)}, u32[]{:S(2)}) collective-permute-start(s32[10]{0:T(128)S(1)} %pad_add_fusion.1), channel_id=1, source_target_pairs={{0,1},{1,2},{2,3},{3,4},{4,5},{5,6},{6,7},{7,8},{8,9},{9,10},{10,1... | collective-permute-start | bytes 128 | tf_op jit(solution)/shard_map/ppermute | solution.py:388
  12.9 1.5 %pad.4 = f32[2,512,512]{2,1,0:T(8,128)S(1)} pad(f32[2,256,512]{2,1,0:T(8,128)} %param.8, f32[]{:T(128)} %constant.25.clone.1), padding=0_0x0_256x0_0 | pad | bytes 3145732 | tf_op jit(solution)/shard_map/jit(_pad)/pad | solution.py:409
  14.4 0.0 collective-permute-done
  14.4 0.0 copy-done.3
  14.5 0.0 copy-done
  14.5 0.0 copy-done.1
  14.5 0.0 copy-start.2
  14.5 1.6 %prepare.1 = (f32[4,256,256]{2,1,0:T(8,128)S(1)}, f32[256,512]{1,0:T(8,128)S(1)}) custom-call(s32[2,10]{1,0:T(2,128)S(1)} %pad_add_fusion.facts, f32[4,256,256]{2,1,0:T(8,128)S(1)} %bitcast.12, f32[2,256,256]{2,1,0:T(8,128)S(1)} %copy-done, bf16[256,256]{1,0:T(8,128)(2,1)S(1)} %copy-done.3), custom_call_target="tpu_custom_call" | custom-call | flops 800000000 | bytes 3200000 | tf_op jit(solution)/shard_map/prepare/pallas_call | solution.py:391
  16.1 2.7 %collective-permute-done.1 = f32[2,256,512]{2,1,0:T(8,128)S(1)} collective-permute-done((f32[2,256,512]{2,1,0:T(8,128)}, f32[2,256,512]{2,1,0:T(8,128)S(1)}, u32[]{:S(2)}, u32[]{:S(2)}) %collective-permute-start.1) | collective-permute-done | bytes 1048608 | tf_op jit(solution)/shard_map/ppermute | solution.py:385
  18.9 0.1 constant_dynamic-update-slice_fusion.ext
  19.0 0.0 copy-done.2
  19.0 3.4 %frames.1 = (f32[256,256]{1,0:T(8,128)S(1)}, f32[256,256]{1,0:T(8,128)S(1)}, f32[2,512,512]{2,1,0:T(8,128)S(1)}) custom-call(s32[2,10]{1,0:T(2,128)S(1)} %pad_add_fusion.facts, f32[2,512,512]{2,1,0:T(8,128)S(1)} %constant_dynamic-update-slice_fusion.ext, f32[2,256,256]{2,1,0:T(8,128)S(1)} %copy-done, f32[4,256,256]{2,1,0:T(8,128)S(1)} %get-tuple-element.16.amp, ...), custom_call_target="tpu_custom_call" | custom-call | flops 3300000000 | bytes 8000000 | tf_op jit(solution)/shard_map/frames/pallas_call | solution.py:412
  22.3 2.7 %collective-permute-start.2 = (f32[256,256]{1,0:T(8,128)S(1)}, f32[256,256]{1,0:T(8,128)S(1)}, u32[]{:S(2)}, u32[]{:S(2)}) collective-permute-start(f32[256,256]{1,0:T(8,128)S(1)} %get-tuple-element.18), channel_id=1, source_target_pairs={{0,1},{1,0},{2,3},{3,2},{4,5},{5,4},{6,7},{7,6},{8,9},{9,8},{10,11... | collective-permute-start | bytes 786440 | tf_op jit(solution)/shard_map/ppermute | solution.py:436
  25.1 1.0 %slice.6 = f32[2,256,512]{2,1,0:T(8,128)} slice(f32[2,512,512]{2,1,0:T(8,128)S(1)} %get-tuple-element.21), slice={[0:2], [256:512], [0:512]} | slice | bytes 2097152 | tf_op jit(solution)/shard_map/slice | solution.py:433
  26.1 3.5 %collective-permute-start.3 = (f32[2,256,512]{2,1,0:T(8,128)}, f32[2,256,512]{2,1,0:T(8,128)}, u32[]{:S(2)}, u32[]{:S(2)}) collective-permute-start(f32[2,256,512]{2,1,0:T(8,128)} %slice.6), channel_id=1, source_target_pairs={{0,1},{1,2},{2,3},{3,4},{4,5},{5,6},{6,7},{7,8},{8,9},{9,10},{10,1... | collective-permute-start | bytes 3145736 | tf_op jit(solution)/shard_map/ppermute | solution.py:437
  29.7 0.0 collective-permute-done.2
  29.7 19.4 %all_to_all.15 = f32[16,16,256]{2,1,0:T(8,128)S(1)} all-to-all(f32[16,16,256]{2,1,0:T(8,128)S(1)} %bitcast.13), channel_id=1, replica_groups={{0,2,4,6,64,66,68,70,128,130,132,134,192,194,196,198},{1,9,17,25,33,41,..., dimensions={0} | all-to-all | bytes 524288 | tf_op jit(solution)/shard_map/all_to_all | solution.py:367
  49.2 24.7 %all_to_all.16 = f32[16,16,256]{2,1,0:T(8,128)S(1)} all-to-all(f32[16,16,256]{2,1,0:T(8,128)S(1)} %broadcast_in_dim.7), channel_id=1, replica_groups={{0,8,16,24,32,40,48,56,256,264,272,280,288,296,304,312},{1,3,5,7,65,67,..., dimensions={0} | all-to-all | bytes 524288 | tf_op jit(solution)/shard_map/all_to_all | solution.py:367
  73.8 0.0 collective-permute-done.3
  73.8 0.7 broadcast_in_dim.8
  74.6 4.5 %all-to-all-start.2 = ((f32[16,16,256]{2,1,0:T(8,128)}), f32[16,16,256]{2,1,0:T(8,128)S(1)}, u32[]{:S(2)}, u32[]{:S(2)}) async-start(f32[16,16,256]{2,1,0:T(8,128)} %broadcast_in_dim.8), calls=%async_computation.2 | async-start | bytes 524288 | tf_op jit(solution)/shard_map/all_to_all | solution.py:367
  79.1 2.9 %multiply_subtract_fusion = f32[2,256,512]{2,1,0:T(8,128)} fusion(f32[2,256,512]{2,1,0:T(8,128)} %param.8, f32[2,256,512]{2,1,0:T(8,128)} %collective-permute-done.3, f32[2,512,512]{2,1,0:T(8,128)S(1)} %get-tuple-element.21, f32[256,512]{1,0:T(8,128)S(1)} %get-tuple-element.23), kind=kLoop, calls=%fused_computation | loop fusion | flops 786432 | bytes 4718592 | tf_op jit(solution)/shard_map/sub | solution.py:443
  82.1 4.8 %all-to-all-done.2 = f32[16,16,256]{2,1,0:T(8,128)S(1)} async-done(((f32[16,16,256]{2,1,0:T(8,128)}), f32[16,16,256]{2,1,0:T(8,128)S(1)}, u32[]{:S(2)}, u32[]{:S(2)}) %all-to-all-start.2) | async-done | bytes 262176 | tf_op jit(solution)/shard_map/all_to_all | solution.py:367
  86.9 6.9 %collective-permute-start.4 = (f32[256,256]{1,0:T(8,128)S(1)}, f32[256,256]{1,0:T(8,128)S(1)}, u32[]{:S(2)}, u32[]{:S(2)}) collective-permute-start(f32[256,256]{1,0:T(8,128)S(1)} %bitcast.10), channel_id=1, source_target_pairs={{0,1},{1,0},{2,3},{3,2},{4,5},{5,4},{6,7},{7,6},{8,9},{9,8},{10,11... | collective-permute-start | bytes 786440 | tf_op jit(solution)/shard_map/ppermute | solution.py:448
  93.8 1.1 %collective-permute-done.4.other_ref = f32[256,256]{1,0:T(8,128)S(1)} collective-permute-done((f32[256,256]{1,0:T(8,128)S(1)}, f32[256,256]{1,0:T(8,128)S(1)}, u32[]{:S(2)}, u32[]{:S(2)}) %collective-permute-start.4) | collective-permute-done | bytes 262176 | tf_op jit(solution)/shard_map/ppermute | solution.py:448
  94.9 1.6 %update.1 = f32[2,256,256]{2,1,0:T(8,128)} custom-call(s32[2,10]{1,0:T(2,128)S(1)} %pad_add_fusion.facts, f32[256,256]{1,0:T(8,128)S(1)} %bitcast.11, f32[256,256]{1,0:T(8,128)S(1)} %collective-permute-done.4.other_ref, f32[2,256,256]{2,1,0:T(8,128)S(1)} %copy-done), custom_call_target="tpu_custom_call" | custom-call | flops 1000000 | bytes 1600000 | tf_op jit(solution)/shard_map/update/pallas_call | solution.py:450
  (5 shorter events, 0.1 us)
Async XLA Ops:
  0.6 13.8 %copy-start.3 = (bf16[256,256]{1,0:T(8,128)(2,1)S(1)}, bf16[256,256]{1,0:T(8,128)(2,1)}, u32[]{:S(2)}) copy-start(bf16[256,256]{1,0:T(8,128)(2,1)} %constant.27.clone.order_ref) | copy-start | bytes 393220
  0.6 13.8 %copy-start = (f32[2,256,256]{2,1,0:T(8,128)S(1)}, f32[2,256,256]{2,1,0:T(8,128)}, u32[]{:S(2)}) copy-start(f32[2,256,256]{2,1,0:T(8,128)} %probe_ref.3) | copy-start | bytes 1572868
  0.7 13.8 %copy-start.1 = (f32[1,1,4,256,256]{4,3,2,1,0:T(8,128)S(1)}, f32[1,1,4,256,256]{4,3,2,1,0:T(8,128)}, u32[]{:S(2)}) copy-start(f32[1,1,4,256,256]{4,3,2,1,0:T(8,128)} %param.10) | copy-start | bytes 3145732
  0.7 18.2 %collective-permute-start.1 = (f32[2,256,512]{2,1,0:T(8,128)}, f32[2,256,512]{2,1,0:T(8,128)S(1)}, u32[]{:S(2)}, u32[]{:S(2)}) collective-permute-start(f32[2,256,512]{2,1,0:T(8,128)} %param.8), channel_id=1, source_target_pairs={{1,0},{2,1},{3,2},{4,3},{5,4},{6,5},{7,6},{8,7},{9,8},{10,9},{11,1... | collective-permute-start | bytes 3145736 | tf_op jit(solution)/shard_map/ppermute | solution.py:385
  11.0 3.4 %collective-permute-start = (s32[10]{0:T(128)S(1)}, s32[10]{0:T(128)S(1)}, u32[]{:S(2)}, u32[]{:S(2)}) collective-permute-start(s32[10]{0:T(128)S(1)} %pad_add_fusion.1), channel_id=1, source_target_pairs={{0,1},{1,2},{2,3},{3,4},{4,5},{5,6},{6,7},{7,8},{8,9},{9,10},{10,1... | collective-permute-start | bytes 128 | tf_op jit(solution)/shard_map/ppermute | solution.py:388
  14.5 4.5 %copy-start.2 = (bf16[4,2,256,256]{3,2,1,0:T(8,128)(2,1)S(1)}, bf16[4,2,256,256]{3,2,1,0:T(8,128)(2,1)}, u32[]{:S(2)}) copy-start(bf16[4,2,256,256]{3,2,1,0:T(8,128)(2,1)} %constant.28.clone.tables) | copy-start | bytes 3145732
  22.3 7.3 %collective-permute-start.2 = (f32[256,256]{1,0:T(8,128)S(1)}, f32[256,256]{1,0:T(8,128)S(1)}, u32[]{:S(2)}, u32[]{:S(2)}) collective-permute-start(f32[256,256]{1,0:T(8,128)S(1)} %get-tuple-element.18), channel_id=1, source_target_pairs={{0,1},{1,0},{2,3},{3,2},{4,5},{5,4},{6,7},{7,6},{8,9},{9,8},{10,11... | collective-permute-start | bytes 786440 | tf_op jit(solution)/shard_map/ppermute | solution.py:436
  26.1 47.7 %collective-permute-start.3 = (f32[2,256,512]{2,1,0:T(8,128)}, f32[2,256,512]{2,1,0:T(8,128)}, u32[]{:S(2)}, u32[]{:S(2)}) collective-permute-start(f32[2,256,512]{2,1,0:T(8,128)} %slice.6), channel_id=1, source_target_pairs={{0,1},{1,2},{2,3},{3,4},{4,5},{5,6},{6,7},{7,8},{8,9},{9,10},{10,1... | collective-permute-start | bytes 3145736 | tf_op jit(solution)/shard_map/ppermute | solution.py:437
  74.6 12.3 %all-to-all-start.2 = ((f32[16,16,256]{2,1,0:T(8,128)}), f32[16,16,256]{2,1,0:T(8,128)S(1)}, u32[]{:S(2)}, u32[]{:S(2)}) async-start(f32[16,16,256]{2,1,0:T(8,128)} %broadcast_in_dim.8), calls=%async_computation.2 | async-start | bytes 524288 | tf_op jit(solution)/shard_map/all_to_all | solution.py:367
  86.9 8.0 %collective-permute-start.4 = (f32[256,256]{1,0:T(8,128)S(1)}, f32[256,256]{1,0:T(8,128)S(1)}, u32[]{:S(2)}, u32[]{:S(2)}) collective-permute-start(f32[256,256]{1,0:T(8,128)S(1)} %bitcast.10), channel_id=1, source_target_pairs={{0,1},{1,0},{2,3},{3,2},{4,5},{5,4},{6,7},{7,6},{8,9},{9,8},{10,11... | collective-permute-start | bytes 786440 | tf_op jit(solution)/shard_map/ppermute | solution.py:448

commit v8 on v6

--- a/solution.py
+++ b/solution.py
@@ -333,14 +333,28 @@
         other_ref[row, :] = jnp.where(first, im, re)
 
 
-def update_kernel(facts, mine_ref, other_ref, probe_ref, out_ref):
+def update_kernel(facts, mine_ref, other_ref, probe_ref, out_ref, held, sems):
     size = mine_ref.shape[0]
-    mine, other = mine_ref[...], other_ref[...]
-    squares = jnp.sum(mine * mine + other * other)
+    total = jnp.zeros((8, size), jnp.float32)
+    for i in range(size // 8):
+        row = slice(8 * i, 8 * i + 8)
+        mine, other = mine_ref[row, :], other_ref[row, :]
+        total = total + (mine * mine + other * other)
+    squares = jnp.sum(total)
     step = 0.25 * lax.rsqrt(jnp.full((1, 1), squares / (2 * size * size) + 1e-06, jnp.float32))
     first = facts[0, CORE] == 0
-    out_ref[0] = probe_ref[0] - step * jnp.where(first, mine, other)
-    out_ref[1] = probe_ref[1] - step * jnp.where(first, other, mine)
+    stores = []
+    for j in range(2):
+        row = slice(j * size // 2, (j + 1) * size // 2)
+        mine, other = mine_ref[row, :], other_ref[row, :]
+        for c, part in ((0, jnp.where(first, mine, other)), (1, jnp.where(first, other, mine))):
+            held[c, row, :] = probe_ref[c, row, :] - step * part
+            stores.append(
+                pltpu.make_async_copy(held.at[c, row], out_ref.at[c, row], sems.at[2 * j + c])
+            )
+            stores[-1].start()
+    for store in stores:
+        store.wait()
 
 
 def place_of(device):
@@ -451,7 +465,8 @@
         update_kernel,
         out_shape=jax.ShapeDtypeStruct(probe.shape, f32),
         in_specs=[smem, vmem, vmem, vmem],
-        out_specs=vmem,
+        out_specs=hbm,
+        scratch_shapes=[pltpu.VMEM(probe.shape, f32), pltpu.SemaphoreType.DMA((4,))],
         compiler_params=pltpu.CompilerParams(vmem_limit_bytes=8 * 1024 * 1024),
         cost_estimate=pl.CostEstimate(flops=1_000_000, bytes_accessed=1_600_000, transcendentals=1),
         name="update",

time: 89.7 us -> 89.5 us (level)
  starting transfers between devices: 42.4 us -> 38.6 us
  Pallas kernels: 7.08 us -> 10.1 us
    pallas_call x1, Pallas kernels: 3.36 us -> 5.97 us  [on_device(): pl.pallas_call(frames_kernel, out_shape=(jax.ShapeDtypeStruct((size, size...]
    all_to_all x2, starting transfers between devices: 19.7 us -> 18.4 us  [exchanged(): lax.all_to_all(parts, AXES, 0, 0, tiled=True, axis_index_groups=groups_al...]
  transfers between devices with their start and end apart: 7 -> 7, of which waited for: 5 -> 5; matrix products, arithmetic and copies ran while one was open for 8% -> 8% of each run, Pallas kernels for 2% -> 3%
where the time goes in v8:
time: 89.5 us; the launch traced here: 88.9 us
  starting transfers between devices  38.6 us (43%)
  blocking collectives  19.2 us (21%)
  waiting for transfers between devices  11.7 us (13%)
  Pallas kernels  10.1 us (11%)
  other arithmetic  4.48 us (5%)
  local copies, waits for them, and re-layouts  3.38 us (4%)
  between operations  1.47 us (2%)
    all_to_all x1, blocking collectives, exchanged(): lax.all_to_all(parts, AXES, 0, 0, tiled=True, axis_index_groups=groups_al...  19.2 us
    all_to_all x2, starting transfers between devices, exchanged(): lax.all_to_all(parts, AXES, 0, 0, tiled=True, axis_index_groups=groups_al...  18.4 us
    ppermute x1, starting transfers between devices, on_device(): lax.ppermute(object_field, 'dev', [(i, i - 1) for i in range(1, peers)])  8.92 us
    all_to_all x2, waiting for transfers between devices, exchanged(): lax.all_to_all(parts, AXES, 0, 0, tiled=True, axis_index_groups=groups_al...  7.2 us
    pallas_call x1, Pallas kernels, on_device(): pl.pallas_call(frames_kernel, out_shape=(jax.ShapeDtypeStruct((size, size...  5.97 us
    ppermute x1, starting transfers between devices, on_device(): incoming = lax.ppermute(over, 'dev', steps)  4.68 us
    sub x1, other arithmetic, on_device(): object_field - jnp.concatenate([own[:, :size] + incoming, own[:, size:]],...  2.95 us
    ppermute x1, starting transfers between devices, on_device(): plane_other = lax.ppermute(plane, 'dev', swap)  2.8 us
  transfers between devices with their start and end apart: 7, of which 5 were waited for; matrix products, arithmetic and copies ran while one was open for 8% of the time, Pallas kernels for 3%

profile of v8, /device:TPU:1, one launch (start us, length us, event | category | flops | bytes accessed | tf_op | source)
XLA Modules:
  0.0 88.9 jit_solution(6169422632741805100)
XLA Ops:
  0.6 0.0 copy-start.3
  0.6 0.0 copy-start
  0.7 0.0 copy-start.1
  0.7 8.9 %collective-permute-start.1 = (f32[2,256,512]{2,1,0:T(8,128)}, f32[2,256,512]{2,1,0:T(8,128)S(1)}, u32[]{:S(2)}, u32[]{:S(2)}) collective-permute-start(f32[2,256,512]{2,1,0:T(8,128)} %param.8), channel_id=1, source_target_pairs={{1,0},{2,1},{3,2},{4,3},{5,4},{6,5},{7,6},{8,7},{9,8},{10,9},{11,1... | collective-permute-start | bytes 3145736 | tf_op jit(solution)/shard_map/ppermute | solution.py:399
  10.2 0.8 pad_add_fusion.1
  11.0 1.9 %collective-permute-start = (s32[10]{0:T(128)S(1)}, s32[10]{0:T(128)S(1)}, u32[]{:S(2)}, u32[]{:S(2)}) collective-permute-start(s32[10]{0:T(128)S(1)} %pad_add_fusion.1), channel_id=1, source_target_pairs={{0,1},{1,2},{2,3},{3,4},{4,5},{5,6},{6,7},{7,8},{8,9},{9,10},{10,1... | collective-permute-start | bytes 128 | tf_op jit(solution)/shard_map/ppermute | solution.py:402
  12.9 1.5 %pad.4 = f32[2,512,512]{2,1,0:T(8,128)S(1)} pad(f32[2,256,512]{2,1,0:T(8,128)} %param.8, f32[]{:T(128)} %constant.25.clone.1), padding=0_0x0_256x0_0 | pad | bytes 3145732 | tf_op jit(solution)/shard_map/jit(_pad)/pad | solution.py:423
  14.4 0.0 collective-permute-done
  14.4 0.0 copy-done.3
  14.5 0.0 copy-done
  14.5 0.0 copy-done.1
  14.5 0.0 copy-start.2
  14.5 2.6 %prepare.1 = (f32[4,256,256]{2,1,0:T(8,128)S(1)}, f32[256,512]{1,0:T(8,128)S(1)}) custom-call(s32[2,10]{1,0:T(2,128)S(1)} %pad_add_fusion.facts, f32[4,256,256]{2,1,0:T(8,128)S(1)} %bitcast.12, f32[2,256,256]{2,1,0:T(8,128)S(1)} %copy-done, bf16[256,256]{1,0:T(8,128)(2,1)S(1)} %copy-done.3), custom_call_target="tpu_custom_call" | custom-call | flops 800000000 | bytes 3200000 | tf_op jit(solution)/shard_map/prepare/pallas_call | solution.py:405
  17.1 1.8 %collective-permute-done.1 = f32[2,256,512]{2,1,0:T(8,128)S(1)} collective-permute-done((f32[2,256,512]{2,1,0:T(8,128)}, f32[2,256,512]{2,1,0:T(8,128)S(1)}, u32[]{:S(2)}, u32[]{:S(2)}) %collective-permute-start.1) | collective-permute-done | bytes 1048608 | tf_op jit(solution)/shard_map/ppermute | solution.py:399
  18.9 0.1 constant_dynamic-update-slice_fusion.ext
  19.0 0.0 copy-done.2
  19.0 6.0 %frames.1 = (f32[256,256]{1,0:T(8,128)S(1)}, f32[256,256]{1,0:T(8,128)S(1)}, f32[2,512,512]{2,1,0:T(8,128)S(1)}) custom-call(s32[2,10]{1,0:T(2,128)S(1)} %pad_add_fusion.facts, f32[2,512,512]{2,1,0:T(8,128)S(1)} %constant_dynamic-update-slice_fusion.ext, f32[2,256,256]{2,1,0:T(8,128)S(1)} %copy-done, f32[4,256,256]{2,1,0:T(8,128)S(1)} %get-tuple-element.15.amp, ...), custom_call_target="tpu_custom_call" | custom-call | flops 3300000000 | bytes 8000000 | tf_op jit(solution)/shard_map/frames/pallas_call | solution.py:426
  24.9 1.9 %collective-permute-start.2 = (f32[256,256]{1,0:T(8,128)S(1)}, f32[256,256]{1,0:T(8,128)S(1)}, u32[]{:S(2)}, u32[]{:S(2)}) collective-permute-start(f32[256,256]{1,0:T(8,128)S(1)} %get-tuple-element.17), channel_id=1, source_target_pairs={{0,1},{1,0},{2,3},{3,2},{4,5},{5,4},{6,7},{7,6},{8,9},{9,8},{10,11... | collective-permute-start | bytes 786440 | tf_op jit(solution)/shard_map/ppermute | solution.py:450
  26.9 1.5 %collective-permute-done.2 = f32[256,256]{1,0:T(8,128)S(1)} collective-permute-done((f32[256,256]{1,0:T(8,128)S(1)}, f32[256,256]{1,0:T(8,128)S(1)}, u32[]{:S(2)}, u32[]{:S(2)}) %collective-permute-start.2) | collective-permute-done | bytes 262176 | tf_op jit(solution)/shard_map/ppermute | solution.py:450
  28.4 0.7 add.13
  29.1 11.1 %all-to-all-start = ((f32[16,16,256]{2,1,0:T(8,128)}), f32[16,16,256]{2,1,0:T(8,128)S(1)}, u32[]{:S(2)}, u32[]{:S(2)}) async-start(f32[16,16,256]{2,1,0:T(8,128)} %bitcast.7), calls=%async_computation | async-start | bytes 524288 | tf_op jit(solution)/shard_map/all_to_all | solution.py:381
  40.2 1.0 %slice.7 = f32[2,256,512]{2,1,0:T(8,128)} slice(f32[2,512,512]{2,1,0:T(8,128)S(1)} %get-tuple-element.20), slice={[0:2], [256:512], [0:512]} | slice | bytes 2097152 | tf_op jit(solution)/shard_map/slice | solution.py:447
  41.2 4.7 %collective-permute-start.3 = (f32[2,256,512]{2,1,0:T(8,128)}, f32[2,256,512]{2,1,0:T(8,128)}, u32[]{:S(2)}, u32[]{:S(2)}) collective-permute-start(f32[2,256,512]{2,1,0:T(8,128)} %slice.7), channel_id=1, source_target_pairs={{0,1},{1,2},{2,3},{3,4},{4,5},{5,6},{6,7},{7,8},{8,9},{9,10},{10,1... | collective-permute-start | bytes 3145736 | tf_op jit(solution)/shard_map/ppermute | solution.py:451
  45.9 2.1 %all-to-all-done = f32[16,16,256]{2,1,0:T(8,128)S(1)} async-done(((f32[16,16,256]{2,1,0:T(8,128)}), f32[16,16,256]{2,1,0:T(8,128)S(1)}, u32[]{:S(2)}, u32[]{:S(2)}) %all-to-all-start) | async-done | bytes 262176 | tf_op jit(solution)/shard_map/all_to_all | solution.py:381
  48.1 19.2 %all_to_all.15 = f32[16,16,256]{2,1,0:T(8,128)S(1)} all-to-all(f32[16,16,256]{2,1,0:T(8,128)S(1)} %broadcast_in_dim.7), channel_id=1, replica_groups={{0,8,16,24,32,40,48,56,256,264,272,280,288,296,304,312},{1,3,5,7,65,67,..., dimensions={0} | all-to-all | bytes 524288 | tf_op jit(solution)/shard_map/all_to_all | solution.py:381
  67.3 0.7 broadcast_in_dim.8
  68.0 7.3 %all-to-all-start.2 = ((f32[16,16,256]{2,1,0:T(8,128)}), f32[16,16,256]{2,1,0:T(8,128)S(1)}, u32[]{:S(2)}, u32[]{:S(2)}) async-start(f32[16,16,256]{2,1,0:T(8,128)} %broadcast_in_dim.8), calls=%async_computation.2 | async-start | bytes 524288 | tf_op jit(solution)/shard_map/all_to_all | solution.py:381
  75.3 0.0 collective-permute-done.3
  75.4 2.9 %multiply_subtract_fusion = f32[2,256,512]{2,1,0:T(8,128)} fusion(f32[2,256,512]{2,1,0:T(8,128)} %param.8, f32[2,256,512]{2,1,0:T(8,128)} %collective-permute-done.3, f32[2,512,512]{2,1,0:T(8,128)S(1)} %get-tuple-element.20, f32[256,512]{1,0:T(8,128)S(1)} %get-tuple-element.21), kind=kLoop, calls=%fused_computation | loop fusion | flops 786432 | bytes 4718592 | tf_op jit(solution)/shard_map/sub | solution.py:457
  78.3 5.1 %all-to-all-done.2 = f32[16,16,256]{2,1,0:T(8,128)S(1)} async-done(((f32[16,16,256]{2,1,0:T(8,128)}), f32[16,16,256]{2,1,0:T(8,128)S(1)}, u32[]{:S(2)}, u32[]{:S(2)}) %all-to-all-start.2) | async-done | bytes 262176 | tf_op jit(solution)/shard_map/all_to_all | solution.py:381
  83.4 2.8 %collective-permute-start.4 = (f32[256,256]{1,0:T(8,128)S(1)}, f32[256,256]{1,0:T(8,128)S(1)}, u32[]{:S(2)}, u32[]{:S(2)}) collective-permute-start(f32[256,256]{1,0:T(8,128)S(1)} %bitcast.10), channel_id=1, source_target_pairs={{0,1},{1,0},{2,3},{3,2},{4,5},{5,4},{6,7},{7,6},{8,9},{9,8},{10,11... | collective-permute-start | bytes 786440 | tf_op jit(solution)/shard_map/ppermute | solution.py:462
  86.2 1.1 %collective-permute-done.4.other_ref = f32[256,256]{1,0:T(8,128)S(1)} collective-permute-done((f32[256,256]{1,0:T(8,128)S(1)}, f32[256,256]{1,0:T(8,128)S(1)}, u32[]{:S(2)}, u32[]{:S(2)}) %collective-permute-start.4) | collective-permute-done | bytes 262176 | tf_op jit(solution)/shard_map/ppermute | solution.py:462
  87.3 1.5 %update.1 = f32[2,256,256]{2,1,0:T(8,128)} custom-call(s32[2,10]{1,0:T(2,128)S(1)} %pad_add_fusion.facts, f32[256,256]{1,0:T(8,128)S(1)} %bitcast.11, f32[256,256]{1,0:T(8,128)S(1)} %collective-permute-done.4.other_ref, f32[2,256,256]{2,1,0:T(8,128)S(1)} %copy-done), custom_call_target="tpu_custom_call" | custom-call | flops 1000000 | bytes 1600000 | tf_op jit(solution)/shard_map/update/pallas_call | solution.py:464
  (4 shorter events, 0.1 us)
Async XLA Ops:
  0.6 13.8 %copy-start.3 = (bf16[256,256]{1,0:T(8,128)(2,1)S(1)}, bf16[256,256]{1,0:T(8,128)(2,1)}, u32[]{:S(2)}) copy-start(bf16[256,256]{1,0:T(8,128)(2,1)} %constant.27.clone.order_ref) | copy-start | bytes 393220
  0.6 13.8 %copy-start = (f32[2,256,256]{2,1,0:T(8,128)S(1)}, f32[2,256,256]{2,1,0:T(8,128)}, u32[]{:S(2)}) copy-start(f32[2,256,256]{2,1,0:T(8,128)} %probe_ref.3) | copy-start | bytes 1572868
  0.7 13.8 %copy-start.1 = (f32[1,1,4,256,256]{4,3,2,1,0:T(8,128)S(1)}, f32[1,1,4,256,256]{4,3,2,1,0:T(8,128)}, u32[]{:S(2)}) copy-start(f32[1,1,4,256,256]{4,3,2,1,0:T(8,128)} %param.10) | copy-start | bytes 3145732
  0.7 18.2 %collective-permute-start.1 = (f32[2,256,512]{2,1,0:T(8,128)}, f32[2,256,512]{2,1,0:T(8,128)S(1)}, u32[]{:S(2)}, u32[]{:S(2)}) collective-permute-start(f32[2,256,512]{2,1,0:T(8,128)} %param.8), channel_id=1, source_target_pairs={{1,0},{2,1},{3,2},{4,3},{5,4},{6,5},{7,6},{8,7},{9,8},{10,9},{11,1... | collective-permute-start | bytes 3145736 | tf_op jit(solution)/shard_map/ppermute | solution.py:399
  11.0 3.4 %collective-permute-start = (s32[10]{0:T(128)S(1)}, s32[10]{0:T(128)S(1)}, u32[]{:S(2)}, u32[]{:S(2)}) collective-permute-start(s32[10]{0:T(128)S(1)} %pad_add_fusion.1), channel_id=1, source_target_pairs={{0,1},{1,2},{2,3},{3,4},{4,5},{5,6},{6,7},{7,8},{8,9},{9,10},{10,1... | collective-permute-start | bytes 128 | tf_op jit(solution)/shard_map/ppermute | solution.py:402
  14.5 4.5 %copy-start.2 = (bf16[4,2,256,256]{3,2,1,0:T(8,128)(2,1)S(1)}, bf16[4,2,256,256]{3,2,1,0:T(8,128)(2,1)}, u32[]{:S(2)}) copy-start(bf16[4,2,256,256]{3,2,1,0:T(8,128)(2,1)} %constant.28.clone.tables) | copy-start | bytes 3145732
  24.9 3.4 %collective-permute-start.2 = (f32[256,256]{1,0:T(8,128)S(1)}, f32[256,256]{1,0:T(8,128)S(1)}, u32[]{:S(2)}, u32[]{:S(2)}) collective-permute-start(f32[256,256]{1,0:T(8,128)S(1)} %get-tuple-element.17), channel_id=1, source_target_pairs={{0,1},{1,0},{2,3},{3,2},{4,5},{5,4},{6,7},{7,6},{8,9},{9,8},{10,11... | collective-permute-start | bytes 786440 | tf_op jit(solution)/shard_map/ppermute | solution.py:450
  29.1 18.9 %all-to-all-start = ((f32[16,16,256]{2,1,0:T(8,128)}), f32[16,16,256]{2,1,0:T(8,128)S(1)}, u32[]{:S(2)}, u32[]{:S(2)}) async-start(f32[16,16,256]{2,1,0:T(8,128)} %bitcast.7), calls=%async_computation | async-start | bytes 524288 | tf_op jit(solution)/shard_map/all_to_all | solution.py:381
  41.2 34.1 %collective-permute-start.3 = (f32[2,256,512]{2,1,0:T(8,128)}, f32[2,256,512]{2,1,0:T(8,128)}, u32[]{:S(2)}, u32[]{:S(2)}) collective-permute-start(f32[2,256,512]{2,1,0:T(8,128)} %slice.7), channel_id=1, source_target_pairs={{0,1},{1,2},{2,3},{3,4},{4,5},{5,6},{6,7},{7,8},{8,9},{9,10},{10,1... | collective-permute-start | bytes 3145736 | tf_op jit(solution)/shard_map/ppermute | solution.py:451
  68.0 15.3 %all-to-all-start.2 = ((f32[16,16,256]{2,1,0:T(8,128)}), f32[16,16,256]{2,1,0:T(8,128)S(1)}, u32[]{:S(2)}, u32[]{:S(2)}) async-start(f32[16,16,256]{2,1,0:T(8,128)} %broadcast_in_dim.8), calls=%async_computation.2 | async-start | bytes 524288 | tf_op jit(solution)/shard_map/all_to_all | solution.py:381
  83.4 3.9 %collective-permute-start.4 = (f32[256,256]{1,0:T(8,128)S(1)}, f32[256,256]{1,0:T(8,128)S(1)}, u32[]{:S(2)}, u32[]{:S(2)}) collective-permute-start(f32[256,256]{1,0:T(8,128)S(1)} %bitcast.10), channel_id=1, source_target_pairs={{0,1},{1,0},{2,3},{3,2},{4,5},{5,4},{6,7},{7,6},{8,9},{9,8},{10,11... | collective-permute-start | bytes 786440 | tf_op jit(solution)/shard_map/ppermute | solution.py:462

commit v9 on v8

--- a/solution.py
+++ b/solution.py
@@ -444,13 +444,13 @@
         cost_estimate=pl.CostEstimate(flops=3_300_000_000, bytes_accessed=8_000_000, transcendentals=262144),
         name="frames",
     )(facts, ext, probe, ordered, jnp.asarray(frame_tables(size)))
-    over = total[:, band:]
     steps = [(i, i + 1) for i in range(peers - 1)]
     swap = [(i, i ^ 1) for i in range(peers)]
     plane = mine + lax.ppermute(other, "dev", swap)
-    incoming = lax.ppermute(over, "dev", steps)
     parts = exchanged(plane.reshape(16, size // 16, size), WIDE)
     share = jnp.sum(parts, axis=0)
+    share, total = lax.optimization_barrier((share, total))
+    incoming = lax.ppermute(total[:, band:], "dev", steps)
     share = jnp.sum(copies(share, LINE), axis=0)
     share, total = lax.optimization_barrier((share, total))
     own = total[:, :band]

time: 89.5 us -> 93.9 us (1.049)
  blocking collectives: 19.2 us -> 40.7 us
  starting transfers between devices: 38.6 us -> 28 us
  Pallas kernels: 10.1 us -> 7.17 us
  waiting for transfers between devices: 11.7 us -> 9.57 us
    all_to_all x1 -> x2, blocking collectives: 19.2 us -> 40.7 us  [exchanged(): lax.all_to_all(parts, AXES, 0, 0, tiled=True, axis_index_groups=groups_al...]
    all_to_all x2 -> x1, starting transfers between devices: 18.4 us -> 7.95 us  [exchanged(): lax.all_to_all(parts, AXES, 0, 0, tiled=True, axis_index_groups=groups_al...]
    pallas_call x1, Pallas kernels: 5.97 us -> 3.37 us  [on_device(): pl.pallas_call(frames_kernel, out_shape=(jax.ShapeDtypeStruct((size, size...]
    all_to_all x2 -> x1, waiting for transfers between devices: 7.2 us -> 4.8 us  [exchanged(): lax.all_to_all(parts, AXES, 0, 0, tiled=True, axis_index_groups=groups_al...]
    ppermute x1, starting transfers between devices: 1.92 us -> 3.19 us  [on_device(): plane = mine + lax.ppermute(other, 'dev', swap)]
  transfers between devices with their start and end apart: 7 -> 6, of which waited for: 5 -> 4; matrix products, arithmetic and copies ran while one was open for 8% -> 6% of each run, Pallas kernels for 3% -> 2%
where the time goes in v9:
time: 93.9 us; the launch traced here: 94.1 us
  blocking collectives  40.7 us (43%)
  starting transfers between devices  28 us (30%)
  waiting for transfers between devices  9.57 us (10%)
  Pallas kernels  7.17 us (8%)
  other arithmetic  3.78 us (4%)
  local copies, waits for them, and re-layouts  3.38 us (4%)
  between operations  1.47 us (2%)
    all_to_all x2, blocking collectives, exchanged(): lax.all_to_all(parts, AXES, 0, 0, tiled=True, axis_index_groups=groups_al...  40.7 us
    ppermute x1, starting transfers between devices, on_device(): lax.ppermute(object_field, 'dev', [(i, i - 1) for i in range(1, peers)])  8.92 us
    all_to_all x1, starting transfers between devices, exchanged(): lax.all_to_all(parts, AXES, 0, 0, tiled=True, axis_index_groups=groups_al...  7.95 us
    all_to_all x1, waiting for transfers between devices, exchanged(): lax.all_to_all(parts, AXES, 0, 0, tiled=True, axis_index_groups=groups_al...  4.8 us
    ppermute x1, starting transfers between devices, on_device(): incoming = lax.ppermute(total[:, band:], 'dev', steps)  4.16 us
    pallas_call x1, Pallas kernels, on_device(): pl.pallas_call(frames_kernel, out_shape=(jax.ShapeDtypeStruct((size, size...  3.37 us
    ppermute x1, starting transfers between devices, on_device(): plane = mine + lax.ppermute(other, 'dev', swap)  3.19 us
    sub x1, other arithmetic, on_device(): object_field - jnp.concatenate([own[:, :size] + incoming, own[:, size:]],...  2.95 us
  transfers between devices with their start and end apart: 6, of which 4 were waited for; matrix products, arithmetic and copies ran while one was open for 6% of the time, Pallas kernels for 2%

profile of v9, /device:TPU:1, one launch (start us, length us, event | category | flops | bytes accessed | tf_op | source)
XLA Modules:
  0.0 94.1 jit_solution(7225435778373131722)
XLA Ops:
  0.6 0.0 copy-start.3
  0.6 0.0 copy-start
  0.7 0.0 copy-start.1
  0.7 8.9 %collective-permute-start.1 = (f32[2,256,512]{2,1,0:T(8,128)}, f32[2,256,512]{2,1,0:T(8,128)S(1)}, u32[]{:S(2)}, u32[]{:S(2)}) collective-permute-start(f32[2,256,512]{2,1,0:T(8,128)} %param.8), channel_id=1, source_target_pairs={{1,0},{2,1},{3,2},{4,3},{5,4},{6,5},{7,6},{8,7},{9,8},{10,9},{11,1... | collective-permute-start | bytes 3145736 | tf_op jit(solution)/shard_map/ppermute | solution.py:399
  10.2 0.8 pad_add_fusion.1
  11.0 1.9 %collective-permute-start = (s32[10]{0:T(128)S(1)}, s32[10]{0:T(128)S(1)}, u32[]{:S(2)}, u32[]{:S(2)}) collective-permute-start(s32[10]{0:T(128)S(1)} %pad_add_fusion.1), channel_id=1, source_target_pairs={{0,1},{1,2},{2,3},{3,4},{4,5},{5,6},{6,7},{7,8},{8,9},{9,10},{10,1... | collective-permute-start | bytes 128 | tf_op jit(solution)/shard_map/ppermute | solution.py:402
  12.9 1.5 %pad.4 = f32[2,512,512]{2,1,0:T(8,128)S(1)} pad(f32[2,256,512]{2,1,0:T(8,128)} %param.8, f32[]{:T(128)} %constant.25.clone.1), padding=0_0x0_256x0_0 | pad | bytes 3145732 | tf_op jit(solution)/shard_map/jit(_pad)/pad | solution.py:423
  14.4 0.0 collective-permute-done
  14.4 0.0 copy-done.3
  14.5 0.0 copy-done
  14.5 0.0 copy-done.1
  14.5 0.0 copy-start.2
  14.5 2.3 %prepare.1 = (f32[4,256,256]{2,1,0:T(8,128)S(1)}, f32[256,512]{1,0:T(8,128)S(1)}) custom-call(s32[2,10]{1,0:T(2,128)S(1)} %pad_add_fusion.facts, f32[4,256,256]{2,1,0:T(8,128)S(1)} %bitcast.12, f32[2,256,256]{2,1,0:T(8,128)S(1)} %copy-done, bf16[256,256]{1,0:T(8,128)(2,1)S(1)} %copy-done.3), custom_call_target="tpu_custom_call" | custom-call | flops 800000000 | bytes 3200000 | tf_op jit(solution)/shard_map/prepare/pallas_call | solution.py:405
  16.7 2.1 %collective-permute-done.1 = f32[2,256,512]{2,1,0:T(8,128)S(1)} collective-permute-done((f32[2,256,512]{2,1,0:T(8,128)}, f32[2,256,512]{2,1,0:T(8,128)S(1)}, u32[]{:S(2)}, u32[]{:S(2)}) %collective-permute-start.1) | collective-permute-done | bytes 1048608 | tf_op jit(solution)/shard_map/ppermute | solution.py:399
  18.9 0.1 constant_dynamic-update-slice_fusion.ext
  19.0 0.0 copy-done.2
  19.0 3.4 %frames.1 = (f32[256,256]{1,0:T(8,128)S(1)}, f32[256,256]{1,0:T(8,128)S(1)}, f32[2,512,512]{2,1,0:T(8,128)S(1)}) custom-call(s32[2,10]{1,0:T(2,128)S(1)} %pad_add_fusion.facts, f32[2,512,512]{2,1,0:T(8,128)S(1)} %constant_dynamic-update-slice_fusion.ext, f32[2,256,256]{2,1,0:T(8,128)S(1)} %copy-done, f32[4,256,256]{2,1,0:T(8,128)S(1)} %get-tuple-element.17.amp, ...), custom_call_target="tpu_custom_call" | custom-call | flops 3300000000 | bytes 8000000 | tf_op jit(solution)/shard_map/frames/pallas_call | solution.py:426
  22.3 3.2 %collective-permute-start.2 = (f32[256,256]{1,0:T(8,128)S(1)}, f32[256,256]{1,0:T(8,128)S(1)}, u32[]{:S(2)}, u32[]{:S(2)}) collective-permute-start(f32[256,256]{1,0:T(8,128)S(1)} %get-tuple-element.19), channel_id=1, source_target_pairs={{0,1},{1,0},{2,3},{3,2},{4,5},{5,4},{6,7},{7,6},{8,9},{9,8},{10,11... | collective-permute-start | bytes 786440 | tf_op jit(solution)/shard_map/ppermute | solution.py:449
  25.5 1.1 %collective-permute-done.2 = f32[256,256]{1,0:T(8,128)S(1)} collective-permute-done((f32[256,256]{1,0:T(8,128)S(1)}, f32[256,256]{1,0:T(8,128)S(1)}, u32[]{:S(2)}, u32[]{:S(2)}) %collective-permute-start.2) | collective-permute-done | bytes 262176 | tf_op jit(solution)/shard_map/ppermute | solution.py:449
  26.7 20.5 %all_to_all.15 = f32[16,16,256]{2,1,0:T(8,128)S(1)} all-to-all(f32[16,16,256]{2,1,0:T(8,128)S(1)} %bitcast.13), channel_id=1, replica_groups={{0,2,4,6,64,66,68,70,128,130,132,134,192,194,196,198},{1,9,17,25,33,41,..., dimensions={0} | all-to-all | bytes 524288 | tf_op jit(solution)/shard_map/all_to_all | solution.py:381
  47.2 1.0 %slice.7 = f32[2,256,512]{2,1,0:T(8,128)} slice(f32[2,512,512]{2,1,0:T(8,128)S(1)} %get-tuple-element.24), slice={[0:2], [256:512], [0:512]} | slice | bytes 2097152 | tf_op jit(solution)/shard_map/slice | solution.py:453
  48.3 4.2 %collective-permute-start.3 = (f32[2,256,512]{2,1,0:T(8,128)}, f32[2,256,512]{2,1,0:T(8,128)}, u32[]{:S(2)}, u32[]{:S(2)}) collective-permute-start(f32[2,256,512]{2,1,0:T(8,128)} %slice.7), channel_id=1, source_target_pairs={{0,1},{1,2},{2,3},{3,4},{4,5},{5,6},{6,7},{7,8},{8,9},{9,10},{10,1... | collective-permute-start | bytes 3145736 | tf_op jit(solution)/shard_map/ppermute | solution.py:453
  52.5 20.2 %all_to_all.16 = f32[16,16,256]{2,1,0:T(8,128)S(1)} all-to-all(f32[16,16,256]{2,1,0:T(8,128)S(1)} %broadcast_in_dim.7), channel_id=1, replica_groups={{0,8,16,24,32,40,48,56,256,264,272,280,288,296,304,312},{1,3,5,7,65,67,..., dimensions={0} | all-to-all | bytes 524288 | tf_op jit(solution)/shard_map/all_to_all | solution.py:381
  72.7 0.7 broadcast_in_dim.8
  73.4 7.9 %all-to-all-start.2 = ((f32[16,16,256]{2,1,0:T(8,128)}), f32[16,16,256]{2,1,0:T(8,128)S(1)}, u32[]{:S(2)}, u32[]{:S(2)}) async-start(f32[16,16,256]{2,1,0:T(8,128)} %broadcast_in_dim.8), calls=%async_computation.2 | async-start | bytes 524288 | tf_op jit(solution)/shard_map/all_to_all | solution.py:381
  81.4 0.0 collective-permute-done.3
  81.4 2.9 %multiply_subtract_fusion = f32[2,256,512]{2,1,0:T(8,128)} fusion(f32[2,256,512]{2,1,0:T(8,128)} %param.8, f32[2,256,512]{2,1,0:T(8,128)} %collective-permute-done.3, f32[2,512,512]{2,1,0:T(8,128)S(1)} %get-tuple-element.24, f32[256,512]{1,0:T(8,128)S(1)} %get-tuple-element.25), kind=kLoop, calls=%fused_computation | loop fusion | flops 786432 | bytes 4718592 | tf_op jit(solution)/shard_map/sub | solution.py:457
  84.3 4.8 %all-to-all-done.2 = f32[16,16,256]{2,1,0:T(8,128)S(1)} async-done(((f32[16,16,256]{2,1,0:T(8,128)}), f32[16,16,256]{2,1,0:T(8,128)S(1)}, u32[]{:S(2)}, u32[]{:S(2)}) %all-to-all-start.2) | async-done | bytes 262176 | tf_op jit(solution)/shard_map/all_to_all | solution.py:381
  89.1 1.9 %collective-permute-start.4 = (f32[256,256]{1,0:T(8,128)S(1)}, f32[256,256]{1,0:T(8,128)S(1)}, u32[]{:S(2)}, u32[]{:S(2)}) collective-permute-start(f32[256,256]{1,0:T(8,128)S(1)} %bitcast.10), channel_id=1, source_target_pairs={{0,1},{1,0},{2,3},{3,2},{4,5},{5,4},{6,7},{7,6},{8,9},{9,8},{10,11... | collective-permute-start | bytes 786440 | tf_op jit(solution)/shard_map/ppermute | solution.py:462
  91.1 1.5 %collective-permute-done.4.other_ref = f32[256,256]{1,0:T(8,128)S(1)} collective-permute-done((f32[256,256]{1,0:T(8,128)S(1)}, f32[256,256]{1,0:T(8,128)S(1)}, u32[]{:S(2)}, u32[]{:S(2)}) %collective-permute-start.4) | collective-permute-done | bytes 262176 | tf_op jit(solution)/shard_map/ppermute | solution.py:462
  92.6 1.5 %update.1 = f32[2,256,256]{2,1,0:T(8,128)} custom-call(s32[2,10]{1,0:T(2,128)S(1)} %pad_add_fusion.facts, f32[256,256]{1,0:T(8,128)S(1)} %bitcast.11, f32[256,256]{1,0:T(8,128)S(1)} %collective-permute-done.4.other_ref, f32[2,256,256]{2,1,0:T(8,128)S(1)} %copy-done), custom_call_target="tpu_custom_call" | custom-call | flops 1000000 | bytes 1600000 | tf_op jit(solution)/shard_map/update/pallas_call | solution.py:464
  (5 shorter events, 0.1 us)
Async XLA Ops:
  0.6 13.8 %copy-start.3 = (bf16[256,256]{1,0:T(8,128)(2,1)S(1)}, bf16[256,256]{1,0:T(8,128)(2,1)}, u32[]{:S(2)}) copy-start(bf16[256,256]{1,0:T(8,128)(2,1)} %constant.27.clone.order_ref) | copy-start | bytes 393220
  0.6 13.8 %copy-start = (f32[2,256,256]{2,1,0:T(8,128)S(1)}, f32[2,256,256]{2,1,0:T(8,128)}, u32[]{:S(2)}) copy-start(f32[2,256,256]{2,1,0:T(8,128)} %probe_ref.3) | copy-start | bytes 1572868
  0.7 13.8 %copy-start.1 = (f32[1,1,4,256,256]{4,3,2,1,0:T(8,128)S(1)}, f32[1,1,4,256,256]{4,3,2,1,0:T(8,128)}, u32[]{:S(2)}) copy-start(f32[1,1,4,256,256]{4,3,2,1,0:T(8,128)} %param.10) | copy-start | bytes 3145732
  0.7 18.2 %collective-permute-start.1 = (f32[2,256,512]{2,1,0:T(8,128)}, f32[2,256,512]{2,1,0:T(8,128)S(1)}, u32[]{:S(2)}, u32[]{:S(2)}) collective-permute-start(f32[2,256,512]{2,1,0:T(8,128)} %param.8), channel_id=1, source_target_pairs={{1,0},{2,1},{3,2},{4,3},{5,4},{6,5},{7,6},{8,7},{9,8},{10,9},{11,1... | collective-permute-start | bytes 3145736 | tf_op jit(solution)/shard_map/ppermute | solution.py:399
  11.0 3.4 %collective-permute-start = (s32[10]{0:T(128)S(1)}, s32[10]{0:T(128)S(1)}, u32[]{:S(2)}, u32[]{:S(2)}) collective-permute-start(s32[10]{0:T(128)S(1)} %pad_add_fusion.1), channel_id=1, source_target_pairs={{0,1},{1,2},{2,3},{3,4},{4,5},{5,6},{6,7},{7,8},{8,9},{9,10},{10,1... | collective-permute-start | bytes 128 | tf_op jit(solution)/shard_map/ppermute | solution.py:402
  14.5 4.5 %copy-start.2 = (bf16[4,2,256,256]{3,2,1,0:T(8,128)(2,1)S(1)}, bf16[4,2,256,256]{3,2,1,0:T(8,128)(2,1)}, u32[]{:S(2)}) copy-start(bf16[4,2,256,256]{3,2,1,0:T(8,128)(2,1)} %constant.28.clone.tables) | copy-start | bytes 3145732
  22.3 4.3 %collective-permute-start.2 = (f32[256,256]{1,0:T(8,128)S(1)}, f32[256,256]{1,0:T(8,128)S(1)}, u32[]{:S(2)}, u32[]{:S(2)}) collective-permute-start(f32[256,256]{1,0:T(8,128)S(1)} %get-tuple-element.19), channel_id=1, source_target_pairs={{0,1},{1,0},{2,3},{3,2},{4,5},{5,4},{6,7},{7,6},{8,9},{9,8},{10,11... | collective-permute-start | bytes 786440 | tf_op jit(solution)/shard_map/ppermute | solution.py:449
  48.3 33.1 %collective-permute-start.3 = (f32[2,256,512]{2,1,0:T(8,128)}, f32[2,256,512]{2,1,0:T(8,128)}, u32[]{:S(2)}, u32[]{:S(2)}) collective-permute-start(f32[2,256,512]{2,1,0:T(8,128)} %slice.7), channel_id=1, source_target_pairs={{0,1},{1,2},{2,3},{3,4},{4,5},{5,6},{6,7},{7,8},{8,9},{9,10},{10,1... | collective-permute-start | bytes 3145736 | tf_op jit(solution)/shard_map/ppermute | solution.py:453
  73.4 15.7 %all-to-all-start.2 = ((f32[16,16,256]{2,1,0:T(8,128)}), f32[16,16,256]{2,1,0:T(8,128)S(1)}, u32[]{:S(2)}, u32[]{:S(2)}) async-start(f32[16,16,256]{2,1,0:T(8,128)} %broadcast_in_dim.8), calls=%async_computation.2 | async-start | bytes 524288 | tf_op jit(solution)/shard_map/all_to_all | solution.py:381
  89.1 3.4 %collective-permute-start.4 = (f32[256,256]{1,0:T(8,128)S(1)}, f32[256,256]{1,0:T(8,128)S(1)}, u32[]{:S(2)}, u32[]{:S(2)}) collective-permute-start(f32[256,256]{1,0:T(8,128)S(1)} %bitcast.10), channel_id=1, source_target_pairs={{0,1},{1,0},{2,3},{3,2},{4,5},{5,4},{6,7},{7,6},{8,9},{9,8},{10,11... | collective-permute-start | bytes 786440 | tf_op jit(solution)/shard_map/ppermute | solution.py:462
